TPU v7x, 512 devices: a whole 4x4x16 slice. The times are simulated.
512 devices in a mesh: ad: 64 (over z, x), tp: 8 (over y, core).
Axes of the slice: x: 4, y: 4, z: 16, core: 2. Of those that a mesh axis runs over, the one named last changes fastest.
Arguments:
- tokens: bfloat16 [4, 3072, 8192], P(None, 'ad', 'tp'), may hold values from -6 to 6
- row_adapter_index: int32 [4, 3072], P(None, 'ad'), may hold values from 0 to 255, as said below
- key_base_weight: bfloat16 [8192, 1024], P('tp'), may hold values from -0.0625 to 0.0625
- adapter_down_weight: bfloat16 [256, 8192, 64], P('ad', 'tp'), may hold values from -0.0625 to 0.0625
- adapter_up_weight: bfloat16 [256, 64, 1024], P('ad', None, 'tp'), may hold values from -0.75 to 0.75
Outputs:
- token_keys_output: bfloat16 [4, 3072, 1024], P(None, 'ad', 'tp')
Inputs may be any that keep to these rules, and one draw needn't show every extreme that they name: `row_adapter_index`: group g holds adapters g * 4 to (g + 1) * 4 - 1. In each step the 48 rows of one index of ad name one group in exactly 2 rows and every other group in at most 1 row; that busiest group is the same for every index of ad in a step, so it receives 2 rows from each.
All inputs are finite; a program needn't handle non-finite values.
Results may differ from a plain program's by a relative error of at most 0.005.
Values may be sent and summed in bfloat16 or wider, within the bound.
A program may use at most 64 MiB of HBM per device.

v0:
```python
import jax
import jax.numpy as jnp
from jax import lax
from jax.sharding import PartitionSpec as P


def adapter_row_output(outgoing_rows, row_labels, down_weight_tile, up_weight_tile):
    adapter_number = down_weight_tile.shape[0]
    row_count = outgoing_rows.shape[0]
    down_all = jnp.einsum(
        "nd,adr->nar", outgoing_rows, down_weight_tile, preferred_element_type=jnp.float32
    )
    labels = (jnp.arange(adapter_number, dtype=jnp.int32) + 1).astype(jnp.bfloat16)
    selector = (row_labels[:, None] == labels[None, :]).astype(jnp.float32)
    down_part = jnp.sum(down_all * selector[:, :, None], axis=1)
    down_sum = lax.psum(down_part, "tp")
    down_low = down_sum.astype(jnp.bfloat16)
    spread_rows = (selector.astype(jnp.bfloat16)[:, :, None] * down_low[:, None, :]).reshape(
        row_count, -1
    )
    up_flat = up_weight_tile.reshape(
        adapter_number * up_weight_tile.shape[1], up_weight_tile.shape[2]
    )
    return jnp.dot(spread_rows, up_flat, preferred_element_type=jnp.float32).astype(jnp.bfloat16)


def body(tokens, row_adapter_index, key_base_weight, adapter_down_weight, adapter_up_weight):
    step_count, row_dev, width_per_shard = tokens.shape
    groups = lax.axis_size("ad")
    adapter_number = adapter_down_weight.shape[0]
    capacity = max(2, 3 * row_dev // groups)
    gathered_rows = tokens.reshape(step_count * row_dev, width_per_shard)
    partial_base = jnp.dot(gathered_rows, key_base_weight, preferred_element_type=jnp.float32)
    base_keys_output = lax.psum_scatter(partial_base, "tp", scatter_dimension=1, tiled=True)
    key_feature_width = base_keys_output.shape[1]
    outputs = []
    for step_index in range(step_count):
        step_rows = tokens[step_index]
        row_index_list = row_adapter_index[step_index]
        owner_group = row_index_list // adapter_number
        local_index = row_index_list % adapter_number
        group_hits = (owner_group[:, None] == jnp.arange(groups, dtype=jnp.int32)[None, :]).astype(
            jnp.int32
        )
        slot_rank = jnp.sum((jnp.cumsum(group_hits, axis=0) - group_hits) * group_hits, axis=1)
        tag_values = (local_index + 1).astype(jnp.float32)
        stays_remote = owner_group >= 0
        slot_index = jnp.where(stays_remote, owner_group * capacity + slot_rank, -1)
        dispatch = (
            slot_index[None, :] == jnp.arange(groups * capacity, dtype=jnp.int32)[:, None]
        ).astype(jnp.bfloat16)
        send_rows = jnp.dot(dispatch, step_rows, preferred_element_type=jnp.float32).astype(
            jnp.bfloat16
        )
        send_rows = send_rows.reshape(groups, capacity, width_per_shard)
        send_tags = (
            jnp.dot(dispatch.astype(jnp.float32), tag_values)
            .astype(jnp.bfloat16)
            .reshape(groups, capacity)
        )
        incoming_rows = lax.all_to_all(send_rows, "ad", split_axis=0, concat_axis=0, tiled=True)
        incoming_labels = lax.all_to_all(send_tags, "ad", split_axis=0, concat_axis=0, tiled=True)
        sender_number, slot_number = incoming_labels.shape
        adapter_update = adapter_row_output(
            incoming_rows.reshape(-1, width_per_shard),
            incoming_labels.reshape(-1),
            adapter_down_weight,
            adapter_up_weight,
        )
        adapter_update = adapter_update.reshape(sender_number, slot_number, key_feature_width)
        rows_sent_back = lax.all_to_all(
            adapter_update, "ad", split_axis=0, concat_axis=0, tiled=True
        )
        routed = jnp.dot(
            dispatch.T,
            rows_sent_back.reshape(groups * capacity, key_feature_width),
            preferred_element_type=jnp.float32,
        )
        step_base = base_keys_output[step_index * row_dev : (step_index + 1) * row_dev]
        outputs.append(step_base + routed)
    return jnp.stack(outputs).astype(jnp.bfloat16)


def solution(mesh):
    placed = (
        P(None, "ad", "tp"),
        P(None, "ad"),
        P("tp", None),
        P("ad", "tp", None),
        P("ad", None, "tp"),
    )
    return jax.shard_map(
        body, mesh=mesh, in_specs=placed, out_specs=P(None, "ad", "tp"), check_vma=False
    )
```

profile of v0, /device:TPU:2, one launch (start us, length us, event | category | flops | bytes accessed | tf_op | source)
XLA Modules:
  0.0 308.1 jit_solution(69769566374800532)
XLA Ops:
  6.5 0.9 and_select_fusion.10
  8.0 0.2 select_reduce_fusion.2
  8.2 0.2 select_reduce_fusion
  8.4 0.9 fusion.56
  9.4 0.8 all_to_all.67
  10.3 18.6 %all-to-all-start.9 = ((bf16[64,1,2]{2,1,0:T(2,128)(2,1)}), bf16[64,1,2]{2,1,0:T(2,128)(2,1)S(1)}, u32[]{:S(2)}, u32[]{:S(2)}) async-start(bf16[64,1,2]{2,1,0:T(2,128)(2,1)} %all_to_all.67), calls=%async_computation.10 | async-start | bytes 65536 | tf_op jit(solution)/shard_map/all_to_all | solution.py:62
  29.0 0.8 all_to_all.65
  29.9 12.9 %all-to-all-done.9 = bf16[64,1,2]{2,1,0:T(2,128)(2,1)S(1)} async-done(((bf16[64,1,2]{2,1,0:T(2,128)(2,1)}), bf16[64,1,2]{2,1,0:T(2,128)(2,1)S(1)}, u32[]{:S(2)}, u32[]{:S(2)}) %all-to-all-start.9) | async-done | bytes 288 | tf_op jit(solution)/shard_map/all_to_all | solution.py:62
  42.7 5.5 %all-to-all-start.3 = ((bf16[64,1,2]{2,1,0:T(2,128)(2,1)}), bf16[64,1,2]{2,1,0:T(2,128)(2,1)S(1)}, u32[]{:S(2)}, u32[]{:S(2)}) async-start(bf16[64,1,2]{2,1,0:T(2,128)(2,1)} %all_to_all.65), calls=%async_computation.4 | async-start | bytes 65536 | tf_op jit(solution)/shard_map/all_to_all | solution.py:62
  48.3 0.8 all_to_all.66
  49.1 12.7 %all-to-all-done.3 = bf16[64,1,2]{2,1,0:T(2,128)(2,1)S(1)} async-done(((bf16[64,1,2]{2,1,0:T(2,128)(2,1)}), bf16[64,1,2]{2,1,0:T(2,128)(2,1)S(1)}, u32[]{:S(2)}, u32[]{:S(2)}) %all-to-all-start.3) | async-done | bytes 288 | tf_op jit(solution)/shard_map/all_to_all | solution.py:62
  61.8 5.6 %all-to-all-start.6 = ((bf16[64,1,2]{2,1,0:T(2,128)(2,1)}), bf16[64,1,2]{2,1,0:T(2,128)(2,1)S(1)}, u32[]{:S(2)}, u32[]{:S(2)}) async-start(bf16[64,1,2]{2,1,0:T(2,128)(2,1)} %all_to_all.66), calls=%async_computation.7 | async-start | bytes 65536 | tf_op jit(solution)/shard_map/all_to_all | solution.py:62
  67.6 0.8 all_to_all.64
  68.4 12.9 %all-to-all-done.6 = bf16[64,1,2]{2,1,0:T(2,128)(2,1)S(1)} async-done(((bf16[64,1,2]{2,1,0:T(2,128)(2,1)}), bf16[64,1,2]{2,1,0:T(2,128)(2,1)S(1)}, u32[]{:S(2)}, u32[]{:S(2)}) %all-to-all-start.6) | async-done | bytes 288 | tf_op jit(solution)/shard_map/all_to_all | solution.py:62
  81.4 0.6 copy-done.5
  82.0 5.5 %all-to-all-start = ((bf16[64,1,2]{2,1,0:T(2,128)(2,1)}), bf16[64,1,2]{2,1,0:T(2,128)(2,1)S(1)}, u32[]{:S(2)}, u32[]{:S(2)}) async-start(bf16[64,1,2]{2,1,0:T(2,128)(2,1)} %all_to_all.64), calls=%async_computation.1 | async-start | bytes 65536 | tf_op jit(solution)/shard_map/all_to_all | solution.py:62
  87.5 1.1 convolution_convert_fusion.3
  88.6 0.8 reshape.453
  89.4 11.9 %all-to-all-done = bf16[64,1,2]{2,1,0:T(2,128)(2,1)S(1)} async-done(((bf16[64,1,2]{2,1,0:T(2,128)(2,1)}), bf16[64,1,2]{2,1,0:T(2,128)(2,1)S(1)}, u32[]{:S(2)}, u32[]{:S(2)}) %all-to-all-start) | async-done | bytes 288 | tf_op jit(solution)/shard_map/all_to_all | solution.py:62
  101.3 5.5 %all-to-all-start.1 = ((bf16[64,2,1024]{2,1,0:T(2,128)(2,1)}), bf16[64,2,1024]{2,1,0:T(2,128)(2,1)S(1)}, u32[]{:S(2)}, u32[]{:S(2)}) async-start(bf16[64,2,1024]{2,1,0:T(2,128)(2,1)} %reshape.453), calls=%async_computation.2 | async-start | bytes 524288 | tf_op jit(solution)/shard_map/all_to_all | solution.py:61
  106.8 0.2 convolution_convert_fusion.1
  107.0 0.8 reshape.461
  107.8 16.6 %all-to-all-done.1 = bf16[64,2,1024]{2,1,0:T(2,128)(2,1)S(1)} async-done(((bf16[64,2,1024]{2,1,0:T(2,128)(2,1)}), bf16[64,2,1024]{2,1,0:T(2,128)(2,1)S(1)}, u32[]{:S(2)}, u32[]{:S(2)}) %all-to-all-start.1) | async-done | bytes 262176 | tf_op jit(solution)/shard_map/all_to_all | solution.py:61
  124.5 5.7 %all-to-all-start.7 = ((bf16[64,2,1024]{2,1,0:T(2,128)(2,1)}), bf16[64,2,1024]{2,1,0:T(2,128)(2,1)S(1)}, u32[]{:S(2)}, u32[]{:S(2)}) async-start(bf16[64,2,1024]{2,1,0:T(2,128)(2,1)} %reshape.461), calls=%async_computation.8 | async-start | bytes 524288 | tf_op jit(solution)/shard_map/all_to_all | solution.py:61
  130.2 0.2 convolution_convert_fusion.2
  130.4 0.8 reshape.457
  131.2 16.9 %all-to-all-done.7 = bf16[64,2,1024]{2,1,0:T(2,128)(2,1)S(1)} async-done(((bf16[64,2,1024]{2,1,0:T(2,128)(2,1)}), bf16[64,2,1024]{2,1,0:T(2,128)(2,1)S(1)}, u32[]{:S(2)}, u32[]{:S(2)}) %all-to-all-start.7) | async-done | bytes 262176 | tf_op jit(solution)/shard_map/all_to_all | solution.py:61
  148.1 6.3 %all-to-all-start.4 = ((bf16[64,2,1024]{2,1,0:T(2,128)(2,1)}), bf16[64,2,1024]{2,1,0:T(2,128)(2,1)}, u32[]{:S(2)}, u32[]{:S(2)}) async-start(bf16[64,2,1024]{2,1,0:T(2,128)(2,1)} %reshape.457), calls=%async_computation.5 | async-start | bytes 524288 | tf_op jit(solution)/shard_map/all_to_all | solution.py:61
  154.4 1.5 fusion.100
  156.0 0.9 convolution_convert_fusion
  156.9 1.8 reshape.465
  158.6 0.9 reduce.3
  159.5 0.1 eq.243
  159.6 0.9 reduce.1
  160.7 0.9 reduce.2
  161.7 0.9 reduce
  162.7 0.7 fusion.52
  163.5 8.6 %all-to-all-done.4 = bf16[64,2,1024]{2,1,0:T(2,128)(2,1)} async-done(((bf16[64,2,1024]{2,1,0:T(2,128)(2,1)}), bf16[64,2,1024]{2,1,0:T(2,128)(2,1)}, u32[]{:S(2)}, u32[]{:S(2)}) %all-to-all-start.4) | async-done | bytes 262176 | tf_op jit(solution)/shard_map/all_to_all | solution.py:61
  172.1 6.6 %all-to-all-start.10 = ((bf16[64,2,1024]{2,1,0:T(2,128)(2,1)}), bf16[64,2,1024]{2,1,0:T(2,128)(2,1)S(1)}, u32[]{:S(2)}, u32[]{:S(2)}) async-start(bf16[64,2,1024]{2,1,0:T(2,128)(2,1)} %reshape.465), calls=%async_computation.11 | async-start | bytes 524288 | tf_op jit(solution)/shard_map/all_to_all | solution.py:61
  178.7 0.3 fusion.101
  179.0 0.6 multiply_reduce_fusion.3
  179.8 0.3 fusion.103
  180.2 1.1 reshape.458
  181.2 0.3 fusion.102
  181.6 15.0 %all-to-all-done.10 = bf16[64,2,1024]{2,1,0:T(2,128)(2,1)S(1)} async-done(((bf16[64,2,1024]{2,1,0:T(2,128)(2,1)}), bf16[64,2,1024]{2,1,0:T(2,128)(2,1)S(1)}, u32[]{:S(2)}, u32[]{:S(2)}) %all-to-all-start.10) | async-done | bytes 262176 | tf_op jit(solution)/shard_map/all_to_all | solution.py:61
  196.6 0.3 fusion.104
  197.0 25.0 %all-reduce.2 = (bf16[128,64]{0,1:T(8,128)(2,1)S(1)}, bf16[128,64]{0,1:T(8,128)(2,1)S(1)}, bf16[128,64]{0,1:T(8,128)(2,1)S(1)}, bf16[128,64]{0,1:T(8,128)(2,1)S(1)}) all-reduce(f32[128,64]{0,1:T(8,128)S(1)} %multiply_reduce_fusion, f32[128,64]{0,1:T(8,128)S(1)} %multiply_reduce_fusion.1, ...), channel_id=1, replica_groups=mesh['ad'=64,'tp'=8] {'tp'}, use_global_device_ids=true, to_apply=%region_16.17 | all-reduce | flops 32768 | bytes 196608 | tf_op jit(solution)/shard_map/psum | solution.py:16
  222.0 0.8 fusion.3
  222.8 5.5 %all-to-all-start.11 = ((bf16[64,2,128]{2,1,0:T(2,128)(2,1)}), bf16[64,2,128]{2,1,0:T(2,128)(2,1)S(1)}, u32[]{:S(2)}, u32[]{:S(2)}) async-start(bf16[64,2,128]{2,1,0:T(2,128)(2,1)} %bitcast.50), calls=%async_computation.12 | async-start | bytes 65536 | tf_op jit(solution)/shard_map/all_to_all | solution.py:71
  228.3 0.8 fusion.2
  229.1 12.9 %all-to-all-done.11 = bf16[64,2,128]{2,1,0:T(2,128)(2,1)S(1)} async-done(((bf16[64,2,128]{2,1,0:T(2,128)(2,1)}), bf16[64,2,128]{2,1,0:T(2,128)(2,1)S(1)}, u32[]{:S(2)}, u32[]{:S(2)}) %all-to-all-start.11) | async-done | bytes 32800 | tf_op jit(solution)/shard_map/all_to_all | solution.py:71
  242.0 5.2 %all-to-all-start.8 = ((bf16[64,2,128]{2,1,0:T(2,128)(2,1)}), bf16[64,2,128]{2,1,0:T(2,128)(2,1)S(1)}, u32[]{:S(2)}, u32[]{:S(2)}) async-start(bf16[64,2,128]{2,1,0:T(2,128)(2,1)} %bitcast.37), calls=%async_computation.9 | async-start | bytes 65536 | tf_op jit(solution)/shard_map/all_to_all | solution.py:71
  247.2 0.8 fusion.1
  248.1 13.1 %all-to-all-done.8 = bf16[64,2,128]{2,1,0:T(2,128)(2,1)S(1)} async-done(((bf16[64,2,128]{2,1,0:T(2,128)(2,1)}), bf16[64,2,128]{2,1,0:T(2,128)(2,1)S(1)}, u32[]{:S(2)}, u32[]{:S(2)}) %all-to-all-start.8) | async-done | bytes 32800 | tf_op jit(solution)/shard_map/all_to_all | solution.py:71
  261.1 5.5 %all-to-all-start.5 = ((bf16[64,2,128]{2,1,0:T(2,128)(2,1)}), bf16[64,2,128]{2,1,0:T(2,128)(2,1)S(1)}, u32[]{:S(2)}, u32[]{:S(2)}) async-start(bf16[64,2,128]{2,1,0:T(2,128)(2,1)} %bitcast.24), calls=%async_computation.6 | async-start | bytes 65536 | tf_op jit(solution)/shard_map/all_to_all | solution.py:71
  266.6 0.8 fusion
  267.4 0.9 fusion.8
  268.3 11.9 %all-to-all-done.5 = bf16[64,2,128]{2,1,0:T(2,128)(2,1)S(1)} async-done(((bf16[64,2,128]{2,1,0:T(2,128)(2,1)}), bf16[64,2,128]{2,1,0:T(2,128)(2,1)S(1)}, u32[]{:S(2)}, u32[]{:S(2)}) %all-to-all-start.5) | async-done | bytes 32800 | tf_op jit(solution)/shard_map/all_to_all | solution.py:71
  280.2 5.5 %all-to-all-start.2 = ((bf16[64,2,128]{2,1,0:T(2,128)(2,1)}), bf16[64,2,128]{2,1,0:T(2,128)(2,1)S(1)}, u32[]{:S(2)}, u32[]{:S(2)}) async-start(bf16[64,2,128]{2,1,0:T(2,128)(2,1)} %bitcast.11), calls=%async_computation.3 | async-start | bytes 65536 | tf_op jit(solution)/shard_map/all_to_all | solution.py:71
  285.8 0.9 fusion.9
  286.7 0.9 fusion.10
  287.7 12.0 %all-to-all-done.2 = bf16[64,2,128]{2,1,0:T(2,128)(2,1)S(1)} async-done(((bf16[64,2,128]{2,1,0:T(2,128)(2,1)}), bf16[64,2,128]{2,1,0:T(2,128)(2,1)S(1)}, u32[]{:S(2)}, u32[]{:S(2)}) %all-to-all-start.2) | async-done | bytes 32800 | tf_op jit(solution)/shard_map/all_to_all | solution.py:71
  299.7 0.9 fusion.11
  300.6 0.6 pad_maximum_fusion
  (66 shorter events, 2.1 us)
Async XLA Ops:
  6.5 147.9 %copy-start = (bf16[1024,1024]{1,0:T(8,128)(2,1)S(1)}, bf16[1024,1024]{1,0:T(8,128)(2,1)}, u32[]{:S(2)}) copy-start(bf16[1024,1024]{1,0:T(8,128)(2,1)} %param.7) | copy-start | bytes 6291460
  6.5 100.3 %copy-start.2 = (bf16[4,48,1024]{2,1,0:T(8,128)(2,1)S(1)}, bf16[4,48,1024]{2,1,0:T(8,128)(2,1)}, u32[]{:S(2)}) copy-start(bf16[4,48,1024]{2,1,0:T(8,128)(2,1)} %param.5) | copy-start | bytes 1179652
  9.3 121.9 %copy-start.8 = (s32[48]{0:T(128)}, s32[48]{0:T(128)S(1)}, u32[]{:S(2)}) copy-start(s32[48]{0:T(128)S(1)} %get-tuple-element.17) | copy-start | bytes 580
  9.3 121.9 %copy-start.10 = (s32[48]{0:T(128)}, s32[48]{0:T(128)S(1)}, u32[]{:S(2)}) copy-start(s32[48]{0:T(128)S(1)} %get-tuple-element.19) | copy-start | bytes 580
  9.3 121.9 %copy-start.12 = (s32[48]{0:T(128)}, s32[48]{0:T(128)S(1)}, u32[]{:S(2)}) copy-start(s32[48]{0:T(128)S(1)} %get-tuple-element.18) | copy-start | bytes 580
  9.3 146.6 %copy-start.14 = (s32[48]{0:T(128)}, s32[48]{0:T(128)S(1)}, u32[]{:S(2)}) copy-start(s32[48]{0:T(128)S(1)} %get-tuple-element.20) | copy-start | bytes 580
  10.3 32.5 %all-to-all-start.9 = ((bf16[64,1,2]{2,1,0:T(2,128)(2,1)}), bf16[64,1,2]{2,1,0:T(2,128)(2,1)S(1)}, u32[]{:S(2)}, u32[]{:S(2)}) async-start(bf16[64,1,2]{2,1,0:T(2,128)(2,1)} %all_to_all.67), calls=%async_computation.10 | async-start | bytes 65536 | tf_op jit(solution)/shard_map/all_to_all | solution.py:62
  42.7 38.6 %copy-start.3 = (bf16[64,1,2]{2,1,0:T(2,128)(2,1)}, bf16[64,1,2]{2,1,0:T(2,128)(2,1)S(1)}, u32[]{:S(2)}) copy-start(bf16[64,1,2]{2,1,0:T(2,128)(2,1)S(1)} %all-to-all-done.9) | copy-start | bytes 772
  42.7 19.1 %all-to-all-start.3 = ((bf16[64,1,2]{2,1,0:T(2,128)(2,1)}), bf16[64,1,2]{2,1,0:T(2,128)(2,1)S(1)}, u32[]{:S(2)}, u32[]{:S(2)}) async-start(bf16[64,1,2]{2,1,0:T(2,128)(2,1)} %all_to_all.65), calls=%async_computation.4 | async-start | bytes 65536 | tf_op jit(solution)/shard_map/all_to_all | solution.py:62
  61.8 19.5 %copy-start.4 = (bf16[64,1,2]{2,1,0:T(2,128)(2,1)}, bf16[64,1,2]{2,1,0:T(2,128)(2,1)S(1)}, u32[]{:S(2)}) copy-start(bf16[64,1,2]{2,1,0:T(2,128)(2,1)S(1)} %all-to-all-done.3) | copy-start | bytes 772
  61.8 19.5 %all-to-all-start.6 = ((bf16[64,1,2]{2,1,0:T(2,128)(2,1)}), bf16[64,1,2]{2,1,0:T(2,128)(2,1)S(1)}, u32[]{:S(2)}, u32[]{:S(2)}) async-start(bf16[64,1,2]{2,1,0:T(2,128)(2,1)} %all_to_all.66), calls=%async_computation.7 | async-start | bytes 65536 | tf_op jit(solution)/shard_map/all_to_all | solution.py:62
  81.4 0.6 copy-start.5
  82.0 19.3 %all-to-all-start = ((bf16[64,1,2]{2,1,0:T(2,128)(2,1)}), bf16[64,1,2]{2,1,0:T(2,128)(2,1)S(1)}, u32[]{:S(2)}, u32[]{:S(2)}) async-start(bf16[64,1,2]{2,1,0:T(2,128)(2,1)} %all_to_all.64), calls=%async_computation.1 | async-start | bytes 65536 | tf_op jit(solution)/shard_map/all_to_all | solution.py:62
  101.3 53.2 %copy-start.6 = (bf16[64,1,2]{2,1,0:T(2,128)(2,1)}, bf16[64,1,2]{2,1,0:T(2,128)(2,1)S(1)}, u32[]{:S(2)}) copy-start(bf16[64,1,2]{2,1,0:T(2,128)(2,1)S(1)} %all-to-all-done) | copy-start | bytes 772
  101.3 23.2 %all-to-all-start.1 = ((bf16[64,2,1024]{2,1,0:T(2,128)(2,1)}), bf16[64,2,1024]{2,1,0:T(2,128)(2,1)S(1)}, u32[]{:S(2)}, u32[]{:S(2)}) async-start(bf16[64,2,1024]{2,1,0:T(2,128)(2,1)} %reshape.453), calls=%async_computation.2 | async-start | bytes 524288 | tf_op jit(solution)/shard_map/all_to_all | solution.py:61
  124.5 23.7 %all-to-all-start.7 = ((bf16[64,2,1024]{2,1,0:T(2,128)(2,1)}), bf16[64,2,1024]{2,1,0:T(2,128)(2,1)S(1)}, u32[]{:S(2)}, u32[]{:S(2)}) async-start(bf16[64,2,1024]{2,1,0:T(2,128)(2,1)} %reshape.461), calls=%async_computation.8 | async-start | bytes 524288 | tf_op jit(solution)/shard_map/all_to_all | solution.py:61
  148.1 24.0 %all-to-all-start.4 = ((bf16[64,2,1024]{2,1,0:T(2,128)(2,1)}), bf16[64,2,1024]{2,1,0:T(2,128)(2,1)}, u32[]{:S(2)}, u32[]{:S(2)}) async-start(bf16[64,2,1024]{2,1,0:T(2,128)(2,1)} %reshape.457), calls=%async_computation.5 | async-start | bytes 524288 | tf_op jit(solution)/shard_map/all_to_all | solution.py:61
  154.4 113.0 %reduce-scatter.2.cloned.1.call-start = ((), (), s32[]{:S(2)}) async-start(), calls=%async_computation.13 | async-start | bytes 884736 | tf_op jit(solution)/shard_map/reduce_scatter | solution.py:34
  155.9 22.8 %copy-start.1 = (bf16[4,1024,64]{1,2,0:T(8,128)(2,1)S(1)}, bf16[4,1024,64]{1,2,0:T(8,128)(2,1)}, u32[]{:S(2)}) copy-start(bf16[4,1024,64]{1,2,0:T(8,128)(2,1)} %param.8) | copy-start | bytes 1572868
  172.1 24.4 %all-to-all-start.10 = ((bf16[64,2,1024]{2,1,0:T(2,128)(2,1)}), bf16[64,2,1024]{2,1,0:T(2,128)(2,1)S(1)}, u32[]{:S(2)}, u32[]{:S(2)}) async-start(bf16[64,2,1024]{2,1,0:T(2,128)(2,1)} %reshape.465), calls=%async_computation.11 | async-start | bytes 524288 | tf_op jit(solution)/shard_map/all_to_all | solution.py:61
  179.7 17.2 %copy-start.7 = (f32[128,64]{0,1:T(8,128)S(1)}, f32[128,64]{0,1:T(8,128)}, u32[]{:S(2)}) copy-start(f32[128,64]{0,1:T(8,128)} %multiply_reduce_fusion.3) | copy-start | bytes 98308
  179.7 42.2 %copy-start.19 = (bf16[128,4]{0,1:T(4,128)(2,1)S(1)}, bf16[128,4]{0,1:T(4,128)(2,1)}, u32[]{:S(2)}) copy-start(bf16[128,4]{0,1:T(4,128)(2,1)} %get-tuple-element.40) | copy-start | bytes 3076
  179.8 42.2 %copy-start.20 = (bf16[4,64,128]{2,1,0:T(8,128)(2,1)S(1)}, bf16[4,64,128]{2,1,0:T(8,128)(2,1)}, u32[]{:S(2)}) copy-start(bf16[4,64,128]{2,1,0:T(8,128)(2,1)} %param.9) | copy-start | bytes 196612
  180.1 48.2 %copy-start.18 = (bf16[128,4]{0,1:T(4,128)(2,1)S(1)}, bf16[128,4]{0,1:T(4,128)(2,1)}, u32[]{:S(2)}) copy-start(bf16[128,4]{0,1:T(4,128)(2,1)} %get-tuple-element.38) | copy-start | bytes 3076
  180.1 67.1 %copy-start.17 = (bf16[128,4]{0,1:T(4,128)(2,1)S(1)}, bf16[128,4]{0,1:T(4,128)(2,1)}, u32[]{:S(2)}) copy-start(bf16[128,4]{0,1:T(4,128)(2,1)} %get-tuple-element.36) | copy-start | bytes 3076
  180.1 86.5 %copy-start.16 = (bf16[128,4]{0,1:T(4,128)(2,1)S(1)}, bf16[128,4]{0,1:T(4,128)(2,1)}, u32[]{:S(2)}) copy-start(bf16[128,4]{0,1:T(4,128)(2,1)} %get-tuple-element.27) | copy-start | bytes 3076
  180.1 87.3 %copy-start.15 = (s32[48]{0:T(128)S(1)}, s32[48]{0:T(128)}, u32[]{:S(2)}) copy-start(s32[48]{0:T(128)} %copy-done.14) | copy-start | bytes 580
  180.1 105.6 %copy-start.13 = (s32[48]{0:T(128)S(1)}, s32[48]{0:T(128)}, u32[]{:S(2)}) copy-start(s32[48]{0:T(128)} %copy-done.12) | copy-start | bytes 580
  180.2 106.6 %copy-start.11 = (s32[48]{0:T(128)S(1)}, s32[48]{0:T(128)}, u32[]{:S(2)}) copy-start(s32[48]{0:T(128)} %copy-done.10) | copy-start | bytes 580
  180.2 119.5 %copy-start.9 = (s32[48]{0:T(128)S(1)}, s32[48]{0:T(128)}, u32[]{:S(2)}) copy-start(s32[48]{0:T(128)} %copy-done.8) | copy-start | bytes 580
  222.8 19.2 %all-to-all-start.11 = ((bf16[64,2,128]{2,1,0:T(2,128)(2,1)}), bf16[64,2,128]{2,1,0:T(2,128)(2,1)S(1)}, u32[]{:S(2)}, u32[]{:S(2)}) async-start(bf16[64,2,128]{2,1,0:T(2,128)(2,1)} %bitcast.50), calls=%async_computation.12 | async-start | bytes 65536 | tf_op jit(solution)/shard_map/all_to_all | solution.py:71
  242.0 19.1 %all-to-all-start.8 = ((bf16[64,2,128]{2,1,0:T(2,128)(2,1)}), bf16[64,2,128]{2,1,0:T(2,128)(2,1)S(1)}, u32[]{:S(2)}, u32[]{:S(2)}) async-start(bf16[64,2,128]{2,1,0:T(2,128)(2,1)} %bitcast.37), calls=%async_computation.9 | async-start | bytes 65536 | tf_op jit(solution)/shard_map/all_to_all | solution.py:71
  261.1 19.1 %all-to-all-start.5 = ((bf16[64,2,128]{2,1,0:T(2,128)(2,1)}), bf16[64,2,128]{2,1,0:T(2,128)(2,1)S(1)}, u32[]{:S(2)}, u32[]{:S(2)}) async-start(bf16[64,2,128]{2,1,0:T(2,128)(2,1)} %bitcast.24), calls=%async_computation.6 | async-start | bytes 65536 | tf_op jit(solution)/shard_map/all_to_all | solution.py:71
  280.2 19.4 %all-to-all-start.2 = ((bf16[64,2,128]{2,1,0:T(2,128)(2,1)}), bf16[64,2,128]{2,1,0:T(2,128)(2,1)S(1)}, u32[]{:S(2)}, u32[]{:S(2)}) async-start(bf16[64,2,128]{2,1,0:T(2,128)(2,1)} %bitcast.11), calls=%async_computation.3 | async-start | bytes 65536 | tf_op jit(solution)/shard_map/all_to_all | solution.py:71
Sparse Core Ops, SparseCore 0:
  158.0 40.8 reduce-scatter.1
where the time goes:
time: 309 us; the launch traced here: 308 us
  waiting for transfers between devices  157 us (51%)
  starting transfers between devices  81 us (26%)
  blocking collectives  25 us (8%)
  between operations  13.9 us (4%)
  matrix products  12.6 us (4%)
  local copies, waits for them, and re-layouts  10 us (3%)
  other arithmetic  8.13 us (3%)
    all_to_all x4, waiting for transfers between devices, body(): lax.all_to_all(send_rows, 'ad', split_axis=0, concat_axis=0, tiled=True)  57.2 us
    all_to_all x4, waiting for transfers between devices, body(): lax.all_to_all(send_tags, 'ad', split_axis=0, concat_axis=0, tiled=True)  50.4 us
    all_to_all x4, waiting for transfers between devices, body(): lax.all_to_all(adapter_update, 'ad', split_axis=0, concat_axis=0, tiled=T...  49.9 us
    all_to_all x4, starting transfers between devices, body(): lax.all_to_all(send_tags, 'ad', split_axis=0, concat_axis=0, tiled=True)  35.2 us
    psum x1, blocking collectives, adapter_row_output(): down_sum = lax.psum(down_part, 'tp')  25 us
    all_to_all x4, starting transfers between devices, body(): lax.all_to_all(send_rows, 'ad', split_axis=0, concat_axis=0, tiled=True)  24.1 us
    all_to_all x4, starting transfers between devices, body(): lax.all_to_all(adapter_update, 'ad', split_axis=0, concat_axis=0, tiled=T...  21.6 us
  transfers between devices with their start and end apart: 13, of which 12 were waited for; matrix products, arithmetic and copies ran while one was open for 7% of the time, Pallas kernels for 0%

commit v1 on v0

v1 whole, which is shorter than its diff:
```python
import jax
import jax.numpy as jnp
from jax import lax
from jax.sharding import PartitionSpec as P

CAP = 2
TAG_WIDTH = 128


def body(tokens, row_adapter_index, key_base_weight, adapter_down_weight, adapter_up_weight):
    step_count, row_dev, width_per_shard = tokens.shape
    groups = lax.axis_size("ad")
    adapter_number = adapter_down_weight.shape[0]
    rank = adapter_down_weight.shape[2]
    row_total = step_count * row_dev
    slots_per_group = step_count * CAP
    slot_total = groups * slots_per_group

    gathered_rows = tokens.reshape(row_total, width_per_shard)
    partial_base = jnp.dot(gathered_rows, key_base_weight, preferred_element_type=jnp.float32)
    base_keys_output = lax.psum_scatter(partial_base, "tp", scatter_dimension=1, tiled=True)
    key_feature_width = base_keys_output.shape[1]

    index_list = row_adapter_index.reshape(step_count, row_dev)
    owner_group = index_list // adapter_number
    local_index = index_list % adapter_number
    group_hits = (owner_group[:, :, None] == jnp.arange(groups, dtype=jnp.int32)[None, None, :]).astype(
        jnp.int32
    )
    slot_rank = jnp.sum((jnp.cumsum(group_hits, axis=1) - group_hits) * group_hits, axis=2)
    step_ids = jnp.arange(step_count, dtype=jnp.int32)[:, None]
    slot_index = (owner_group * slots_per_group + step_ids * CAP + slot_rank).reshape(row_total)
    dispatch = (
        slot_index[None, :] == jnp.arange(slot_total, dtype=jnp.int32)[:, None]
    ).astype(jnp.bfloat16)

    tag_values = (local_index + 1).astype(jnp.bfloat16).reshape(row_total, 1)
    tag_block = jnp.broadcast_to(tag_values, (row_total, TAG_WIDTH))
    rows_tagged = jnp.concatenate([gathered_rows, tag_block], axis=1)
    send_rows = jnp.dot(dispatch, rows_tagged, preferred_element_type=jnp.float32).astype(jnp.bfloat16)
    send_rows = send_rows.reshape(groups, slots_per_group, width_per_shard + TAG_WIDTH)
    incoming = lax.all_to_all(send_rows, "ad", split_axis=0, concat_axis=0, tiled=True)
    incoming = incoming.reshape(slot_total, width_per_shard + TAG_WIDTH)
    incoming_rows = incoming[:, :width_per_shard]
    incoming_labels = incoming[:, width_per_shard]

    down_all = jnp.einsum(
        "nd,adr->nar", incoming_rows, adapter_down_weight, preferred_element_type=jnp.float32
    )
    labels = (jnp.arange(adapter_number, dtype=jnp.int32) + 1).astype(jnp.bfloat16)
    selector = (incoming_labels[:, None] == labels[None, :]).astype(jnp.float32)
    down_part = jnp.sum(down_all * selector[:, :, None], axis=1)
    down_sum = lax.psum(down_part, "tp")
    down_low = down_sum.astype(jnp.bfloat16)
    spread_rows = (selector.astype(jnp.bfloat16)[:, :, None] * down_low[:, None, :]).reshape(
        slot_total, adapter_number * rank
    )
    up_flat = adapter_up_weight.reshape(adapter_number * rank, key_feature_width)
    adapter_update = jnp.dot(spread_rows, up_flat, preferred_element_type=jnp.float32).astype(
        jnp.bfloat16
    )
    adapter_update = adapter_update.reshape(groups, slots_per_group, key_feature_width)
    rows_sent_back = lax.all_to_all(adapter_update, "ad", split_axis=0, concat_axis=0, tiled=True)
    routed = jnp.dot(
        dispatch.T,
        rows_sent_back.reshape(slot_total, key_feature_width),
        preferred_element_type=jnp.float32,
    )
    out = (base_keys_output + routed).astype(jnp.bfloat16)
    return out.reshape(step_count, row_dev, key_feature_width)


def solution(mesh):
    placed = (
        P(None, "ad", "tp"),
        P(None, "ad"),
        P("tp", None),
        P("ad", "tp", None),
        P("ad", None, "tp"),
    )
    return jax.shard_map(
        body, mesh=mesh, in_specs=placed, out_specs=P(None, "ad", "tp"), check_vma=False
    )
```

time: 309 us -> 151 us (0.49)
  waiting for transfers between devices: 157 us -> 74.3 us
  starting transfers between devices: 81 us -> 26.6 us
  local copies, waits for them, and re-layouts: 10 us -> 1.31 us
  other arithmetic: 8.13 us -> 1.47 us
  matrix products: 12.6 us -> 8.57 us
    all_to_all x4 -> x0, waiting for transfers between devices: 50.4 us -> none  [body(): lax.all_to_all(send_tags, 'ad', split_axis=0, concat_axis=0, tiled=True)]
    all_to_all x4 -> x0, starting transfers between devices: 35.2 us -> none  [body(): lax.all_to_all(send_tags, 'ad', split_axis=0, concat_axis=0, tiled=True)]
    all_to_all x4 -> x1, waiting for transfers between devices: 49.9 us -> 15.2 us  [body(): lax.all_to_all(adapter_update, 'ad', split_axis=0, concat_axis=0, tiled=T...]
    all_to_all x4 -> x1, starting transfers between devices: 21.6 us -> 7.63 us  [body(): lax.all_to_all(adapter_update, 'ad', split_axis=0, concat_axis=0, tiled=T...]
    reshape x8 -> x0, local copies, waits for them, and re-layouts: 5.52 us -> none  [the longest x4 4.17 us: body(): send_rows = send_rows.reshape(groups, capacity, width_per_shard)]
    all_to_all x4 -> x1, starting transfers between devices: 24.1 us -> 18.9 us  [body(): lax.all_to_all(send_rows, 'ad', split_axis=0, concat_axis=0, tiled=True)]
    dot_general x16 -> x3, matrix products: 9.96 us -> 5.31 us  [the longest x1 2.56 us: body(): jnp.dot(dispatch, rows_tagged, preferred_element_type=jnp.float32)]
    all_to_all x4 -> x0, other arithmetic: 3.44 us -> none  [body(): lax.all_to_all(send_tags, 'ad', split_axis=0, concat_axis=0, tiled=True)]
  transfers between devices with their start and end apart: 13 -> 3, of which waited for: 12 -> 2; matrix products, arithmetic and copies ran while one was open for 7% -> 4% of each run, Pallas kernels for 0% -> 0%
where the time goes in v1:
time: 151 us
  waiting for transfers between devices  74.3 us (49%)
  starting transfers between devices  26.6 us (18%)
  blocking collectives  24.9 us (16%)
  between operations  13.5 us (9%)
  matrix products  8.57 us (6%)
    all_to_all x1, waiting for transfers between devices, body(): lax.all_to_all(send_rows, 'ad', split_axis=0, concat_axis=0, tiled=True)  59.1 us
    psum x1, blocking collectives, body(): down_sum = lax.psum(down_part, 'tp')  24.9 us
    all_to_all x1, starting transfers between devices, body(): lax.all_to_all(send_rows, 'ad', split_axis=0, concat_axis=0, tiled=True)  18.9 us
    all_to_all x1, waiting for transfers between devices, body(): lax.all_to_all(adapter_update, 'ad', split_axis=0, concat_axis=0, tiled=T...  15.2 us
    all_to_all x1, starting transfers between devices, body(): lax.all_to_all(adapter_update, 'ad', split_axis=0, concat_axis=0, tiled=T...  7.63 us
  transfers between devices with their start and end apart: 3, of which 2 were waited for; matrix products, arithmetic and copies ran while one was open for 4% of the time, Pallas kernels for 0%

profile of v1, /device:TPU:2, one launch (start us, length us, event | category | flops | bytes accessed | tf_op | source)
XLA Modules:
  0.0 150.7 jit_solution(14923197466587427254)
XLA Ops:
  6.5 0.0 copy-start
  6.5 0.8 fusion.18
  7.4 0.1 fusion.15
  7.5 0.1 reduce_window_sum.11
  7.6 0.2 select_reduce_fusion
  7.8 0.1 add_add_fusion
  7.9 0.1 eq.53
  8.0 0.1 broadcast_in_dim.4
  8.1 0.1 broadcast_in_dim.5
  8.2 2.6 %fusion = bf16[64,8,1152]{2,1,0:T(8,128)(2,1)} fusion(bf16[192,128]{1,0:T(8,128)(2,1)S(1)} %broadcast_in_dim.5, bf16[192,1024]{1,0:T(8,128)(2,1)} %bitcast.24, s32[192]{0:T(256)S(1)} %eq.53), kind=kOutput, calls=%fused_computation.1 | convolution fusion | flops 228065280 | bytes 1622784 | tf_op jit(solution)/shard_map/dot_general | solution.py:40
  10.7 0.0 copy-start.1
  10.7 18.9 %all-to-all-start = ((bf16[64,8,1152]{2,1,0:T(8,128)(2,1)}), bf16[64,8,1152]{2,1,0:T(8,128)(2,1)}, u32[]{:S(2)}, u32[]{:S(2)}) async-start(bf16[64,8,1152]{2,1,0:T(8,128)(2,1)} %fusion), calls=%async_computation.1 | async-start | bytes 2359296 | tf_op jit(solution)/shard_map/all_to_all | solution.py:42
  29.7 0.0 copy-start.2
  29.7 0.0 reduce-scatter.2.cloned.1.call-start
  29.7 0.0 copy-done
  29.7 0.0 copy-done.1
  29.7 1.5 fusion.21
  31.2 0.0 reduce-scatter.2.cloned.1.call-update
  31.3 59.1 %all-to-all-done = bf16[64,8,1152]{2,1,0:T(8,128)(2,1)} async-done(((bf16[64,8,1152]{2,1,0:T(8,128)(2,1)}), bf16[64,8,1152]{2,1,0:T(8,128)(2,1)}, u32[]{:S(2)}, u32[]{:S(2)}) %all-to-all-start) | async-done | bytes 1179680 | tf_op jit(solution)/shard_map/all_to_all | solution.py:42
  90.4 1.0 slice_reduce_fusion
  91.4 0.1 fusion.16
  91.5 0.0 copy-done.2
  91.5 0.0 copy-start.3
  91.5 1.8 %fusion.4 = f32[512,256]{0,1:S(1)} fusion(bf16[1024,256]{0,1:T(8,128)(2,1)S(1)} %bitcast.27, bf16[512,1152]{1,0:T(8,128)(2,1)} %bitcast.2), kind=kOutput, calls=%fused_computation.7 | convolution fusion | flops 268435456 | bytes 2097152
  93.3 0.1 multiply_reduce_fusion
  93.3 24.9 %all-reduce.1 = bf16[512,64]{0,1:T(8,128)(2,1)S(1)} all-reduce(f32[512,64]{0,1:T(8,128)S(1)} %multiply_reduce_fusion), channel_id=1, replica_groups=mesh['ad'=64,'tp'=8] {'tp'}, use_global_device_ids=true, to_apply=%region_4.5 | all-reduce | flops 32768 | bytes 196608 | tf_op jit(solution)/shard_map/psum | solution.py:53
  118.2 0.0 copy-done.3
  118.2 0.9 fusion.2
  119.1 7.6 %all-to-all-start.1 = ((bf16[64,8,128]{2,1,0:T(8,128)(2,1)}), bf16[64,8,128]{2,1,0:T(8,128)(2,1)S(1)}, u32[]{:S(2)}, u32[]{:S(2)}) async-start(bf16[64,8,128]{2,1,0:T(8,128)(2,1)} %fusion.2), calls=%async_computation.2 | async-start | bytes 262144 | tf_op jit(solution)/shard_map/all_to_all | solution.py:63
  126.8 0.0 reduce-scatter.2.cloned.1.call-done
  126.8 15.2 %all-to-all-done.1 = bf16[64,8,128]{2,1,0:T(8,128)(2,1)S(1)} async-done(((bf16[64,8,128]{2,1,0:T(8,128)(2,1)}), bf16[64,8,128]{2,1,0:T(8,128)(2,1)S(1)}, u32[]{:S(2)}, u32[]{:S(2)}) %all-to-all-start.1) | async-done | bytes 131104 | tf_op jit(solution)/shard_map/all_to_all | solution.py:63
  142.0 1.8 %fusion.3 = bf16[192,128]{1,0:T(8,128)(2,1)} fusion(f32[192,128]{1,0:T(8,128)} %reduce-scatter.2.cloned.1.call-done, s32[192]{0:T(256)S(1)} %eq.53, bf16[64,8,128]{2,1,0:T(8,128)(2,1)S(1)} %all-to-all-done.1), kind=kOutput, calls=%fused_computation.6 | convolution fusion | flops 25313280 | bytes 279296 | tf_op jit(solution)/shard_map/dot_general | solution.py:64
  (2 shorter events, 0.0 us)
Async XLA Ops:
  6.5 23.2 %copy-start = (bf16[1024,1024]{1,0:T(8,128)(2,1)S(1)}, bf16[1024,1024]{1,0:T(8,128)(2,1)}, u32[]{:S(2)}) copy-start(bf16[1024,1024]{1,0:T(8,128)(2,1)} %param.7) | copy-start | bytes 6291460
  10.7 19.0 %copy-start.1 = (bf16[4,48,1024]{2,1,0:T(8,128)(2,1)S(1)}, bf16[4,48,1024]{2,1,0:T(8,128)(2,1)}, u32[]{:S(2)}) copy-start(bf16[4,48,1024]{2,1,0:T(8,128)(2,1)} %param.5) | copy-start | bytes 1179652
  10.7 79.7 %all-to-all-start = ((bf16[64,8,1152]{2,1,0:T(8,128)(2,1)}), bf16[64,8,1152]{2,1,0:T(8,128)(2,1)}, u32[]{:S(2)}, u32[]{:S(2)}) async-start(bf16[64,8,1152]{2,1,0:T(8,128)(2,1)} %fusion), calls=%async_computation.1 | async-start | bytes 2359296 | tf_op jit(solution)/shard_map/all_to_all | solution.py:42
  29.7 61.8 %copy-start.2 = (bf16[4,1024,64]{1,2,0:T(8,128)(2,1)S(1)}, bf16[4,1024,64]{1,2,0:T(8,128)(2,1)}, u32[]{:S(2)}) copy-start(bf16[4,1024,64]{1,2,0:T(8,128)(2,1)} %param.8) | copy-start | bytes 1572868
  29.7 97.1 %reduce-scatter.2.cloned.1.call-start = ((), (), s32[]{:S(2)}) async-start(), calls=%async_computation.3 | async-start | bytes 884736 | tf_op jit(solution)/shard_map/reduce_scatter | solution.py:21
  91.5 26.7 %copy-start.3 = (bf16[4,64,128]{2,1,0:T(8,128)(2,1)S(1)}, bf16[4,64,128]{2,1,0:T(8,128)(2,1)}, u32[]{:S(2)}) copy-start(bf16[4,64,128]{2,1,0:T(8,128)(2,1)} %param.9) | copy-start | bytes 196612
  119.1 22.8 %all-to-all-start.1 = ((bf16[64,8,128]{2,1,0:T(8,128)(2,1)}), bf16[64,8,128]{2,1,0:T(8,128)(2,1)S(1)}, u32[]{:S(2)}, u32[]{:S(2)}) async-start(bf16[64,8,128]{2,1,0:T(8,128)(2,1)} %fusion.2), calls=%async_computation.2 | async-start | bytes 262144 | tf_op jit(solution)/shard_map/all_to_all | solution.py:63
Sparse Core Ops, SparseCore 0:
  33.3 41.2 reduce-scatter.1

commit v2 on v1

v2 whole, which is shorter than its diff:
```python
import jax
import jax.numpy as jnp
from jax import lax
from jax.sharding import PartitionSpec as P

TAG_WIDTH = 128


def body(tokens, row_adapter_index, key_base_weight, adapter_down_weight, adapter_up_weight):
    step_count, row_dev, width_per_shard = tokens.shape
    groups = lax.axis_size("ad")
    me = lax.axis_index("ad")
    adapter_number = adapter_down_weight.shape[0]
    rank = adapter_down_weight.shape[2]
    row_total = step_count * row_dev
    regular_total = groups * step_count
    wide = width_per_shard + TAG_WIDTH

    gathered_rows = tokens.reshape(row_total, width_per_shard)

    index_list = row_adapter_index.reshape(step_count, row_dev)
    owner_group = index_list // adapter_number
    local_index = index_list % adapter_number
    group_hits = (owner_group[:, :, None] == jnp.arange(groups, dtype=jnp.int32)[None, None, :]).astype(
        jnp.int32
    )
    slot_rank = jnp.sum((jnp.cumsum(group_hits, axis=1) - group_hits) * group_hits, axis=2)
    step_ids = jnp.arange(step_count, dtype=jnp.int32)[:, None]
    first = slot_rank == 0
    regular_slot = jnp.where(first, owner_group * step_count + step_ids, -1).reshape(row_total)
    overflow_slot = jnp.where(slot_rank == 1, step_ids, -1).reshape(row_total)
    dispatch = (
        regular_slot[None, :] == jnp.arange(regular_total, dtype=jnp.int32)[:, None]
    ).astype(jnp.bfloat16)
    dispatch_over = (
        overflow_slot[None, :] == jnp.arange(step_count, dtype=jnp.int32)[:, None]
    ).astype(jnp.bfloat16)

    tag_values = jnp.where(first, local_index + 1, index_list + 1).astype(jnp.bfloat16)
    tag_block = jnp.broadcast_to(tag_values.reshape(row_total, 1), (row_total, TAG_WIDTH))
    rows_tagged = jnp.concatenate([gathered_rows, tag_block], axis=1)
    send_rows = jnp.dot(dispatch, rows_tagged, preferred_element_type=jnp.float32).astype(jnp.bfloat16)
    send_rows = send_rows.reshape(groups, step_count, wide)
    send_over = jnp.dot(dispatch_over, rows_tagged, preferred_element_type=jnp.float32).astype(
        jnp.bfloat16
    )
    incoming_over = lax.all_gather(send_over, "ad", tiled=True)
    incoming = lax.all_to_all(send_rows, "ad", split_axis=0, concat_axis=0, tiled=True)

    partial_base = jnp.dot(gathered_rows, key_base_weight, preferred_element_type=jnp.float32)
    partial_base, incoming_over = lax.optimization_barrier((partial_base, incoming_over))
    base_keys_output = lax.psum_scatter(partial_base, "tp", scatter_dimension=1, tiled=True)
    key_feature_width = base_keys_output.shape[1]

    incoming = jnp.concatenate([incoming.reshape(regular_total, wide), incoming_over], axis=0)
    slot_total = incoming.shape[0]
    incoming_rows = incoming[:, :width_per_shard]
    regular_labels = incoming[:regular_total, width_per_shard].astype(jnp.float32)
    over_labels = incoming[regular_total:, width_per_shard].astype(jnp.float32) - (
        me * adapter_number
    ).astype(jnp.float32)
    incoming_labels = jnp.concatenate([regular_labels, over_labels])

    down_all = jnp.einsum(
        "nd,adr->nar", incoming_rows, adapter_down_weight, preferred_element_type=jnp.float32
    )
    labels = (jnp.arange(adapter_number, dtype=jnp.int32) + 1).astype(jnp.float32)
    selector = (incoming_labels[:, None] == labels[None, :]).astype(jnp.float32)
    down_part = jnp.sum(down_all * selector[:, :, None], axis=1)
    down_sum = lax.psum(down_part, "tp")
    down_low = down_sum.astype(jnp.bfloat16)
    spread_rows = (selector.astype(jnp.bfloat16)[:, :, None] * down_low[:, None, :]).reshape(
        slot_total, adapter_number * rank
    )
    up_flat = adapter_up_weight.reshape(adapter_number * rank, key_feature_width)
    adapter_update = jnp.dot(spread_rows, up_flat, preferred_element_type=jnp.float32).astype(
        jnp.bfloat16
    )
    update_regular = adapter_update[:regular_total].reshape(groups, step_count, key_feature_width)
    update_over = adapter_update[regular_total:].reshape(groups, step_count, key_feature_width)
    send_back = jnp.concatenate([update_regular, update_over], axis=1)
    rows_sent_back = lax.all_to_all(send_back, "ad", split_axis=0, concat_axis=0, tiled=True)
    back_regular = rows_sent_back[:, :step_count].reshape(regular_total, key_feature_width)
    back_over = jnp.sum(rows_sent_back[:, step_count:].astype(jnp.float32), axis=0)
    routed = jnp.dot(dispatch.T, back_regular, preferred_element_type=jnp.float32) + jnp.dot(
        dispatch_over.T.astype(jnp.float32), back_over, preferred_element_type=jnp.float32
    )
    out = (base_keys_output + routed).astype(jnp.bfloat16)
    return out.reshape(step_count, row_dev, key_feature_width)


def solution(mesh):
    placed = (
        P(None, "ad", "tp"),
        P(None, "ad"),
        P("tp", None),
        P("ad", "tp", None),
        P("ad", None, "tp"),
    )
    return jax.shard_map(
        body, mesh=mesh, in_specs=placed, out_specs=P(None, "ad", "tp"), check_vma=False
    )
```

time: 151 us -> 222 us (1.47)
  blocking collectives: 24.9 us -> 174 us
  waiting for transfers between devices: 74.3 us -> 0.03 us
  starting transfers between devices: 26.6 us -> 18.7 us
  other arithmetic: 1.47 us -> 4.05 us
    all_gather x0 -> x1, blocking collectives: none -> 121 us  [body(): incoming_over = lax.all_gather(send_over, 'ad', tiled=True)]
    all_to_all x1, waiting for transfers between devices: 59.1 us -> 0.01 us  [body(): lax.all_to_all(send_rows, 'ad', split_axis=0, concat_axis=0, tiled=True)]
    all_to_all x0 -> x1, blocking collectives: none -> 28.5 us  [body(): lax.all_to_all(send_back, 'ad', split_axis=0, concat_axis=0, tiled=True)]
    all_to_all x1 -> x0, waiting for transfers between devices: 15.2 us -> none  [body(): lax.all_to_all(adapter_update, 'ad', split_axis=0, concat_axis=0, tiled=T...]
    all_to_all x1 -> x0, starting transfers between devices: 7.63 us -> none  [body(): lax.all_to_all(adapter_update, 'ad', split_axis=0, concat_axis=0, tiled=T...]
  transfers between devices with their start and end apart: 3 -> 2, of which waited for: 2 -> 0; matrix products, arithmetic and copies ran while one was open for 4% -> 4% of each run, Pallas kernels for 0% -> 0%
where the time goes in v2:
time: 222 us; the launch traced here: 221 us
  blocking collectives  174 us (78%)
  starting transfers between devices  18.7 us (8%)
  between operations  13.5 us (6%)
  matrix products  7.98 us (4%)
  other arithmetic  4.05 us (2%)
  local copies, waits for them, and re-layouts  3.28 us (1%)
    all_gather x1, blocking collectives, body(): incoming_over = lax.all_gather(send_over, 'ad', tiled=True)  121 us
    all_to_all x1, blocking collectives, body(): lax.all_to_all(send_back, 'ad', split_axis=0, concat_axis=0, tiled=True)  28.5 us
    psum x1, blocking collectives, body(): down_sum = lax.psum(down_part, 'tp')  24.9 us
    all_to_all x1, starting transfers between devices, body(): lax.all_to_all(send_rows, 'ad', split_axis=0, concat_axis=0, tiled=True)  18.6 us
  transfers between devices with their start and end apart: 2, of which 0 were waited for; matrix products, arithmetic and copies ran while one was open for 4% of the time, Pallas kernels for 0%

profile of v2, /device:TPU:2, one launch (start us, length us, event | category | flops | bytes accessed | tf_op | source)
XLA Modules:
  0.0 221.5 jit_solution(2728375814923560662)
XLA Ops:
  6.5 0.0 copy-start
  6.5 0.0 copy-start.2
  6.5 0.8 add_select_fusion.1
  7.4 0.1 fusion.11
  7.5 0.1 reduce_window_sum.11
  7.6 0.2 select_reduce_fusion
  7.8 0.7 add_select_fusion.2
  8.5 0.7 fusion.15
  9.2 0.1 broadcast_in_dim.19
  9.3 0.1 eq.83
  9.4 0.1 broadcast_in_dim.20
  9.5 1.3 convolution_convert_fusion
  10.8 1.0 reshape.110
  11.8 18.6 %all-to-all-start = ((bf16[64,4,1152]{2,1,0:T(4,128)(2,1)}), bf16[64,4,1152]{2,1,0:T(4,128)(2,1)S(1)}, u32[]{:S(2)}, u32[]{:S(2)}) async-start(bf16[64,4,1152]{2,1,0:T(4,128)(2,1)} %reshape.110), calls=%async_computation.1 | async-start | bytes 1179648 | tf_op jit(solution)/shard_map/all_to_all | solution.py:48
  30.4 0.0 reduce-scatter.2.cloned.1.call-start
  30.5 0.1 select_n.32
  30.6 0.0 copy-done.2
  30.6 0.2 fusion
  30.7 120.6 %all-gather = bf16[64,4,1152]{2,1,0:T(4,128)(2,1)S(1)} all-gather(bf16[1,4,1152]{2,1,0:T(4,128)(2,1)S(1)} %fusion), channel_id=1, replica_groups=mesh['ad'=64,'tp'=8] {'ad'}, dimensions={0}, use_global_device_ids=true | all-gather | bytes 599040 | tf_op jit(solution)/shard_map/all_gather | solution.py:47
  151.3 1.0 reshape.118
  152.3 0.0 copy-done
  152.3 0.0 copy-start.1
  152.3 2.5 %fusion.25 = f32[192,1024]{1,0:T(8,128)} fusion(bf16[192,1024]{1,0:T(8,128)(2,1)} %bitcast.23, bf16[1024,1024]{1,0:T(8,128)(2,1)S(1)} %copy-done), kind=kOutput, calls=%fused_computation.52 | convolution fusion | flops 402653184 | bytes 3276800 | tf_op jit(solution)/shard_map/dot_general | solution.py:50
  154.8 0.0 reduce-scatter.2.cloned.1.call-update
  154.9 0.0 copy-done.1
  154.9 0.1 subtract_reduce_fusion
  155.0 0.0 all-to-all-done
  155.0 1.0 reshape.111
  156.0 0.0 copy-start.3
  156.0 1.0 convert_reduce_fusion
  156.9 1.7 fusion.4
  158.7 0.1 fusion.23
  158.7 0.1 multiply_reduce_fusion
  158.8 24.9 %all-reduce.1 = bf16[512,64]{0,1:T(8,128)(2,1)S(1)} all-reduce(f32[512,64]{0,1:T(8,128)S(1)} %multiply_reduce_fusion), channel_id=1, replica_groups=mesh['ad'=64,'tp'=8] {'tp'}, use_global_device_ids=true, to_apply=%region_4.5 | all-reduce | flops 32768 | bytes 196608 | tf_op jit(solution)/shard_map/psum | solution.py:70
  183.7 0.0 copy-done.3
  183.7 0.3 fusion.1
  184.0 0.1 pad_maximum_fusion.5
  184.0 28.5 %all_to_all.10 = bf16[64,8,128]{2,1,0:T(8,128)(2,1)S(1)} all-to-all(bf16[64,8,128]{2,1,0:T(8,128)(2,1)S(1)} %pad_maximum_fusion.5), channel_id=1, replica_groups=mesh['ad'=64,'tp'=8] {'ad'}, dimensions={0} | all-to-all | bytes 262144 | tf_op jit(solution)/shard_map/all_to_all | solution.py:82
  212.6 0.1 convert_reduce_fusion.1
  212.6 0.2 fusion.12
  212.9 0.0 reduce-scatter.2.cloned.1.call-done
  212.9 1.8 fusion.3
  (4 shorter events, 0.0 us)
Async XLA Ops:
  6.5 145.8 %copy-start = (bf16[1024,1024]{1,0:T(8,128)(2,1)S(1)}, bf16[1024,1024]{1,0:T(8,128)(2,1)}, u32[]{:S(2)}) copy-start(bf16[1024,1024]{1,0:T(8,128)(2,1)} %param.7) | copy-start | bytes 6291460
  6.5 24.0 %copy-start.2 = (bf16[4,48,1024]{2,1,0:T(8,128)(2,1)S(1)}, bf16[4,48,1024]{2,1,0:T(8,128)(2,1)}, u32[]{:S(2)}) copy-start(bf16[4,48,1024]{2,1,0:T(8,128)(2,1)} %param.5) | copy-start | bytes 1179652
  11.8 143.2 %all-to-all-start = ((bf16[64,4,1152]{2,1,0:T(4,128)(2,1)}), bf16[64,4,1152]{2,1,0:T(4,128)(2,1)S(1)}, u32[]{:S(2)}, u32[]{:S(2)}) async-start(bf16[64,4,1152]{2,1,0:T(4,128)(2,1)} %reshape.110), calls=%async_computation.1 | async-start | bytes 1179648 | tf_op jit(solution)/shard_map/all_to_all | solution.py:48
  30.4 182.5 %reduce-scatter.2.cloned.1.call-start = ((), (), s32[]{:S(2)}) async-start(), calls=%async_computation.3 | async-start | bytes 884736 | tf_op jit(solution)/shard_map/reduce_scatter | solution.py:52
  152.3 2.6 %copy-start.1 = (bf16[256,1152]{1,0:T(8,128)(2,1)S(1)}, bf16[256,1152]{1,0:T(8,128)(2,1)}, u32[]{:S(2)}) copy-start(bf16[256,1152]{1,0:T(8,128)(2,1)} %reshape.118) | copy-start | bytes 1769476
  156.0 27.7 %copy-start.3 = (bf16[4,64,128]{2,1,0:T(8,128)(2,1)S(1)}, bf16[4,64,128]{2,1,0:T(8,128)(2,1)}, u32[]{:S(2)}) copy-start(bf16[4,64,128]{2,1,0:T(8,128)(2,1)} %param.9) | copy-start | bytes 196612
Sparse Core Ops, SparseCore 0:
  155.0 38.6 reduce-scatter.1

commit v3 on v1

--- a/solution.py
+++ b/solution.py
@@ -50,7 +50,8 @@
     labels = (jnp.arange(adapter_number, dtype=jnp.int32) + 1).astype(jnp.bfloat16)
     selector = (incoming_labels[:, None] == labels[None, :]).astype(jnp.float32)
     down_part = jnp.sum(down_all * selector[:, :, None], axis=1)
-    down_sum = lax.psum(down_part, "tp")
+    down_part, base_keys_output = lax.optimization_barrier((down_part, base_keys_output))
+    down_sum = jnp.sum(lax.all_gather(down_part, "tp"), axis=0)
     down_low = down_sum.astype(jnp.bfloat16)
     spread_rows = (selector.astype(jnp.bfloat16)[:, :, None] * down_low[:, None, :]).reshape(
         slot_total, adapter_number * rank

time: 151 us -> 160 us (1.060)
  waiting for transfers between devices: 74.3 us -> 82 us
  blocking collectives: 24.9 us -> 32.5 us
  starting transfers between devices: 26.6 us -> 19 us
  local copies, waits for them, and re-layouts: 1.31 us -> 3.17 us
    all_to_all x0 -> x1, blocking collectives: none -> 32.5 us  [body(): lax.all_to_all(adapter_update, 'ad', split_axis=0, concat_axis=0, tiled=T...]
    psum x1 -> x0, blocking collectives: 24.9 us -> none  [body(): down_sum = lax.psum(down_part, 'tp')]
    all_gather x0 -> x1, waiting for transfers between devices: none -> 22.9 us  [body(): down_sum = jnp.sum(lax.all_gather(down_part, 'tp'), axis=0)]
    all_to_all x1 -> x0, waiting for transfers between devices: 15.2 us -> none  [body(): lax.all_to_all(adapter_update, 'ad', split_axis=0, concat_axis=0, tiled=T...]
    all_to_all x1 -> x0, starting transfers between devices: 7.63 us -> none  [body(): lax.all_to_all(adapter_update, 'ad', split_axis=0, concat_axis=0, tiled=T...]
    unnamed x8 -> x11, local copies, waits for them, and re-layouts: 0.02 us -> 1.88 us
  transfers between devices with their start and end apart: 3 -> 3, of which waited for: 2 -> 2; matrix products, arithmetic and copies ran while one was open for 4% -> 3% of each run, Pallas kernels for 0% -> 0%
where the time goes in v3:
time: 160 us
  waiting for transfers between devices  82 us (51%)
  blocking collectives  32.5 us (20%)
  starting transfers between devices  19 us (12%)
  between operations  13.5 us (8%)
  matrix products  7.01 us (4%)
  local copies, waits for them, and re-layouts  3.17 us (2%)
  other arithmetic  2.38 us (1%)
    all_to_all x1, waiting for transfers between devices, body(): lax.all_to_all(send_rows, 'ad', split_axis=0, concat_axis=0, tiled=True)  59.1 us
    all_to_all x1, blocking collectives, body(): lax.all_to_all(adapter_update, 'ad', split_axis=0, concat_axis=0, tiled=T...  32.5 us
    all_gather x1, waiting for transfers between devices, body(): down_sum = jnp.sum(lax.all_gather(down_part, 'tp'), axis=0)  22.9 us
    all_to_all x1, starting transfers between devices, body(): lax.all_to_all(send_rows, 'ad', split_axis=0, concat_axis=0, tiled=True)  18.9 us
  transfers between devices with their start and end apart: 3, of which 2 were waited for; matrix products, arithmetic and copies ran while one was open for 3% of the time, Pallas kernels for 0%

profile of v3, /device:TPU:2, one launch (start us, length us, event | category | flops | bytes accessed | tf_op | source)
XLA Modules:
  0.0 159.6 jit_solution(1004776902123214604)
XLA Ops:
  6.5 0.0 copy-start
  6.5 0.8 add_select_fusion.1
  7.4 0.1 fusion.15
  7.5 0.1 reduce_window_sum.11
  7.6 0.2 select_reduce_fusion
  7.8 0.1 add_add_fusion
  7.9 0.1 eq.53
  8.0 0.1 broadcast_in_dim.4
  8.1 0.1 broadcast_in_dim.5
  8.2 2.6 %fusion = bf16[64,8,1152]{2,1,0:T(8,128)(2,1)} fusion(bf16[192,128]{1,0:T(8,128)(2,1)S(1)} %broadcast_in_dim.5, bf16[192,1024]{1,0:T(8,128)(2,1)} %bitcast.29, s32[192]{0:T(256)S(1)} %eq.53), kind=kOutput, calls=%fused_computation.1 | convolution fusion | flops 228065280 | bytes 1622784 | tf_op jit(solution)/shard_map/dot_general | solution.py:40
  10.7 0.0 copy-start.1
  10.7 18.9 %all-to-all-start = ((bf16[64,8,1152]{2,1,0:T(8,128)(2,1)}), bf16[64,8,1152]{2,1,0:T(8,128)(2,1)}, u32[]{:S(2)}, u32[]{:S(2)}) async-start(bf16[64,8,1152]{2,1,0:T(8,128)(2,1)} %fusion), calls=%async_computation | async-start | bytes 2359296 | tf_op jit(solution)/shard_map/all_to_all | solution.py:42
  29.7 0.0 copy-start.2
  29.7 0.0 reduce-scatter.2.cloned.1.call-start
  29.7 0.0 copy-done
  29.7 0.0 copy-done.1
  29.7 1.5 fusion.21
  31.2 0.0 reduce-scatter.2.cloned.1.call-update
  31.3 0.0 all-gather.3.cloned.1.call-start
  31.3 59.1 %all-to-all-done = bf16[64,8,1152]{2,1,0:T(8,128)(2,1)} async-done(((bf16[64,8,1152]{2,1,0:T(8,128)(2,1)}), bf16[64,8,1152]{2,1,0:T(8,128)(2,1)}, u32[]{:S(2)}, u32[]{:S(2)}) %all-to-all-start) | async-done | bytes 1179680 | tf_op jit(solution)/shard_map/all_to_all | solution.py:42
  90.4 1.0 slice_reduce_fusion
  91.4 0.1 fusion.16
  91.5 0.0 copy-done.2
  91.5 1.8 %fusion.4 = f32[512,256]{0,1:S(1)} fusion(bf16[1024,256]{0,1:T(8,128)(2,1)S(1)} %bitcast.33, bf16[512,1152]{1,0:T(8,128)(2,1)} %bitcast.2), kind=kOutput, calls=%fused_computation.8 | convolution fusion | flops 268435456 | bytes 2097152
  93.3 0.7 multiply_reduce_fusion
  94.0 0.0 reduce-scatter.2.cloned.1.call-done
  94.0 0.0 all-gather.3.cloned.1.call-update
  94.0 22.9 %all-gather.3.cloned.1.call-done = f32[4096,64]{0,1:T(8,128)} async-done(((f32[512,64]{0,1:T(8,128)}), f32[4096,64]{0,1:T(8,128)}) %all-gather.3.cloned.1.call-update) | async-done | bytes 1048592 | tf_op jit(solution)/shard_map/all_gather | solution.py:54
  116.8 0.0 copy-start.4
  116.9 1.9 %copy.6 = f32[8,8,8,512]{3,2,1,0:T(8,128)S(1)} copy(f32[8,8,8,512]{3,1,2,0:T(8,128)} %bitcast.31) | data formatting | bytes 2097152
  118.7 0.0 copy-start.3
  118.7 0.3 bitcast_reduce_fusion
  119.0 0.0 copy-done.4
  119.0 0.3 fusion.2
  119.3 32.5 %all_to_all.10 = bf16[64,8,128]{2,1,0:T(8,128)(2,1)S(1)} all-to-all(bf16[64,8,128]{2,1,0:T(8,128)(2,1)S(1)} %fusion.2), channel_id=1, replica_groups=mesh['ad'=64,'tp'=8] {'ad'}, dimensions={0} | all-to-all | bytes 262144 | tf_op jit(solution)/shard_map/all_to_all | solution.py:64
  151.8 0.0 copy-done.3
  151.8 0.9 fusion.3
  (2 shorter events, 0.0 us)
Async XLA Ops:
  6.5 23.2 %copy-start = (bf16[1024,1024]{1,0:T(8,128)(2,1)S(1)}, bf16[1024,1024]{1,0:T(8,128)(2,1)}, u32[]{:S(2)}) copy-start(bf16[1024,1024]{1,0:T(8,128)(2,1)} %param.7) | copy-start | bytes 6291460
  10.7 19.0 %copy-start.1 = (bf16[4,48,1024]{2,1,0:T(8,128)(2,1)S(1)}, bf16[4,48,1024]{2,1,0:T(8,128)(2,1)}, u32[]{:S(2)}) copy-start(bf16[4,48,1024]{2,1,0:T(8,128)(2,1)} %param.5) | copy-start | bytes 1179652
  10.7 79.7 %all-to-all-start = ((bf16[64,8,1152]{2,1,0:T(8,128)(2,1)}), bf16[64,8,1152]{2,1,0:T(8,128)(2,1)}, u32[]{:S(2)}, u32[]{:S(2)}) async-start(bf16[64,8,1152]{2,1,0:T(8,128)(2,1)} %fusion), calls=%async_computation | async-start | bytes 2359296 | tf_op jit(solution)/shard_map/all_to_all | solution.py:42
  29.7 61.8 %copy-start.2 = (bf16[4,1024,64]{1,2,0:T(8,128)(2,1)S(1)}, bf16[4,1024,64]{1,2,0:T(8,128)(2,1)}, u32[]{:S(2)}) copy-start(bf16[4,1024,64]{1,2,0:T(8,128)(2,1)} %param.8) | copy-start | bytes 1572868
  29.7 64.3 %reduce-scatter.2.cloned.1.call-start = ((), (), s32[]{:S(2)}) async-start(), calls=%async_computation.3 | async-start | bytes 884736 | tf_op jit(solution)/shard_map/reduce_scatter | solution.py:21
  31.3 85.6 %all-gather.3.cloned.1.call-start = ((), (), s32[]{:S(2)}) async-start(), calls=%async_computation.4 | async-start | bytes 1179648 | tf_op jit(solution)/shard_map/all_gather | solution.py:54
  116.8 2.1 %copy-start.4 = (bf16[4,64,128]{2,1,0:T(8,128)(2,1)S(1)}, bf16[4,64,128]{2,1,0:T(8,128)(2,1)}, u32[]{:S(2)}) copy-start(bf16[4,64,128]{2,1,0:T(8,128)(2,1)} %param.9) | copy-start | bytes 196612
  118.7 33.1 %copy-start.3 = (f32[192,128]{1,0:T(8,128)S(1)}, f32[192,128]{1,0:T(8,128)}, u32[]{:S(2)}) copy-start(f32[192,128]{1,0:T(8,128)} %reduce-scatter.2.cloned.1.call-done) | copy-start | bytes 294916
Sparse Core Ops, SparseCore 0:
  33.3 41.2 reduce-scatter.1
  94.1 22.7 all-gather.2

commit v4 on v1

--- a/solution.py
+++ b/solution.py
@@ -35,14 +35,17 @@
     ).astype(jnp.bfloat16)
 
     tag_values = (local_index + 1).astype(jnp.bfloat16).reshape(row_total, 1)
-    tag_block = jnp.broadcast_to(tag_values, (row_total, TAG_WIDTH))
-    rows_tagged = jnp.concatenate([gathered_rows, tag_block], axis=1)
-    send_rows = jnp.dot(dispatch, rows_tagged, preferred_element_type=jnp.float32).astype(jnp.bfloat16)
-    send_rows = send_rows.reshape(groups, slots_per_group, width_per_shard + TAG_WIDTH)
-    incoming = lax.all_to_all(send_rows, "ad", split_axis=0, concat_axis=0, tiled=True)
-    incoming = incoming.reshape(slot_total, width_per_shard + TAG_WIDTH)
-    incoming_rows = incoming[:, :width_per_shard]
-    incoming_labels = incoming[:, width_per_shard]
+    send_rows = jnp.dot(dispatch, gathered_rows, preferred_element_type=jnp.float32).astype(jnp.bfloat16)
+    send_tags = jnp.dot(dispatch, tag_values, preferred_element_type=jnp.float32).astype(jnp.bfloat16)
+    send_tags = jnp.pad(send_tags.reshape(groups, slots_per_group), ((0, 0), (0, TAG_WIDTH - slots_per_group)))
+    send_all = jnp.concatenate(
+        [send_rows.reshape(groups, slots_per_group * width_per_shard), send_tags], axis=1
+    )
+    incoming = lax.all_to_all(send_all, "ad", split_axis=0, concat_axis=0, tiled=True)
+    incoming_rows = incoming[:, : slots_per_group * width_per_shard].reshape(slot_total, width_per_shard)
+    incoming_labels = incoming[:, slots_per_group * width_per_shard :][:, :slots_per_group].reshape(
+        slot_total
+    )
 
     down_all = jnp.einsum(
         "nd,adr->nar", incoming_rows, adapter_down_weight, preferred_element_type=jnp.float32

time: 151 us -> 160 us (1.060)
  local copies, waits for them, and re-layouts: 1.31 us -> 12.8 us
  waiting for transfers between devices: 74.3 us -> 69.2 us
  other arithmetic: 1.47 us -> 4.91 us
    unnamed x8 -> x7, local copies, waits for them, and re-layouts: 0.02 us -> 7.92 us
    all_to_all x1, waiting for transfers between devices: 59.1 us -> 54 us  [body(): lax.all_to_all(send_all, 'ad', split_axis=0, concat_axis=0, tiled=True)]
    all_to_all x0 -> x2, other arithmetic: none -> 3.44 us  [body(): lax.all_to_all(send_all, 'ad', split_axis=0, concat_axis=0, tiled=True)]
    reshape x0 -> x4, local copies, waits for them, and re-layouts: none -> 3.1 us  [the longest x1 1.59 us: body(): incoming[:, :slots_per_group * width_per_shard]]
  transfers between devices with their start and end apart: 3 -> 3, of which waited for: 2 -> 2; matrix products, arithmetic and copies ran while one was open for 4% -> 8% of each run, Pallas kernels for 0% -> 0%
where the time goes in v4:
time: 160 us
  waiting for transfers between devices  69.2 us (43%)
  starting transfers between devices  26 us (16%)
  blocking collectives  24.9 us (16%)
  between operations  13.5 us (8%)
  local copies, waits for them, and re-layouts  12.8 us (8%)
  matrix products  8.41 us (5%)
  other arithmetic  4.91 us (3%)
    all_to_all x1, waiting for transfers between devices, body(): lax.all_to_all(send_all, 'ad', split_axis=0, concat_axis=0, tiled=True)  54 us
    psum x1, blocking collectives, body(): down_sum = lax.psum(down_part, 'tp')  24.9 us
    all_to_all x1, starting transfers between devices, body(): lax.all_to_all(send_all, 'ad', split_axis=0, concat_axis=0, tiled=True)  18.6 us
    all_to_all x1, waiting for transfers between devices, body(): lax.all_to_all(adapter_update, 'ad', split_axis=0, concat_axis=0, tiled=T...  15.2 us
    unnamed x7, local copies, waits for them, and re-layouts  7.92 us
    all_to_all x1, starting transfers between devices, body(): lax.all_to_all(adapter_update, 'ad', split_axis=0, concat_axis=0, tiled=T...  7.31 us
    all_to_all x2, other arithmetic, body(): lax.all_to_all(send_all, 'ad', split_axis=0, concat_axis=0, tiled=True)  3.44 us
  transfers between devices with their start and end apart: 3, of which 2 were waited for; matrix products, arithmetic and copies ran while one was open for 8% of the time, Pallas kernels for 0%

profile of v4, /device:TPU:2, one launch (start us, length us, event | category | flops | bytes accessed | tf_op | source)
XLA Modules:
  0.0 159.7 jit_solution(3485160766764923592)
XLA Ops:
  6.5 0.0 copy-start
  6.5 0.8 fusion.17
  7.4 0.1 fusion.14
  7.5 0.1 reduce_window_sum.11
  7.6 0.2 select_reduce_fusion
  7.8 0.1 add_add_fusion
  7.9 0.1 eq.55
  8.0 1.4 convolution_convert_fusion
  9.4 1.3 reshape.109
  10.7 0.1 reshape.116
  10.8 0.2 fusion.6
  11.1 0.1 reshape.111
  11.2 1.3 fusion.5
  12.5 0.5 broadcast.94
  13.0 2.1 %reduce = bf16[64,8320]{1,0:T(8,128)(2,1)} reduce(bf16[64,1,8320]{2,0,1:T(8,128)(2,1)S(1)} %fusion.5, bf16[]{:T(256)} %broadcast.94), dimensions={1}, to_apply=%copy.8.reduce_sub_computation | reduce | bytes 2129922 | tf_op jit(solution)/shard_map/all_to_all | solution.py:44
  15.1 2.6 %reshape.122 = bf16[64,2,4160]{2,1,0:T(2,128)(2,1)} reshape(bf16[64,8320]{1,0:T(8,128)(2,1)} %reduce) | data formatting | bytes 2129920
  17.7 18.6 %all-to-all-start = ((bf16[64,2,4160]{2,1,0:T(2,128)(2,1)}), bf16[64,2,4160]{2,1,0:T(2,128)(2,1)S(1)}, u32[]{:S(2)}, u32[]{:S(2)}) async-start(bf16[64,2,4160]{2,1,0:T(2,128)(2,1)} %reshape.122), calls=%async_computation.1 | async-start | bytes 2162688 | tf_op jit(solution)/shard_map/all_to_all | solution.py:44
  36.4 0.0 reduce-scatter.2.cloned.1.call-start
  36.4 0.0 copy-done
  36.4 2.5 %fusion.19 = f32[192,1024]{1,0:T(8,128)} fusion(bf16[192,1024]{1,0:T(8,128)(2,1)} %bitcast.34, bf16[1024,1024]{1,0:T(8,128)(2,1)S(1)} %copy-done), kind=kOutput, calls=%fused_computation.39 | convolution fusion | flops 402653184 | bytes 3276800 | tf_op jit(solution)/shard_map/dot_general | solution.py:20
  38.9 0.0 reduce-scatter.2.cloned.1.call-update
  39.0 54.0 %all-to-all-done = bf16[64,2,4160]{2,1,0:T(2,128)(2,1)S(1)} async-done(((bf16[64,2,4160]{2,1,0:T(2,128)(2,1)}), bf16[64,2,4160]{2,1,0:T(2,128)(2,1)S(1)}, u32[]{:S(2)}, u32[]{:S(2)}) %all-to-all-start) | async-done | bytes 1064992 | tf_op jit(solution)/shard_map/all_to_all | solution.py:44
  93.0 3.6 %reshape.123 = bf16[64,1,8320]{2,1,0:T(2,128)(2,1)} reshape(bf16[64,2,4160]{2,1,0:T(2,128)(2,1)S(1)} %all-to-all-done) | data formatting | bytes 2129920
  96.5 1.7 %copy.11 = bf16[64,1,8320]{2,0,1:T(8,128)(2,1)S(1)} copy(bf16[64,1,8320]{2,1,0:T(2,128)(2,1)} %reshape.123) | data formatting | bytes 2129920
  98.3 1.1 slice.11
  99.3 0.1 eq.59
  99.4 0.0 copy-start.1
  99.4 1.6 reshape.112
  101.0 0.1 fusion.15
  101.1 1.5 fusion.20
  102.6 0.1 multiply_reduce_fusion
  102.7 24.9 %all-reduce.2 = bf16[512,64]{0,1:T(8,128)(2,1)S(1)} all-reduce(f32[512,64]{0,1:T(8,128)S(1)} %multiply_reduce_fusion), channel_id=1, replica_groups=mesh['ad'=64,'tp'=8] {'tp'}, use_global_device_ids=true, to_apply=%region_4.5 | all-reduce | flops 32768 | bytes 196608 | tf_op jit(solution)/shard_map/psum | solution.py:56
  127.6 0.0 copy-done.1
  127.6 0.9 fusion.2
  128.5 7.3 %all-to-all-start.1 = ((bf16[64,8,128]{2,1,0:T(8,128)(2,1)}), bf16[64,8,128]{2,1,0:T(8,128)(2,1)S(1)}, u32[]{:S(2)}, u32[]{:S(2)}) async-start(bf16[64,8,128]{2,1,0:T(8,128)(2,1)} %fusion.2), calls=%async_computation.2 | async-start | bytes 262144 | tf_op jit(solution)/shard_map/all_to_all | solution.py:66
  135.8 0.0 reduce-scatter.2.cloned.1.call-done
  135.8 15.2 %all-to-all-done.1 = bf16[64,8,128]{2,1,0:T(8,128)(2,1)S(1)} async-done(((bf16[64,8,128]{2,1,0:T(8,128)(2,1)}), bf16[64,8,128]{2,1,0:T(8,128)(2,1)S(1)}, u32[]{:S(2)}, u32[]{:S(2)}) %all-to-all-start.1) | async-done | bytes 131104 | tf_op jit(solution)/shard_map/all_to_all | solution.py:66
  151.0 1.8 %fusion.3 = bf16[192,128]{1,0:T(8,128)(2,1)} fusion(f32[192,128]{1,0:T(8,128)} %reduce-scatter.2.cloned.1.call-done, s32[192]{0:T(256)S(1)} %eq.55, bf16[64,8,128]{2,1,0:T(8,128)(2,1)S(1)} %all-to-all-done.1), kind=kOutput, calls=%fused_computation.7 | convolution fusion | flops 25313280 | bytes 279296 | tf_op jit(solution)/shard_map/dot_general | solution.py:67
  (4 shorter events, 0.0 us)
Async XLA Ops:
  6.5 29.9 %copy-start = (bf16[1024,1024]{1,0:T(8,128)(2,1)S(1)}, bf16[1024,1024]{1,0:T(8,128)(2,1)}, u32[]{:S(2)}) copy-start(bf16[1024,1024]{1,0:T(8,128)(2,1)} %param.7) | copy-start | bytes 6291460
  17.7 75.2 %all-to-all-start = ((bf16[64,2,4160]{2,1,0:T(2,128)(2,1)}), bf16[64,2,4160]{2,1,0:T(2,128)(2,1)S(1)}, u32[]{:S(2)}, u32[]{:S(2)}) async-start(bf16[64,2,4160]{2,1,0:T(2,128)(2,1)} %reshape.122), calls=%async_computation.1 | async-start | bytes 2162688 | tf_op jit(solution)/shard_map/all_to_all | solution.py:44
  36.4 99.4 %reduce-scatter.2.cloned.1.call-start = ((), (), s32[]{:S(2)}) async-start(), calls=%async_computation.3 | async-start | bytes 884736 | tf_op jit(solution)/shard_map/reduce_scatter | solution.py:21
  99.4 28.1 %copy-start.1 = (bf16[4,64,128]{2,1,0:T(8,128)(2,1)S(1)}, bf16[4,64,128]{2,1,0:T(8,128)(2,1)}, u32[]{:S(2)}) copy-start(bf16[4,64,128]{2,1,0:T(8,128)(2,1)} %param.9) | copy-start | bytes 196612
  128.5 22.5 %all-to-all-start.1 = ((bf16[64,8,128]{2,1,0:T(8,128)(2,1)}), bf16[64,8,128]{2,1,0:T(8,128)(2,1)S(1)}, u32[]{:S(2)}, u32[]{:S(2)}) async-start(bf16[64,8,128]{2,1,0:T(8,128)(2,1)} %fusion.2), calls=%async_computation.2 | async-start | bytes 262144 | tf_op jit(solution)/shard_map/all_to_all | solution.py:66
Sparse Core Ops, SparseCore 0:
  40.0 40.9 reduce-scatter.1

commit v5 on v1

--- a/solution.py
+++ b/solution.py
@@ -37,7 +37,13 @@
     tag_values = (local_index + 1).astype(jnp.bfloat16).reshape(row_total, 1)
     tag_block = jnp.broadcast_to(tag_values, (row_total, TAG_WIDTH))
     rows_tagged = jnp.concatenate([gathered_rows, tag_block], axis=1)
-    send_rows = jnp.dot(dispatch, rows_tagged, preferred_element_type=jnp.float32).astype(jnp.bfloat16)
+    row_of_slot = jnp.sum(
+        (slot_index[None, :] == jnp.arange(slot_total, dtype=jnp.int32)[:, None]).astype(jnp.int32)
+        * (jnp.arange(row_total, dtype=jnp.int32)[None, :] - row_total),
+        axis=1,
+    ) + row_total
+    rows_padded = jnp.concatenate([rows_tagged, jnp.zeros((1, rows_tagged.shape[1]), rows_tagged.dtype)])
+    send_rows = jnp.take(rows_padded, row_of_slot, axis=0, mode="clip")
     send_rows = send_rows.reshape(groups, slots_per_group, width_per_shard + TAG_WIDTH)
     incoming = lax.all_to_all(send_rows, "ad", split_axis=0, concat_axis=0, tiled=True)
     incoming = incoming.reshape(slot_total, width_per_shard + TAG_WIDTH)

time: 151 us -> 152 us (level)
  local copies, waits for them, and re-layouts: 1.31 us -> 4.15 us
  matrix products: 8.57 us -> 5.9 us
    gather x0 -> x1, local copies, waits for them, and re-layouts: none -> 2.85 us  [body(): send_rows = jnp.take(rows_padded, row_of_slot, axis=0, mode='clip')]
    dot_general x1 -> x0, matrix products: 2.56 us -> none  [body(): jnp.dot(dispatch, rows_tagged, preferred_element_type=jnp.float32)]
  transfers between devices with their start and end apart: 3 -> 3, of which waited for: 2 -> 2; matrix products, arithmetic and copies ran while one was open for 4% -> 3% of each run, Pallas kernels for 0% -> 0%
where the time goes in v5:
time: 152 us
  waiting for transfers between devices  74.3 us (49%)
  starting transfers between devices  26.6 us (18%)
  blocking collectives  24.9 us (16%)
  between operations  13.5 us (9%)
  matrix products  5.9 us (4%)
  local copies, waits for them, and re-layouts  4.15 us (3%)
  other arithmetic  2.66 us (2%)
    all_to_all x1, waiting for transfers between devices, body(): lax.all_to_all(send_rows, 'ad', split_axis=0, concat_axis=0, tiled=True)  59.1 us
    psum x1, blocking collectives, body(): down_sum = lax.psum(down_part, 'tp')  24.9 us
    all_to_all x1, starting transfers between devices, body(): lax.all_to_all(send_rows, 'ad', split_axis=0, concat_axis=0, tiled=True)  18.9 us
    all_to_all x1, waiting for transfers between devices, body(): lax.all_to_all(adapter_update, 'ad', split_axis=0, concat_axis=0, tiled=T...  15.2 us
    all_to_all x1, starting transfers between devices, body(): lax.all_to_all(adapter_update, 'ad', split_axis=0, concat_axis=0, tiled=T...  7.63 us
  transfers between devices with their start and end apart: 3, of which 2 were waited for; matrix products, arithmetic and copies ran while one was open for 3% of the time, Pallas kernels for 0%

profile of v5, /device:TPU:2, one launch (start us, length us, event | category | flops | bytes accessed | tf_op | source)
XLA Modules:
  0.0 152.0 jit_solution(15213085406163273528)
XLA Ops:
  6.5 0.0 copy-start
  6.5 0.8 fusion.16
  7.4 0.1 fusion.13
  7.5 0.1 reduce_window_sum.11
  7.6 0.2 select_reduce_fusion.1
  7.8 0.1 add_add_fusion
  7.9 0.1 eq.60
  8.0 0.1 select_reduce_fusion
  8.1 0.1 broadcast_in_dim.5
  8.2 0.1 broadcast_in_dim.6
  8.3 1.0 fusion.7
  9.4 2.9 %gather_fusion = bf16[512,1152]{1,0:T(8,128)(2,1)} fusion(bf16[193,1152]{1,0:T(8,128)(2,1)S(1)} %fusion.7, s32[1024]{0:T(1024)S(1)} %pad_clamp_fusion), kind=kCustom, calls=%fused_computation | custom fusion | bytes 2361344 | tf_op jit(solution)/shard_map/jit(_take)/gather | solution.py:46
  12.2 0.0 copy-start.1
  12.2 18.9 %all-to-all-start = ((bf16[64,8,1152]{2,1,0:T(8,128)(2,1)}), bf16[64,8,1152]{2,1,0:T(8,128)(2,1)}, u32[]{:S(2)}, u32[]{:S(2)}) async-start(bf16[64,8,1152]{2,1,0:T(8,128)(2,1)} %bitcast.23), calls=%async_computation.1 | async-start | bytes 2359296 | tf_op jit(solution)/shard_map/all_to_all | solution.py:48
  31.2 0.0 copy-start.2
  31.2 0.0 reduce-scatter.2.cloned.1.call-start
  31.2 0.0 copy-done
  31.2 0.0 copy-done.1
  31.2 1.5 fusion.18
  32.7 0.0 reduce-scatter.2.cloned.1.call-update
  32.8 59.1 %all-to-all-done = bf16[64,8,1152]{2,1,0:T(8,128)(2,1)} async-done(((bf16[64,8,1152]{2,1,0:T(8,128)(2,1)}), bf16[64,8,1152]{2,1,0:T(8,128)(2,1)}, u32[]{:S(2)}, u32[]{:S(2)}) %all-to-all-start) | async-done | bytes 1179680 | tf_op jit(solution)/shard_map/all_to_all | solution.py:48
  91.9 1.0 slice_reduce_fusion
  92.9 0.1 fusion.14
  93.0 0.0 copy-done.2
  93.0 0.0 copy-start.3
  93.0 1.7 %fusion.3 = f32[512,256]{0,1:S(1)} fusion(bf16[1024,256]{0,1:T(8,128)(2,1)S(1)} %bitcast.27, bf16[512,1152]{1,0:T(8,128)(2,1)} %bitcast.2), kind=kOutput, calls=%fused_computation.6 | convolution fusion | flops 268435456 | bytes 2097152
  94.7 0.1 multiply_reduce_fusion
  94.8 24.9 %all-reduce.2 = bf16[512,64]{0,1:T(8,128)(2,1)S(1)} all-reduce(f32[512,64]{0,1:T(8,128)S(1)} %multiply_reduce_fusion), channel_id=1, replica_groups=mesh['ad'=64,'tp'=8] {'tp'}, use_global_device_ids=true, to_apply=%region_5.6 | all-reduce | flops 32768 | bytes 196608 | tf_op jit(solution)/shard_map/psum | solution.py:59
  119.7 0.0 copy-done.3
  119.7 0.9 fusion.1
  120.6 7.6 %all-to-all-start.1 = ((bf16[64,8,128]{2,1,0:T(8,128)(2,1)}), bf16[64,8,128]{2,1,0:T(8,128)(2,1)S(1)}, u32[]{:S(2)}, u32[]{:S(2)}) async-start(bf16[64,8,128]{2,1,0:T(8,128)(2,1)} %fusion.1), calls=%async_computation.2 | async-start | bytes 262144 | tf_op jit(solution)/shard_map/all_to_all | solution.py:69
  128.2 0.0 reduce-scatter.2.cloned.1.call-done
  128.3 15.2 %all-to-all-done.1 = bf16[64,8,128]{2,1,0:T(8,128)(2,1)S(1)} async-done(((bf16[64,8,128]{2,1,0:T(8,128)(2,1)}), bf16[64,8,128]{2,1,0:T(8,128)(2,1)S(1)}, u32[]{:S(2)}, u32[]{:S(2)}) %all-to-all-start.1) | async-done | bytes 131104 | tf_op jit(solution)/shard_map/all_to_all | solution.py:69
  143.4 1.8 %fusion.2 = bf16[192,128]{1,0:T(8,128)(2,1)} fusion(f32[192,128]{1,0:T(8,128)} %reduce-scatter.2.cloned.1.call-done, s32[192]{0:T(256)S(1)} %eq.60, bf16[64,8,128]{2,1,0:T(8,128)(2,1)S(1)} %all-to-all-done.1), kind=kOutput, calls=%fused_computation.5 | convolution fusion | flops 25313280 | bytes 279296 | tf_op jit(solution)/shard_map/dot_general | solution.py:70
  (5 shorter events, 0.0 us)
Async XLA Ops:
  6.5 24.7 %copy-start = (bf16[1024,1024]{1,0:T(8,128)(2,1)S(1)}, bf16[1024,1024]{1,0:T(8,128)(2,1)}, u32[]{:S(2)}) copy-start(bf16[1024,1024]{1,0:T(8,128)(2,1)} %param.7) | copy-start | bytes 6291460
  12.2 19.0 %copy-start.1 = (bf16[4,48,1024]{2,1,0:T(8,128)(2,1)S(1)}, bf16[4,48,1024]{2,1,0:T(8,128)(2,1)}, u32[]{:S(2)}) copy-start(bf16[4,48,1024]{2,1,0:T(8,128)(2,1)} %param.5) | copy-start | bytes 1179652
  12.2 79.7 %all-to-all-start = ((bf16[64,8,1152]{2,1,0:T(8,128)(2,1)}), bf16[64,8,1152]{2,1,0:T(8,128)(2,1)}, u32[]{:S(2)}, u32[]{:S(2)}) async-start(bf16[64,8,1152]{2,1,0:T(8,128)(2,1)} %bitcast.23), calls=%async_computation.1 | async-start | bytes 2359296 | tf_op jit(solution)/shard_map/all_to_all | solution.py:48
  31.2 61.8 %copy-start.2 = (bf16[4,1024,64]{1,2,0:T(8,128)(2,1)S(1)}, bf16[4,1024,64]{1,2,0:T(8,128)(2,1)}, u32[]{:S(2)}) copy-start(bf16[4,1024,64]{1,2,0:T(8,128)(2,1)} %param.8) | copy-start | bytes 1572868
  31.2 97.1 %reduce-scatter.2.cloned.1.call-start = ((), (), s32[]{:S(2)}) async-start(), calls=%async_computation.3 | async-start | bytes 884736 | tf_op jit(solution)/shard_map/reduce_scatter | solution.py:21
  93.0 26.7 %copy-start.3 = (bf16[4,64,128]{2,1,0:T(8,128)(2,1)S(1)}, bf16[4,64,128]{2,1,0:T(8,128)(2,1)}, u32[]{:S(2)}) copy-start(bf16[4,64,128]{2,1,0:T(8,128)(2,1)} %param.9) | copy-start | bytes 196612
  120.6 22.8 %all-to-all-start.1 = ((bf16[64,8,128]{2,1,0:T(8,128)(2,1)}), bf16[64,8,128]{2,1,0:T(8,128)(2,1)S(1)}, u32[]{:S(2)}, u32[]{:S(2)}) async-start(bf16[64,8,128]{2,1,0:T(8,128)(2,1)} %fusion.1), calls=%async_computation.2 | async-start | bytes 262144 | tf_op jit(solution)/shard_map/all_to_all | solution.py:69
Sparse Core Ops, SparseCore 0:
  34.8 41.2 reduce-scatter.1

commit v6 on v1

--- a/solution.py
+++ b/solution.py
@@ -50,7 +50,13 @@
     labels = (jnp.arange(adapter_number, dtype=jnp.int32) + 1).astype(jnp.bfloat16)
     selector = (incoming_labels[:, None] == labels[None, :]).astype(jnp.float32)
     down_part = jnp.sum(down_all * selector[:, :, None], axis=1)
-    down_sum = lax.psum(down_part, "tp")
+    shards = lax.axis_size("tp")
+    chunks = down_part.reshape(shards, slot_total // shards, rank)
+    chunk_sum = jnp.sum(lax.all_to_all(chunks, "tp", split_axis=0, concat_axis=0, tiled=True), axis=0)
+    spread = jnp.broadcast_to(chunk_sum[None], (shards,) + chunk_sum.shape)
+    down_sum = lax.all_to_all(spread, "tp", split_axis=0, concat_axis=0, tiled=True).reshape(
+        slot_total, rank
+    )
     down_low = down_sum.astype(jnp.bfloat16)
     spread_rows = (selector.astype(jnp.bfloat16)[:, :, None] * down_low[:, None, :]).reshape(
         slot_total, adapter_number * rank

time: 151 us -> 147 us (0.974)
  blocking collectives: 24.9 us -> 18.5 us
  starting transfers between devices: 26.6 us -> 24.9 us
    psum x1 -> x0, blocking collectives: 24.9 us -> none  [body(): down_sum = lax.psum(down_part, 'tp')]
    all_to_all x0 -> x2, blocking collectives: none -> 18.5 us  [the longest x1 10.5 us: body(): lax.all_to_all(chunks, 'tp', split_axis=0, concat_axis=0, tiled=True)]
    all_to_all x1, starting transfers between devices: 7.63 us -> 5.94 us  [body(): lax.all_to_all(adapter_update, 'ad', split_axis=0, concat_axis=0, tiled=T...]
  transfers between devices with their start and end apart: 3 -> 3, of which waited for: 2 -> 2; matrix products, arithmetic and copies ran while one was open for 4% -> 5% of each run, Pallas kernels for 0% -> 0%
where the time goes in v6:
time: 147 us; the launch traced here: 146 us
  waiting for transfers between devices  75.6 us (51%)
  starting transfers between devices  24.9 us (17%)
  blocking collectives  18.5 us (13%)
  between operations  13.6 us (9%)
  matrix products  8.5 us (6%)
  local copies, waits for them, and re-layouts  2.81 us (2%)
  other arithmetic  2.44 us (2%)
    all_to_all x1, waiting for transfers between devices, body(): lax.all_to_all(send_rows, 'ad', split_axis=0, concat_axis=0, tiled=True)  59.1 us
    all_to_all x1, starting transfers between devices, body(): lax.all_to_all(send_rows, 'ad', split_axis=0, concat_axis=0, tiled=True)  18.9 us
    all_to_all x1, waiting for transfers between devices, body(): lax.all_to_all(adapter_update, 'ad', split_axis=0, concat_axis=0, tiled=T...  16.5 us
    all_to_all x1, blocking collectives, body(): lax.all_to_all(chunks, 'tp', split_axis=0, concat_axis=0, tiled=True)  10.5 us
    all_to_all x1, blocking collectives, body(): lax.all_to_all(spread, 'tp', split_axis=0, concat_axis=0, tiled=True)  8 us
    all_to_all x1, starting transfers between devices, body(): lax.all_to_all(adapter_update, 'ad', split_axis=0, concat_axis=0, tiled=T...  5.94 us
  transfers between devices with their start and end apart: 3, of which 2 were waited for; matrix products, arithmetic and copies ran while one was open for 5% of the time, Pallas kernels for 0%

profile of v6, /device:TPU:2, one launch (start us, length us, event | category | flops | bytes accessed | tf_op | source)
XLA Modules:
  0.0 146.4 jit_solution(7992108253649706490)
XLA Ops:
  6.5 0.0 copy-start
  6.5 0.8 fusion.18
  7.4 0.1 fusion.15
  7.5 0.1 reduce_window_sum.11
  7.6 0.2 select_reduce_fusion
  7.8 0.1 add_add_fusion
  7.9 0.1 eq.53
  8.0 0.1 broadcast_in_dim.6
  8.1 0.1 broadcast_in_dim.7
  8.2 2.6 %fusion = bf16[64,8,1152]{2,1,0:T(8,128)(2,1)} fusion(bf16[192,128]{1,0:T(8,128)(2,1)S(1)} %broadcast_in_dim.7, bf16[192,1024]{1,0:T(8,128)(2,1)} %bitcast.36, s32[192]{0:T(256)S(1)} %eq.53), kind=kOutput, calls=%fused_computation.1 | convolution fusion | flops 228065280 | bytes 1622784 | tf_op jit(solution)/shard_map/dot_general | solution.py:40
  10.7 0.0 copy-start.1
  10.7 18.9 %all-to-all-start = ((bf16[64,8,1152]{2,1,0:T(8,128)(2,1)}), bf16[64,8,1152]{2,1,0:T(8,128)(2,1)}, u32[]{:S(2)}, u32[]{:S(2)}) async-start(bf16[64,8,1152]{2,1,0:T(8,128)(2,1)} %fusion), calls=%async_computation.1 | async-start | bytes 2359296 | tf_op jit(solution)/shard_map/all_to_all | solution.py:42
  29.7 0.0 copy-start.2
  29.7 0.0 reduce-scatter.2.cloned.1.call-start
  29.7 0.0 copy-done
  29.7 0.0 copy-done.1
  29.7 1.5 %fusion.21 = f32[192,1024]{1,0:T(8,128)} fusion(bf16[192,1024]{1,0:T(8,128)(2,1)S(1)} %bitcast.37, bf16[1024,1024]{1,0:T(8,128)(2,1)S(1)} %copy-done), kind=kOutput, calls=%fused_computation.43 | convolution fusion | flops 402653184 | bytes 3276800 | tf_op jit(solution)/shard_map/dot_general | solution.py:20
  31.2 0.0 reduce-scatter.2.cloned.1.call-update
  31.3 59.1 %all-to-all-done = bf16[64,8,1152]{2,1,0:T(8,128)(2,1)} async-done(((bf16[64,8,1152]{2,1,0:T(8,128)(2,1)}), bf16[64,8,1152]{2,1,0:T(8,128)(2,1)}, u32[]{:S(2)}, u32[]{:S(2)}) %all-to-all-start) | async-done | bytes 1179680 | tf_op jit(solution)/shard_map/all_to_all | solution.py:42
  90.4 1.0 slice_reduce_fusion
  91.4 0.1 fusion.16
  91.5 0.0 copy-done.2
  91.5 1.7 %fusion.4 = f32[512,256]{0,1:S(1)} fusion(bf16[1024,256]{0,1:T(8,128)(2,1)S(1)} %bitcast.41, bf16[512,1152]{1,0:T(8,128)(2,1)} %bitcast.2), kind=kOutput, calls=%fused_computation.7 | convolution fusion | flops 268435456 | bytes 2097152
  93.2 0.1 multiply_reduce_fusion
  93.3 0.1 reshape.107
  93.4 0.1 copy.10
  93.4 0.2 reshape.115
  93.6 0.0 copy-start.3
  93.6 10.5 %all_to_all.20 = f32[8,1,4096]{2,1,0:T(1,128)S(1)} all-to-all(f32[8,1,4096]{2,1,0:T(1,128)S(1)} %reshape.115), channel_id=1, replica_groups=mesh['ad'=64,'tp'=8] {'tp'}, dimensions={0} | all-to-all | bytes 262144 | tf_op jit(solution)/shard_map/all_to_all | solution.py:55
  104.1 0.5 broadcast.91
  104.6 1.0 reduce.2
  105.6 0.1 reshape.116
  105.8 0.2 reshape.117
  105.9 8.0 %all_to_all.21 = bf16[8,2,2048]{2,1,0:T(2,128)(2,1)S(1)} all-to-all(bf16[8,2,2048]{2,1,0:T(2,128)(2,1)S(1)} %reshape.117), channel_id=1, replica_groups=mesh['ad'=64,'tp'=8] {'tp'}, dimensions={0} | all-to-all | bytes 131072 | tf_op jit(solution)/shard_map/all_to_all | solution.py:57
  113.9 0.1 reshape.118
  114.1 0.1 copy.8
  114.2 0.1 convert_element_type.57
  114.3 0.0 copy-done.3
  114.3 0.9 fusion.2
  115.2 5.9 %all-to-all-start.3 = ((bf16[64,8,128]{2,1,0:T(8,128)(2,1)}), bf16[64,8,128]{2,1,0:T(8,128)(2,1)S(1)}, u32[]{:S(2)}, u32[]{:S(2)}) async-start(bf16[64,8,128]{2,1,0:T(8,128)(2,1)} %fusion.2), calls=%async_computation.4 | async-start | bytes 262144 | tf_op jit(solution)/shard_map/all_to_all | solution.py:69
  121.2 0.0 reduce-scatter.2.cloned.1.call-done
  121.2 16.5 %all-to-all-done.3 = bf16[64,8,128]{2,1,0:T(8,128)(2,1)S(1)} async-done(((bf16[64,8,128]{2,1,0:T(8,128)(2,1)}), bf16[64,8,128]{2,1,0:T(8,128)(2,1)S(1)}, u32[]{:S(2)}, u32[]{:S(2)}) %all-to-all-start.3) | async-done | bytes 131104 | tf_op jit(solution)/shard_map/all_to_all | solution.py:69
  137.7 1.8 %fusion.3 = bf16[192,128]{1,0:T(8,128)(2,1)} fusion(f32[192,128]{1,0:T(8,128)} %reduce-scatter.2.cloned.1.call-done, s32[192]{0:T(256)S(1)} %eq.53, bf16[64,8,128]{2,1,0:T(8,128)(2,1)S(1)} %all-to-all-done.3), kind=kOutput, calls=%fused_computation.6 | convolution fusion | flops 25313280 | bytes 279296 | tf_op jit(solution)/shard_map/dot_general | solution.py:70
  (4 shorter events, 0.1 us)
Async XLA Ops:
  6.5 23.2 %copy-start = (bf16[1024,1024]{1,0:T(8,128)(2,1)S(1)}, bf16[1024,1024]{1,0:T(8,128)(2,1)}, u32[]{:S(2)}) copy-start(bf16[1024,1024]{1,0:T(8,128)(2,1)} %param.7) | copy-start | bytes 6291460
  10.7 19.0 %copy-start.1 = (bf16[4,48,1024]{2,1,0:T(8,128)(2,1)S(1)}, bf16[4,48,1024]{2,1,0:T(8,128)(2,1)}, u32[]{:S(2)}) copy-start(bf16[4,48,1024]{2,1,0:T(8,128)(2,1)} %param.5) | copy-start | bytes 1179652
  10.7 79.7 %all-to-all-start = ((bf16[64,8,1152]{2,1,0:T(8,128)(2,1)}), bf16[64,8,1152]{2,1,0:T(8,128)(2,1)}, u32[]{:S(2)}, u32[]{:S(2)}) async-start(bf16[64,8,1152]{2,1,0:T(8,128)(2,1)} %fusion), calls=%async_computation.1 | async-start | bytes 2359296 | tf_op jit(solution)/shard_map/all_to_all | solution.py:42
  29.7 61.8 %copy-start.2 = (bf16[4,1024,64]{1,2,0:T(8,128)(2,1)S(1)}, bf16[4,1024,64]{1,2,0:T(8,128)(2,1)}, u32[]{:S(2)}) copy-start(bf16[4,1024,64]{1,2,0:T(8,128)(2,1)} %param.8) | copy-start | bytes 1572868
  29.7 91.5 %reduce-scatter.2.cloned.1.call-start = ((), (), s32[]{:S(2)}) async-start(), calls=%async_computation.5 | async-start | bytes 884736 | tf_op jit(solution)/shard_map/reduce_scatter | solution.py:21
  93.6 20.7 %copy-start.3 = (bf16[4,64,128]{2,1,0:T(8,128)(2,1)S(1)}, bf16[4,64,128]{2,1,0:T(8,128)(2,1)}, u32[]{:S(2)}) copy-start(bf16[4,64,128]{2,1,0:T(8,128)(2,1)} %param.9) | copy-start | bytes 196612
  115.2 22.5 %all-to-all-start.3 = ((bf16[64,8,128]{2,1,0:T(8,128)(2,1)}), bf16[64,8,128]{2,1,0:T(8,128)(2,1)S(1)}, u32[]{:S(2)}, u32[]{:S(2)}) async-start(bf16[64,8,128]{2,1,0:T(8,128)(2,1)} %fusion.2), calls=%async_computation.4 | async-start | bytes 262144 | tf_op jit(solution)/shard_map/all_to_all | solution.py:69
Sparse Core Ops, SparseCore 0:
  33.3 41.2 reduce-scatter.1

commit v7 on v6

--- a/solution.py
+++ b/solution.py
@@ -18,8 +18,12 @@
 
     gathered_rows = tokens.reshape(row_total, width_per_shard)
     partial_base = jnp.dot(gathered_rows, key_base_weight, preferred_element_type=jnp.float32)
-    base_keys_output = lax.psum_scatter(partial_base, "tp", scatter_dimension=1, tiled=True)
-    key_feature_width = base_keys_output.shape[1]
+    tp_size = lax.axis_size("tp")
+    key_feature_width = partial_base.shape[1] // tp_size
+    base_pieces = partial_base.reshape(row_total, tp_size, key_feature_width).transpose(1, 0, 2)
+    base_keys_output = jnp.sum(
+        lax.all_to_all(base_pieces, "tp", split_axis=0, concat_axis=0, tiled=True), axis=0
+    )
 
     index_list = row_adapter_index.reshape(step_count, row_dev)
     owner_group = index_list // adapter_number
@@ -40,6 +44,7 @@
     send_rows = jnp.dot(dispatch, rows_tagged, preferred_element_type=jnp.float32).astype(jnp.bfloat16)
     send_rows = send_rows.reshape(groups, slots_per_group, width_per_shard + TAG_WIDTH)
     incoming = lax.all_to_all(send_rows, "ad", split_axis=0, concat_axis=0, tiled=True)
+    incoming, base_keys_output = lax.optimization_barrier((incoming, base_keys_output))
     incoming = incoming.reshape(slot_total, width_per_shard + TAG_WIDTH)
     incoming_rows = incoming[:, :width_per_shard]
     incoming_labels = incoming[:, width_per_shard]

time: 147 us -> 145 us (0.986)
  blocking collectives: 18.5 us -> 38.7 us
  between operations: 13.6 us -> 0.16 us
  waiting for transfers between devices: 75.6 us -> 71.2 us
  matrix products: 8.5 us -> 4.98 us
  local copies, waits for them, and re-layouts: 2.81 us -> 4.84 us
  starting transfers between devices: 24.9 us -> 23.1 us
    all_to_all x0 -> x1, blocking collectives: none -> 22.3 us  [body(): lax.all_to_all(adapter_update, 'ad', split_axis=0, concat_axis=0, tiled=T...]
    all_to_all x1, waiting for transfers between devices: 16.5 us -> 10.8 us  [body(): lax.all_to_all(base_pieces, 'tp', split_axis=0, concat_axis=0, tiled=True)]
    dot_general x0 -> x1, local copies, waits for them, and re-layouts: none -> 2.94 us  [body(): jnp.dot(gathered_rows, key_base_weight, preferred_element_type=jnp.float32)]
    all_to_all x1, blocking collectives: 10.5 us -> 8.49 us  [body(): lax.all_to_all(chunks, 'tp', split_axis=0, concat_axis=0, tiled=True)]
    all_to_all x1, starting transfers between devices: 5.94 us -> 4.47 us  [body(): lax.all_to_all(base_pieces, 'tp', split_axis=0, concat_axis=0, tiled=True)]
  transfers between devices with their start and end apart: 3 -> 2, of which waited for: 2 -> 2; matrix products, arithmetic and copies ran while one was open for 5% -> 2% of each run, Pallas kernels for 0% -> 0%
where the time goes in v7:
time: 145 us
  waiting for transfers between devices  71.2 us (49%)
  blocking collectives  38.7 us (27%)
  starting transfers between devices  23.1 us (16%)
  matrix products  4.98 us (3%)
  local copies, waits for them, and re-layouts  4.84 us (3%)
  other arithmetic  1.66 us (1%)
    all_to_all x1, waiting for transfers between devices, body(): lax.all_to_all(send_rows, 'ad', split_axis=0, concat_axis=0, tiled=True)  60.4 us
    all_to_all x1, blocking collectives, body(): lax.all_to_all(adapter_update, 'ad', split_axis=0, concat_axis=0, tiled=T...  22.3 us
    all_to_all x1, starting transfers between devices, body(): lax.all_to_all(send_rows, 'ad', split_axis=0, concat_axis=0, tiled=True)  18.6 us
    all_to_all x1, waiting for transfers between devices, body(): lax.all_to_all(base_pieces, 'tp', split_axis=0, concat_axis=0, tiled=True)  10.8 us
    all_to_all x1, blocking collectives, body(): lax.all_to_all(chunks, 'tp', split_axis=0, concat_axis=0, tiled=True)  8.49 us
    all_to_all x1, blocking collectives, body(): lax.all_to_all(spread, 'tp', split_axis=0, concat_axis=0, tiled=True)  8 us
    all_to_all x1, starting transfers between devices, body(): lax.all_to_all(base_pieces, 'tp', split_axis=0, concat_axis=0, tiled=True)  4.47 us
    dot_general x1, local copies, waits for them, and re-layouts, body(): jnp.dot(gathered_rows, key_base_weight, preferred_element_type=jnp.float32)  2.94 us
  transfers between devices with their start and end apart: 2, of which 2 were waited for; matrix products, arithmetic and copies ran while one was open for 2% of the time, Pallas kernels for 0%

profile of v7, /device:TPU:2, one launch (start us, length us, event | category | flops | bytes accessed | tf_op | source)
XLA Modules:
  0.0 144.7 jit_solution(146803213331804687)
XLA Ops:
  0.0 0.0 copy-start
  0.0 0.0 copy-start.1
  0.0 2.9 %copy.14 = bf16[1024,1024]{1,0:T(8,128)(2,1)S(1)} copy(bf16[1024,1024]{0,1:T(8,128)(2,1)} %bitcast.44) | data formatting | bytes 4194304 | tf_op jit(solution)/shard_map/dot_general | solution.py:20
  3.0 0.0 copy-done.1
  3.0 0.0 copy-start.2
  3.0 1.8 %convolution_bitcast_fusion = f32[8,192,128]{2,1,0:T(8,128)} fusion(bf16[192,1024,1]{1,0,2:T(8,128)(2,1)S(1)} %bitcast.45, bf16[8,128,1024]{2,1,0:T(8,128)(2,1)S(1)} %bitcast.43), kind=kOutput, calls=%fused_computation.2 | convolution fusion | flops 402653184 | bytes 3276800 | tf_op jit(solution)/shard_map/dot_general | solution.py:20
  4.7 4.5 %all-to-all-start.1 = ((f32[8,192,128]{2,1,0:T(8,128)}), f32[8,192,128]{2,1,0:T(8,128)S(1)}, u32[]{:S(2)}, u32[]{:S(2)}) async-start(f32[8,192,128]{2,1,0:T(8,128)} %convolution_bitcast_fusion), calls=%async_computation.1 | async-start | bytes 1572864 | tf_op jit(solution)/shard_map/all_to_all | solution.py:25
  9.2 0.0 copy-done.2
  9.2 0.1 fusion.15
  9.3 0.1 reduce_window_sum.11
  9.5 0.2 select_reduce_fusion
  9.7 0.1 add_add_fusion
  9.7 0.1 eq.53
  9.8 0.1 broadcast_in_dim.6
  9.9 0.1 broadcast_in_dim.7
  10.0 1.5 %fusion = bf16[64,8,1152]{2,1,0:T(8,128)(2,1)} fusion(bf16[192,128]{1,0:T(8,128)(2,1)S(1)} %broadcast_in_dim.7, bf16[192,1024]{1,0:T(8,128)(2,1)S(1)} %bitcast.46, s32[192]{0:T(256)S(1)} %eq.53), kind=kOutput, calls=%fused_computation.1 | convolution fusion | flops 228065280 | bytes 1622784 | tf_op jit(solution)/shard_map/dot_general | solution.py:44
  11.5 10.8 %all-to-all-done.1 = f32[8,192,128]{2,1,0:T(8,128)S(1)} async-done(((f32[8,192,128]{2,1,0:T(8,128)}), f32[8,192,128]{2,1,0:T(8,128)S(1)}, u32[]{:S(2)}, u32[]{:S(2)}) %all-to-all-start.1) | async-done | bytes 786464 | tf_op jit(solution)/shard_map/all_to_all | solution.py:25
  22.3 18.6 %all-to-all-start = ((bf16[64,8,1152]{2,1,0:T(8,128)(2,1)}), bf16[64,8,1152]{2,1,0:T(8,128)(2,1)S(1)}, u32[]{:S(2)}, u32[]{:S(2)}) async-start(bf16[64,8,1152]{2,1,0:T(8,128)(2,1)} %fusion), calls=%async_computation | async-start | bytes 2359296 | tf_op jit(solution)/shard_map/all_to_all | solution.py:46
  41.0 60.4 %all-to-all-done = bf16[64,8,1152]{2,1,0:T(8,128)(2,1)S(1)} async-done(((bf16[64,8,1152]{2,1,0:T(8,128)(2,1)}), bf16[64,8,1152]{2,1,0:T(8,128)(2,1)S(1)}, u32[]{:S(2)}, u32[]{:S(2)}) %all-to-all-start) | async-done | bytes 1179680 | tf_op jit(solution)/shard_map/all_to_all | solution.py:46
  101.5 0.1 slice_reduce_fusion
  101.6 0.0 copy-done
  101.6 0.5 fusion.4
  102.1 0.1 fusion.16
  102.2 0.0 copy-start.3
  102.2 0.1 multiply_reduce_fusion
  102.2 0.1 reshape.109
  102.3 0.1 copy.16
  102.4 0.2 reshape.118
  102.6 8.5 %all_to_all.25 = f32[8,1,4096]{2,1,0:T(1,128)S(1)} all-to-all(f32[8,1,4096]{2,1,0:T(1,128)S(1)} %reshape.118), channel_id=1, replica_groups=mesh['ad'=64,'tp'=8] {'tp'}, dimensions={0} | all-to-all | bytes 262144 | tf_op jit(solution)/shard_map/all_to_all | solution.py:60
  111.0 0.5 broadcast.91
  111.6 1.0 reduce.2
  112.5 0.1 reshape.119
  112.7 0.2 reshape.120
  112.8 8.0 %all_to_all.26 = bf16[8,2,2048]{2,1,0:T(2,128)(2,1)S(1)} all-to-all(bf16[8,2,2048]{2,1,0:T(2,128)(2,1)S(1)} %reshape.120), channel_id=1, replica_groups=mesh['ad'=64,'tp'=8] {'tp'}, dimensions={0} | all-to-all | bytes 131072 | tf_op jit(solution)/shard_map/all_to_all | solution.py:62
  120.8 0.1 reshape.121
  121.0 0.1 copy.13
  121.1 0.1 convert_element_type.57
  121.2 0.0 copy-done.3
  121.2 0.3 fusion.2
  121.5 22.3 %all_to_all.27 = bf16[64,8,128]{2,1,0:T(8,128)(2,1)S(1)} all-to-all(bf16[64,8,128]{2,1,0:T(8,128)(2,1)S(1)} %fusion.2), channel_id=1, replica_groups=mesh['ad'=64,'tp'=8] {'ad'}, dimensions={0} | all-to-all | bytes 262144 | tf_op jit(solution)/shard_map/all_to_all | solution.py:74
  143.8 0.9 fusion.3
  (6 shorter events, 0.1 us)
Async XLA Ops:
  0.0 101.6 %copy-start = (bf16[4,1024,64]{1,2,0:T(8,128)(2,1)S(1)}, bf16[4,1024,64]{1,2,0:T(8,128)(2,1)}, u32[]{:S(2)}) copy-start(bf16[4,1024,64]{1,2,0:T(8,128)(2,1)} %param.8) | copy-start | bytes 1572868
  0.0 3.0 %copy-start.1 = (bf16[4,48,1024]{2,1,0:T(8,128)(2,1)S(1)}, bf16[4,48,1024]{2,1,0:T(8,128)(2,1)}, u32[]{:S(2)}) copy-start(bf16[4,48,1024]{2,1,0:T(8,128)(2,1)} %param.5) | copy-start | bytes 1179652
  3.0 6.3 %copy-start.2 = (s32[4,48]{1,0:T(4,128)S(1)}, s32[4,48]{1,0:T(4,128)}, u32[]{:S(2)}) copy-start(s32[4,48]{1,0:T(4,128)} %param.6) | copy-start | bytes 2308
  4.7 17.6 %all-to-all-start.1 = ((f32[8,192,128]{2,1,0:T(8,128)}), f32[8,192,128]{2,1,0:T(8,128)S(1)}, u32[]{:S(2)}, u32[]{:S(2)}) async-start(f32[8,192,128]{2,1,0:T(8,128)} %convolution_bitcast_fusion), calls=%async_computation.1 | async-start | bytes 1572864 | tf_op jit(solution)/shard_map/all_to_all | solution.py:25
  22.3 79.1 %all-to-all-start = ((bf16[64,8,1152]{2,1,0:T(8,128)(2,1)}), bf16[64,8,1152]{2,1,0:T(8,128)(2,1)S(1)}, u32[]{:S(2)}, u32[]{:S(2)}) async-start(bf16[64,8,1152]{2,1,0:T(8,128)(2,1)} %fusion), calls=%async_computation | async-start | bytes 2359296 | tf_op jit(solution)/shard_map/all_to_all | solution.py:46
  102.2 19.1 %copy-start.3 = (bf16[4,64,128]{2,1,0:T(8,128)(2,1)S(1)}, bf16[4,64,128]{2,1,0:T(8,128)(2,1)}, u32[]{:S(2)}) copy-start(bf16[4,64,128]{2,1,0:T(8,128)(2,1)} %param.9) | copy-start | bytes 196612

commit v8 on v7

--- a/solution.py
+++ b/solution.py
@@ -17,10 +17,14 @@
     slot_total = groups * slots_per_group
 
     gathered_rows = tokens.reshape(row_total, width_per_shard)
-    partial_base = jnp.dot(gathered_rows, key_base_weight, preferred_element_type=jnp.float32)
     tp_size = lax.axis_size("tp")
-    key_feature_width = partial_base.shape[1] // tp_size
-    base_pieces = partial_base.reshape(row_total, tp_size, key_feature_width).transpose(1, 0, 2)
+    key_feature_width = key_base_weight.shape[1] // tp_size
+    base_pieces = jnp.einsum(
+        "nd,dkf->knf",
+        gathered_rows,
+        key_base_weight.reshape(width_per_shard, tp_size, key_feature_width),
+        preferred_element_type=jnp.float32,
+    )
     base_keys_output = jnp.sum(
         lax.all_to_all(base_pieces, "tp", split_axis=0, concat_axis=0, tiled=True), axis=0
     )

time: 145 us -> 147 us (1.014)
  matrix products: 4.98 us -> 7.01 us
    dot_general x1 -> x0, local copies, waits for them, and re-layouts: 2.94 us -> none  [body(): jnp.dot(gathered_rows, key_base_weight, preferred_element_type=jnp.float32)]
    unnamed x13 -> x15, local copies, waits for them, and re-layouts: 0.62 us -> 2.21 us
where the time goes in v8:
time: 147 us; the launch traced here: 146 us
  waiting for transfers between devices  71.2 us (48%)
  blocking collectives  38.7 us (26%)
  starting transfers between devices  23.3 us (16%)
  matrix products  7.01 us (5%)
  local copies, waits for them, and re-layouts  4.39 us (3%)
  other arithmetic  1.66 us (1%)
    all_to_all x1, waiting for transfers between devices, body(): lax.all_to_all(send_rows, 'ad', split_axis=0, concat_axis=0, tiled=True)  60.4 us
    all_to_all x1, blocking collectives, body(): lax.all_to_all(adapter_update, 'ad', split_axis=0, concat_axis=0, tiled=T...  22.3 us
    all_to_all x1, starting transfers between devices, body(): lax.all_to_all(send_rows, 'ad', split_axis=0, concat_axis=0, tiled=True)  18.8 us
    all_to_all x1, waiting for transfers between devices, body(): lax.all_to_all(base_pieces, 'tp', split_axis=0, concat_axis=0, tiled=True)  10.8 us
    all_to_all x1, blocking collectives, body(): lax.all_to_all(chunks, 'tp', split_axis=0, concat_axis=0, tiled=True)  8.49 us
    all_to_all x1, blocking collectives, body(): lax.all_to_all(spread, 'tp', split_axis=0, concat_axis=0, tiled=True)  8 us
    all_to_all x1, starting transfers between devices, body(): lax.all_to_all(base_pieces, 'tp', split_axis=0, concat_axis=0, tiled=True)  4.47 us
  transfers between devices with their start and end apart: 2, of which 2 were waited for; matrix products, arithmetic and copies ran while one was open for 2% of the time, Pallas kernels for 0%

profile of v8, /device:TPU:2, one launch (start us, length us, event | category | flops | bytes accessed | tf_op | source)
XLA Modules:
  0.0 146.4 jit_solution(3018707064114537416)
XLA Ops:
  0.0 0.0 copy-start
  0.0 1.6 %copy-done = bf16[1024,1024]{1,0:T(8,128)(2,1)S(1)} copy-done((bf16[1024,1024]{1,0:T(8,128)(2,1)S(1)}, bf16[1024,1024]{1,0:T(8,128)(2,1)}, u32[]{:S(2)}) %copy-start) | copy-done | bytes 2097176
  1.6 0.0 copy-start.2
  1.6 0.0 copy-start.1
  1.6 2.6 %fusion.4 = f32[8,192,128]{2,1,0:T(8,128)} fusion(bf16[192,1024,1]{1,0,2:T(8,128)(2,1)} %bitcast.51, bf16[1024,1024]{1,0:T(8,128)(2,1)S(1)} %copy-done), kind=kOutput, calls=%fused_computation.5 | convolution fusion | flops 402653184 | bytes 3276800 | tf_op jit(solution)/shard_map/nd,dkf->knf/dot_general | solution.py:22
  4.2 4.5 %all-to-all-start.1 = ((f32[8,192,128]{2,1,0:T(8,128)}), f32[8,192,128]{2,1,0:T(8,128)S(1)}, u32[]{:S(2)}, u32[]{:S(2)}) async-start(f32[8,192,128]{2,1,0:T(8,128)} %fusion.4), calls=%async_computation.1 | async-start | bytes 1572864 | tf_op jit(solution)/shard_map/all_to_all | solution.py:29
  8.6 0.0 copy-done.2
  8.7 0.1 fusion.21
  8.8 0.1 broadcast_in_dim.6
  8.8 0.1 reduce_window_sum.11
  9.0 0.2 select_reduce_fusion
  9.2 0.1 add_add_fusion
  9.3 0.1 eq.53
  9.3 0.1 broadcast_in_dim.7
  9.4 0.0 copy-done.1
  9.5 1.5 %fusion = bf16[64,8,1152]{2,1,0:T(8,128)(2,1)} fusion(bf16[192,128]{1,0:T(8,128)(2,1)S(1)} %broadcast_in_dim.7, bf16[192,1024]{1,0:T(8,128)(2,1)S(1)} %bitcast.52, s32[192]{0:T(256)S(1)} %eq.53), kind=kOutput, calls=%fused_computation.1 | convolution fusion | flops 228065280 | bytes 1622784 | tf_op jit(solution)/shard_map/dot_general | solution.py:48
  11.0 0.0 copy-start.3
  11.0 10.8 %all-to-all-done.1 = f32[8,192,128]{2,1,0:T(8,128)S(1)} async-done(((f32[8,192,128]{2,1,0:T(8,128)}), f32[8,192,128]{2,1,0:T(8,128)S(1)}, u32[]{:S(2)}, u32[]{:S(2)}) %all-to-all-start.1) | async-done | bytes 786464 | tf_op jit(solution)/shard_map/all_to_all | solution.py:29
  21.8 18.8 %all-to-all-start = ((bf16[64,8,1152]{2,1,0:T(8,128)(2,1)}), bf16[64,8,1152]{2,1,0:T(8,128)(2,1)}, u32[]{:S(2)}, u32[]{:S(2)}) async-start(bf16[64,8,1152]{2,1,0:T(8,128)(2,1)} %fusion), calls=%async_computation | async-start | bytes 2359296 | tf_op jit(solution)/shard_map/all_to_all | solution.py:50
  40.6 60.4 %all-to-all-done = bf16[64,8,1152]{2,1,0:T(8,128)(2,1)} async-done(((bf16[64,8,1152]{2,1,0:T(8,128)(2,1)}), bf16[64,8,1152]{2,1,0:T(8,128)(2,1)}, u32[]{:S(2)}, u32[]{:S(2)}) %all-to-all-start) | async-done | bytes 1179680 | tf_op jit(solution)/shard_map/all_to_all | solution.py:50
  101.0 1.0 slice_reduce_fusion
  102.0 0.0 copy-done.3
  102.0 1.7 %fusion.10 = f32[512,256]{0,1:S(1)} fusion(bf16[1024,256]{0,1:T(8,128)(2,1)S(1)} %bitcast.53, bf16[512,1152]{1,0:T(8,128)(2,1)} %bitcast.4), kind=kOutput, calls=%fused_computation.11 | convolution fusion | flops 268435456 | bytes 2097152
  103.8 0.1 fusion.22
  103.8 0.0 copy-start.4
  103.8 0.1 multiply_reduce_fusion
  103.9 0.1 reshape.111
  104.0 0.1 copy.22
  104.0 0.2 reshape.120
  104.2 8.5 %all_to_all.25 = f32[8,1,4096]{2,1,0:T(1,128)S(1)} all-to-all(f32[8,1,4096]{2,1,0:T(1,128)S(1)} %reshape.120), channel_id=1, replica_groups=mesh['ad'=64,'tp'=8] {'tp'}, dimensions={0} | all-to-all | bytes 262144 | tf_op jit(solution)/shard_map/all_to_all | solution.py:64
  112.7 0.5 broadcast.91
  113.2 1.0 reduce.2
  114.2 0.1 reshape.121
  114.4 0.2 reshape.122
  114.5 8.0 %all_to_all.26 = bf16[8,2,2048]{2,1,0:T(2,128)(2,1)S(1)} all-to-all(bf16[8,2,2048]{2,1,0:T(2,128)(2,1)S(1)} %reshape.122), channel_id=1, replica_groups=mesh['ad'=64,'tp'=8] {'tp'}, dimensions={0} | all-to-all | bytes 131072 | tf_op jit(solution)/shard_map/all_to_all | solution.py:66
  122.5 0.1 reshape.123
  122.7 0.1 copy.13
  122.8 0.1 convert_element_type.57
  122.9 0.0 copy-done.4
  122.9 0.3 fusion.8
  123.2 22.3 %all_to_all.27 = bf16[64,8,128]{2,1,0:T(8,128)(2,1)S(1)} all-to-all(bf16[64,8,128]{2,1,0:T(8,128)(2,1)S(1)} %fusion.8), channel_id=1, replica_groups=mesh['ad'=64,'tp'=8] {'ad'}, dimensions={0} | all-to-all | bytes 262144 | tf_op jit(solution)/shard_map/all_to_all | solution.py:78
  145.5 0.9 fusion.9
  (6 shorter events, 0.1 us)
Async XLA Ops:
  0.0 1.6 %copy-start = (bf16[1024,1024]{1,0:T(8,128)(2,1)S(1)}, bf16[1024,1024]{1,0:T(8,128)(2,1)}, u32[]{:S(2)}) copy-start(bf16[1024,1024]{1,0:T(8,128)(2,1)} %param.7) | copy-start | bytes 6291460
  1.6 7.0 %copy-start.2 = (s32[4,48]{1,0:T(4,128)S(1)}, s32[4,48]{1,0:T(4,128)}, u32[]{:S(2)}) copy-start(s32[4,48]{1,0:T(4,128)} %param.6) | copy-start | bytes 2308
  1.6 7.9 %copy-start.1 = (bf16[4,48,1024]{2,1,0:T(8,128)(2,1)S(1)}, bf16[4,48,1024]{2,1,0:T(8,128)(2,1)}, u32[]{:S(2)}) copy-start(bf16[4,48,1024]{2,1,0:T(8,128)(2,1)} %param.5) | copy-start | bytes 1179652
  4.2 17.6 %all-to-all-start.1 = ((f32[8,192,128]{2,1,0:T(8,128)}), f32[8,192,128]{2,1,0:T(8,128)S(1)}, u32[]{:S(2)}, u32[]{:S(2)}) async-start(f32[8,192,128]{2,1,0:T(8,128)} %fusion.4), calls=%async_computation.1 | async-start | bytes 1572864 | tf_op jit(solution)/shard_map/all_to_all | solution.py:29
  11.0 91.1 %copy-start.3 = (bf16[4,1024,64]{1,2,0:T(8,128)(2,1)S(1)}, bf16[4,1024,64]{1,2,0:T(8,128)(2,1)}, u32[]{:S(2)}) copy-start(bf16[4,1024,64]{1,2,0:T(8,128)(2,1)} %param.8) | copy-start | bytes 1572868
  21.8 79.2 %all-to-all-start = ((bf16[64,8,1152]{2,1,0:T(8,128)(2,1)}), bf16[64,8,1152]{2,1,0:T(8,128)(2,1)}, u32[]{:S(2)}, u32[]{:S(2)}) async-start(bf16[64,8,1152]{2,1,0:T(8,128)(2,1)} %fusion), calls=%async_computation | async-start | bytes 2359296 | tf_op jit(solution)/shard_map/all_to_all | solution.py:50
  103.8 19.1 %copy-start.4 = (bf16[4,64,128]{2,1,0:T(8,128)(2,1)S(1)}, bf16[4,64,128]{2,1,0:T(8,128)(2,1)}, u32[]{:S(2)}) copy-start(bf16[4,64,128]{2,1,0:T(8,128)(2,1)} %param.9) | copy-start | bytes 196612

commit v9 on v7

--- a/solution.py
+++ b/solution.py
@@ -21,9 +21,6 @@
     tp_size = lax.axis_size("tp")
     key_feature_width = partial_base.shape[1] // tp_size
     base_pieces = partial_base.reshape(row_total, tp_size, key_feature_width).transpose(1, 0, 2)
-    base_keys_output = jnp.sum(
-        lax.all_to_all(base_pieces, "tp", split_axis=0, concat_axis=0, tiled=True), axis=0
-    )
 
     index_list = row_adapter_index.reshape(step_count, row_dev)
     owner_group = index_list // adapter_number
@@ -44,7 +41,6 @@
     send_rows = jnp.dot(dispatch, rows_tagged, preferred_element_type=jnp.float32).astype(jnp.bfloat16)
     send_rows = send_rows.reshape(groups, slots_per_group, width_per_shard + TAG_WIDTH)
     incoming = lax.all_to_all(send_rows, "ad", split_axis=0, concat_axis=0, tiled=True)
-    incoming, base_keys_output = lax.optimization_barrier((incoming, base_keys_output))
     incoming = incoming.reshape(slot_total, width_per_shard + TAG_WIDTH)
     incoming_rows = incoming[:, :width_per_shard]
     incoming_labels = incoming[:, width_per_shard]
@@ -56,8 +52,15 @@
     selector = (incoming_labels[:, None] == labels[None, :]).astype(jnp.float32)
     down_part = jnp.sum(down_all * selector[:, :, None], axis=1)
     shards = lax.axis_size("tp")
-    chunks = down_part.reshape(shards, slot_total // shards, rank)
-    chunk_sum = jnp.sum(lax.all_to_all(chunks, "tp", split_axis=0, concat_axis=0, tiled=True), axis=0)
+    chunk_width = slot_total // shards * rank
+    chunks = jnp.concatenate(
+        [down_part.reshape(shards, chunk_width), base_pieces.reshape(shards, -1)], axis=1
+    )
+    moved = lax.all_to_all(chunks, "tp", split_axis=0, concat_axis=0, tiled=True)
+    chunk_sum = jnp.sum(moved[:, :chunk_width], axis=0).reshape(slot_total // shards, rank)
+    base_keys_output = jnp.sum(
+        moved[:, chunk_width:].reshape(shards, row_total, key_feature_width), axis=0
+    )
     spread = jnp.broadcast_to(chunk_sum[None], (shards,) + chunk_sum.shape)
     down_sum = lax.all_to_all(spread, "tp", split_axis=0, concat_axis=0, tiled=True).reshape(
         slot_total, rank

time: 145 us -> 141 us (0.972)
  blocking collectives: 38.7 us -> 27 us
  local copies, waits for them, and re-layouts: 4.84 us -> 6.85 us
  matrix products: 4.98 us -> 6.97 us
  starting transfers between devices: 23.1 us -> 24.7 us
  waiting for transfers between devices: 71.2 us -> 72.8 us
    all_to_all x1 -> x0, blocking collectives: 22.3 us -> none  [body(): lax.all_to_all(adapter_update, 'ad', split_axis=0, concat_axis=0, tiled=T...]
    all_to_all x1, blocking collectives: 8.49 us -> 19 us  [body(): lax.all_to_all(chunks, 'tp', split_axis=0, concat_axis=0, tiled=True)]
    all_to_all x1, waiting for transfers between devices: 10.8 us -> 16.3 us  [body(): lax.all_to_all(adapter_update, 'ad', split_axis=0, concat_axis=0, tiled=T...]
    all_to_all x1, waiting for transfers between devices: 60.4 us -> 56.5 us  [body(): lax.all_to_all(send_rows, 'ad', split_axis=0, concat_axis=0, tiled=True)]
    all_to_all x1, starting transfers between devices: 4.47 us -> 5.94 us  [body(): lax.all_to_all(adapter_update, 'ad', split_axis=0, concat_axis=0, tiled=T...]
  transfers between devices with their start and end apart: 2 -> 2, of which waited for: 2 -> 2; matrix products, arithmetic and copies ran while one was open for 2% -> 3% of each run, Pallas kernels for 0% -> 0%
where the time goes in v9:
time: 141 us; the launch traced here: 140 us
  waiting for transfers between devices  72.8 us (52%)
  blocking collectives  27 us (19%)
  starting transfers between devices  24.7 us (18%)
  matrix products  6.97 us (5%)
  local copies, waits for them, and re-layouts  6.85 us (5%)
  other arithmetic  1.67 us (1%)
    all_to_all x1, waiting for transfers between devices, body(): lax.all_to_all(send_rows, 'ad', split_axis=0, concat_axis=0, tiled=True)  56.5 us
    all_to_all x1, blocking collectives, body(): lax.all_to_all(chunks, 'tp', split_axis=0, concat_axis=0, tiled=True)  19 us
    all_to_all x1, starting transfers between devices, body(): lax.all_to_all(send_rows, 'ad', split_axis=0, concat_axis=0, tiled=True)  18.8 us
    all_to_all x1, waiting for transfers between devices, body(): lax.all_to_all(adapter_update, 'ad', split_axis=0, concat_axis=0, tiled=T...  16.3 us
    all_to_all x1, blocking collectives, body(): lax.all_to_all(spread, 'tp', split_axis=0, concat_axis=0, tiled=True)  8 us
    all_to_all x1, starting transfers between devices, body(): lax.all_to_all(adapter_update, 'ad', split_axis=0, concat_axis=0, tiled=T...  5.94 us
    dot_general x1, local copies, waits for them, and re-layouts, body(): jnp.dot(gathered_rows, key_base_weight, preferred_element_type=jnp.float32)  2.91 us
  transfers between devices with their start and end apart: 2, of which 2 were waited for; matrix products, arithmetic and copies ran while one was open for 3% of the time, Pallas kernels for 0%

profile of v9, /device:TPU:2, one launch (start us, length us, event | category | flops | bytes accessed | tf_op | source)
XLA Modules:
  0.0 140.2 jit_solution(6244041455832528338)
XLA Ops:
  0.0 0.0 copy-start
  0.0 0.8 fusion.18
  0.8 0.1 broadcast_in_dim.8
  0.8 0.1 fusion.15
  0.9 0.1 reduce_window_sum.11
  1.1 0.2 select_reduce_fusion
  1.3 0.1 add_add_fusion
  1.3 0.1 eq.53
  1.4 0.1 broadcast_in_dim.9
  1.5 2.6 %fusion = bf16[64,8,1152]{2,1,0:T(8,128)(2,1)} fusion(bf16[192,128]{1,0:T(8,128)(2,1)S(1)} %broadcast_in_dim.9, bf16[192,1024]{1,0:T(8,128)(2,1)} %bitcast.50, s32[192]{0:T(256)S(1)} %eq.53), kind=kOutput, calls=%fused_computation.1 | convolution fusion | flops 228065280 | bytes 1622784 | tf_op jit(solution)/shard_map/dot_general | solution.py:41
  4.1 18.8 %all-to-all-start = ((bf16[64,8,1152]{2,1,0:T(8,128)(2,1)}), bf16[64,8,1152]{2,1,0:T(8,128)(2,1)}, u32[]{:S(2)}, u32[]{:S(2)}) async-start(bf16[64,8,1152]{2,1,0:T(8,128)(2,1)} %fusion), calls=%async_computation | async-start | bytes 2359296 | tf_op jit(solution)/shard_map/all_to_all | solution.py:43
  22.9 0.0 copy-start.1
  22.9 2.9 %copy.16 = bf16[1024,1024]{1,0:T(8,128)(2,1)S(1)} copy(bf16[1024,1024]{0,1:T(8,128)(2,1)} %bitcast.49) | data formatting | bytes 4194304 | tf_op jit(solution)/shard_map/dot_general | solution.py:20
  25.8 0.0 copy-done.1
  25.8 0.8 convolution_bitcast_fusion
  26.7 0.5 copy.22
  27.2 56.5 %all-to-all-done = bf16[64,8,1152]{2,1,0:T(8,128)(2,1)} async-done(((bf16[64,8,1152]{2,1,0:T(8,128)(2,1)}), bf16[64,8,1152]{2,1,0:T(8,128)(2,1)}, u32[]{:S(2)}, u32[]{:S(2)}) %all-to-all-start) | async-done | bytes 1179680 | tf_op jit(solution)/shard_map/all_to_all | solution.py:43
  83.6 1.0 slice_reduce_fusion.2
  84.7 0.0 copy-done
  84.7 1.7 %fusion.4 = f32[512,256]{0,1:S(1)} fusion(bf16[1024,256]{0,1:T(8,128)(2,1)S(1)} %bitcast.44, bf16[512,1152]{1,0:T(8,128)(2,1)} %bitcast.2), kind=kOutput, calls=%fused_computation.8 | convolution fusion | flops 268435456 | bytes 2097152
  86.4 0.1 fusion.16
  86.5 0.1 multiply_reduce_fusion
  86.5 0.1 copy.12
  86.6 0.1 reshape.116
  86.8 0.1 pad_maximum_fusion
  86.8 0.7 all_to_all.18
  87.5 0.0 copy-start.2
  87.5 19.0 %all_to_all.27 = f32[8,1,28672]{2,1,0:T(1,128)S(1)} all-to-all(f32[8,1,28672]{2,1,0:T(1,128)S(1)} %all_to_all.18), channel_id=1, replica_groups=mesh['ad'=64,'tp'=8] {'tp'}, dimensions={0} | all-to-all | bytes 1835008 | tf_op jit(solution)/shard_map/all_to_all | solution.py:59
  106.5 0.5 copy.21
  107.1 0.1 broadcast_in_dim.10
  107.2 0.1 copy.14
  107.3 0.2 reshape.126
  107.4 8.0 %all_to_all.28 = bf16[8,2,2048]{2,1,0:T(2,128)(2,1)S(1)} all-to-all(bf16[8,2,2048]{2,1,0:T(2,128)(2,1)S(1)} %reshape.126), channel_id=1, replica_groups=mesh['ad'=64,'tp'=8] {'tp'}, dimensions={0} | all-to-all | bytes 131072 | tf_op jit(solution)/shard_map/all_to_all | solution.py:65
  115.4 0.1 reshape.127
  115.6 0.1 copy.15
  115.7 0.1 convert_element_type.57
  115.8 0.0 copy-done.2
  115.8 0.9 fusion.2
  116.8 5.9 %all-to-all-start.3 = ((bf16[64,8,128]{2,1,0:T(8,128)(2,1)}), bf16[64,8,128]{2,1,0:T(8,128)(2,1)S(1)}, u32[]{:S(2)}, u32[]{:S(2)}) async-start(bf16[64,8,128]{2,1,0:T(8,128)(2,1)} %fusion.2), calls=%async_computation.3 | async-start | bytes 262144 | tf_op jit(solution)/shard_map/all_to_all | solution.py:77
  122.7 0.2 slice_reduce_fusion
  122.9 16.3 %all-to-all-done.3 = bf16[64,8,128]{2,1,0:T(8,128)(2,1)S(1)} async-done(((bf16[64,8,128]{2,1,0:T(8,128)(2,1)}), bf16[64,8,128]{2,1,0:T(8,128)(2,1)S(1)}, u32[]{:S(2)}, u32[]{:S(2)}) %all-to-all-start.3) | async-done | bytes 131104 | tf_op jit(solution)/shard_map/all_to_all | solution.py:77
  139.2 0.9 fusion.3
  (4 shorter events, 0.1 us)
Async XLA Ops:
  0.0 84.7 %copy-start = (bf16[4,1024,64]{1,2,0:T(8,128)(2,1)S(1)}, bf16[4,1024,64]{1,2,0:T(8,128)(2,1)}, u32[]{:S(2)}) copy-start(bf16[4,1024,64]{1,2,0:T(8,128)(2,1)} %param.8) | copy-start | bytes 1572868
  4.1 79.5 %all-to-all-start = ((bf16[64,8,1152]{2,1,0:T(8,128)(2,1)}), bf16[64,8,1152]{2,1,0:T(8,128)(2,1)}, u32[]{:S(2)}, u32[]{:S(2)}) async-start(bf16[64,8,1152]{2,1,0:T(8,128)(2,1)} %fusion), calls=%async_computation | async-start | bytes 2359296 | tf_op jit(solution)/shard_map/all_to_all | solution.py:43
  22.9 2.9 %copy-start.1 = (bf16[4,48,1024]{2,1,0:T(8,128)(2,1)S(1)}, bf16[4,48,1024]{2,1,0:T(8,128)(2,1)}, u32[]{:S(2)}) copy-start(bf16[4,48,1024]{2,1,0:T(8,128)(2,1)} %param.5) | copy-start | bytes 1179652
  87.5 28.3 %copy-start.2 = (bf16[4,64,128]{2,1,0:T(8,128)(2,1)S(1)}, bf16[4,64,128]{2,1,0:T(8,128)(2,1)}, u32[]{:S(2)}) copy-start(bf16[4,64,128]{2,1,0:T(8,128)(2,1)} %param.9) | copy-start | bytes 196612
  116.8 22.5 %all-to-all-start.3 = ((bf16[64,8,128]{2,1,0:T(8,128)(2,1)}), bf16[64,8,128]{2,1,0:T(8,128)(2,1)S(1)}, u32[]{:S(2)}, u32[]{:S(2)}) async-start(bf16[64,8,128]{2,1,0:T(8,128)(2,1)} %fusion.2), calls=%async_computation.3 | async-start | bytes 262144 | tf_op jit(solution)/shard_map/all_to_all | solution.py:77

commit v10 on v9

--- a/solution.py
+++ b/solution.py
@@ -53,13 +53,18 @@
     down_part = jnp.sum(down_all * selector[:, :, None], axis=1)
     shards = lax.axis_size("tp")
     chunk_width = slot_total // shards * rank
+    down_flat = down_part.reshape(shards, chunk_width)
+    down_high = down_flat.astype(jnp.bfloat16)
+    down_low_part = (down_flat - down_high.astype(jnp.float32)).astype(jnp.bfloat16)
     chunks = jnp.concatenate(
-        [down_part.reshape(shards, chunk_width), base_pieces.reshape(shards, -1)], axis=1
+        [down_high, down_low_part, base_pieces.reshape(shards, -1).astype(jnp.bfloat16)], axis=1
     )
-    moved = lax.all_to_all(chunks, "tp", split_axis=0, concat_axis=0, tiled=True)
-    chunk_sum = jnp.sum(moved[:, :chunk_width], axis=0).reshape(slot_total // shards, rank)
+    moved = lax.all_to_all(chunks, "tp", split_axis=0, concat_axis=0, tiled=True).astype(jnp.float32)
+    chunk_sum = jnp.sum(
+        moved[:, :chunk_width] + moved[:, chunk_width : 2 * chunk_width], axis=0
+    ).reshape(slot_total // shards, rank)
     base_keys_output = jnp.sum(
-        moved[:, chunk_width:].reshape(shards, row_total, key_feature_width), axis=0
+        moved[:, 2 * chunk_width :].reshape(shards, row_total, key_feature_width), axis=0
     )
     spread = jnp.broadcast_to(chunk_sum[None], (shards,) + chunk_sum.shape)
     down_sum = lax.all_to_all(spread, "tp", split_axis=0, concat_axis=0, tiled=True).reshape(

time: 141 us -> 138 us (0.979)
  blocking collectives: 27 us -> 22.6 us
    all_to_all x1, blocking collectives: 19 us -> 14.6 us  [body(): lax.all_to_all(chunks, 'tp', split_axis=0, concat_axis=0, tiled=True)]
where the time goes in v10:
time: 138 us
  waiting for transfers between devices  73 us (53%)
  starting transfers between devices  24.7 us (18%)
  blocking collectives  22.6 us (16%)
  local copies, waits for them, and re-layouts  7.49 us (5%)
  matrix products  6.96 us (5%)
  other arithmetic  2.69 us (2%)
    all_to_all x1, waiting for transfers between devices, body(): lax.all_to_all(send_rows, 'ad', split_axis=0, concat_axis=0, tiled=True)  56.7 us
    all_to_all x1, starting transfers between devices, body(): lax.all_to_all(send_rows, 'ad', split_axis=0, concat_axis=0, tiled=True)  18.8 us
    all_to_all x1, waiting for transfers between devices, body(): lax.all_to_all(adapter_update, 'ad', split_axis=0, concat_axis=0, tiled=T...  16.3 us
    all_to_all x1, blocking collectives, body(): lax.all_to_all(chunks, 'tp', split_axis=0, concat_axis=0, tiled=True)  14.6 us
    all_to_all x1, blocking collectives, body(): lax.all_to_all(spread, 'tp', split_axis=0, concat_axis=0, tiled=True)  8 us
    all_to_all x1, starting transfers between devices, body(): lax.all_to_all(adapter_update, 'ad', split_axis=0, concat_axis=0, tiled=T...  5.94 us
    dot_general x1, local copies, waits for them, and re-layouts, body(): jnp.dot(gathered_rows, key_base_weight, preferred_element_type=jnp.float32)  2.91 us
  transfers between devices with their start and end apart: 2, of which 2 were waited for; matrix products, arithmetic and copies ran while one was open for 3% of the time, Pallas kernels for 0%

profile of v10, /device:TPU:2, one launch (start us, length us, event | category | flops | bytes accessed | tf_op | source)
XLA Modules:
  0.0 137.7 jit_solution(1529537217612380819)
XLA Ops:
  0.0 0.0 copy-start
  0.0 0.8 fusion.20
  0.8 0.1 fusion.17
  0.9 0.1 reduce_window_sum.11
  1.0 0.2 select_reduce_fusion
  1.2 0.1 add_add_fusion
  1.3 0.1 eq.53
  1.3 0.1 broadcast_in_dim.8
  1.4 0.1 broadcast_in_dim.9
  1.5 2.6 %fusion = bf16[64,8,1152]{2,1,0:T(8,128)(2,1)} fusion(bf16[192,128]{1,0:T(8,128)(2,1)S(1)} %broadcast_in_dim.9, bf16[192,1024]{1,0:T(8,128)(2,1)} %bitcast.52, s32[192]{0:T(256)S(1)} %eq.53), kind=kOutput, calls=%fused_computation.1 | convolution fusion | flops 228065280 | bytes 1622784 | tf_op jit(solution)/shard_map/dot_general | solution.py:41
  4.1 18.8 %all-to-all-start = ((bf16[64,8,1152]{2,1,0:T(8,128)(2,1)}), bf16[64,8,1152]{2,1,0:T(8,128)(2,1)}, u32[]{:S(2)}, u32[]{:S(2)}) async-start(bf16[64,8,1152]{2,1,0:T(8,128)(2,1)} %fusion), calls=%async_computation | async-start | bytes 2359296 | tf_op jit(solution)/shard_map/all_to_all | solution.py:43
  22.9 0.0 copy-start.1
  22.9 2.9 %copy.17 = bf16[1024,1024]{1,0:T(8,128)(2,1)S(1)} copy(bf16[1024,1024]{0,1:T(8,128)(2,1)} %bitcast.50) | data formatting | bytes 4194304 | tf_op jit(solution)/shard_map/dot_general | solution.py:20
  25.8 0.0 copy-done.1
  25.9 0.8 fusion.1
  26.7 0.3 copy.23
  27.0 56.7 %all-to-all-done = bf16[64,8,1152]{2,1,0:T(8,128)(2,1)} async-done(((bf16[64,8,1152]{2,1,0:T(8,128)(2,1)}), bf16[64,8,1152]{2,1,0:T(8,128)(2,1)}, u32[]{:S(2)}, u32[]{:S(2)}) %all-to-all-start) | async-done | bytes 1179680 | tf_op jit(solution)/shard_map/all_to_all | solution.py:43
  83.6 1.0 slice_reduce_fusion.1
  84.7 0.0 copy-done
  84.7 1.7 %fusion.5 = f32[512,256]{0,1:S(1)} fusion(bf16[1024,256]{0,1:T(8,128)(2,1)S(1)} %bitcast.46, bf16[512,1152]{1,0:T(8,128)(2,1)} %bitcast.2), kind=kOutput, calls=%fused_computation.9 | convolution fusion | flops 268435456 | bytes 2097152
  86.4 0.1 fusion.18
  86.5 0.1 multiply_reduce_fusion
  86.5 0.1 copy.12
  86.6 0.1 reshape.117
  86.8 0.5 broadcast.90
  87.3 1.0 reduce.3
  88.4 0.4 reshape.127
  88.8 14.6 %all_to_all.24 = bf16[8,2,16384]{2,1,0:T(2,128)(2,1)S(1)} all-to-all(bf16[8,2,16384]{2,1,0:T(2,128)(2,1)S(1)} %reshape.127), channel_id=1, replica_groups=mesh['ad'=64,'tp'=8] {'tp'}, dimensions={0} | all-to-all | bytes 1048576 | tf_op jit(solution)/shard_map/all_to_all | solution.py:62
  103.4 0.5 reshape.128
  103.9 0.0 copy-start.2
  103.9 0.6 copy.22
  104.5 0.1 fusion.13
  104.6 0.1 broadcast_in_dim.10
  104.7 0.1 copy.15
  104.8 0.2 reshape.129
  105.0 8.0 %all_to_all.25 = bf16[8,2,2048]{2,1,0:T(2,128)(2,1)S(1)} all-to-all(bf16[8,2,2048]{2,1,0:T(2,128)(2,1)S(1)} %reshape.129), channel_id=1, replica_groups=mesh['ad'=64,'tp'=8] {'tp'}, dimensions={0} | all-to-all | bytes 131072 | tf_op jit(solution)/shard_map/all_to_all | solution.py:70
  113.0 0.1 reshape.130
  113.1 0.1 copy.16
  113.2 0.1 convert_element_type.89
  113.4 0.0 copy-done.2
  113.4 0.9 fusion.3
  114.3 5.9 %all-to-all-start.3 = ((bf16[64,8,128]{2,1,0:T(8,128)(2,1)}), bf16[64,8,128]{2,1,0:T(8,128)(2,1)S(1)}, u32[]{:S(2)}, u32[]{:S(2)}) async-start(bf16[64,8,128]{2,1,0:T(8,128)(2,1)} %fusion.3), calls=%async_computation.3 | async-start | bytes 262144 | tf_op jit(solution)/shard_map/all_to_all | solution.py:82
  120.2 0.2 slice_reduce_fusion
  120.4 16.3 %all-to-all-done.3 = bf16[64,8,128]{2,1,0:T(8,128)(2,1)S(1)} async-done(((bf16[64,8,128]{2,1,0:T(8,128)(2,1)}), bf16[64,8,128]{2,1,0:T(8,128)(2,1)S(1)}, u32[]{:S(2)}, u32[]{:S(2)}) %all-to-all-start.3) | async-done | bytes 131104 | tf_op jit(solution)/shard_map/all_to_all | solution.py:82
  136.7 0.9 fusion.4
  (5 shorter events, 0.1 us)
Async XLA Ops:
  0.0 84.7 %copy-start = (bf16[4,1024,64]{1,2,0:T(8,128)(2,1)S(1)}, bf16[4,1024,64]{1,2,0:T(8,128)(2,1)}, u32[]{:S(2)}) copy-start(bf16[4,1024,64]{1,2,0:T(8,128)(2,1)} %param.8) | copy-start | bytes 1572868
  4.1 79.5 %all-to-all-start = ((bf16[64,8,1152]{2,1,0:T(8,128)(2,1)}), bf16[64,8,1152]{2,1,0:T(8,128)(2,1)}, u32[]{:S(2)}, u32[]{:S(2)}) async-start(bf16[64,8,1152]{2,1,0:T(8,128)(2,1)} %fusion), calls=%async_computation | async-start | bytes 2359296 | tf_op jit(solution)/shard_map/all_to_all | solution.py:43
  22.9 2.9 %copy-start.1 = (bf16[4,48,1024]{2,1,0:T(8,128)(2,1)S(1)}, bf16[4,48,1024]{2,1,0:T(8,128)(2,1)}, u32[]{:S(2)}) copy-start(bf16[4,48,1024]{2,1,0:T(8,128)(2,1)} %param.5) | copy-start | bytes 1179652
  103.9 9.4 %copy-start.2 = (bf16[4,64,128]{2,1,0:T(8,128)(2,1)S(1)}, bf16[4,64,128]{2,1,0:T(8,128)(2,1)}, u32[]{:S(2)}) copy-start(bf16[4,64,128]{2,1,0:T(8,128)(2,1)} %param.9) | copy-start | bytes 196612
  114.3 22.5 %all-to-all-start.3 = ((bf16[64,8,128]{2,1,0:T(8,128)(2,1)}), bf16[64,8,128]{2,1,0:T(8,128)(2,1)S(1)}, u32[]{:S(2)}, u32[]{:S(2)}) async-start(bf16[64,8,128]{2,1,0:T(8,128)(2,1)} %fusion.3), calls=%async_computation.3 | async-start | bytes 262144 | tf_op jit(solution)/shard_map/all_to_all | solution.py:82

commit v11 on v9

--- a/solution.py
+++ b/solution.py
@@ -21,6 +21,12 @@
     tp_size = lax.axis_size("tp")
     key_feature_width = partial_base.shape[1] // tp_size
     base_pieces = partial_base.reshape(row_total, tp_size, key_feature_width).transpose(1, 0, 2)
+    half_rows = row_total // 2
+    base_halves = base_pieces.reshape(tp_size, 2, half_rows, key_feature_width)
+    core = lax.axis_index("tp") % 2
+    keep = lax.dynamic_index_in_dim(base_halves, core, axis=1, keepdims=False)
+    give = lax.dynamic_index_in_dim(base_halves, 1 - core, axis=1, keepdims=False)
+    pair_sum = keep + lax.ppermute(give, "tp", [(k, k ^ 1) for k in range(tp_size)])
 
     index_list = row_adapter_index.reshape(step_count, row_dev)
     owner_group = index_list // adapter_number
@@ -54,13 +60,13 @@
     shards = lax.axis_size("tp")
     chunk_width = slot_total // shards * rank
     chunks = jnp.concatenate(
-        [down_part.reshape(shards, chunk_width), base_pieces.reshape(shards, -1)], axis=1
+        [down_part.reshape(shards, chunk_width), pair_sum.reshape(shards, -1)], axis=1
     )
     moved = lax.all_to_all(chunks, "tp", split_axis=0, concat_axis=0, tiled=True)
     chunk_sum = jnp.sum(moved[:, :chunk_width], axis=0).reshape(slot_total // shards, rank)
     base_keys_output = jnp.sum(
-        moved[:, chunk_width:].reshape(shards, row_total, key_feature_width), axis=0
-    )
+        moved[:, chunk_width:].reshape(shards // 2, 2, half_rows, key_feature_width), axis=0
+    ).reshape(row_total, key_feature_width)
     spread = jnp.broadcast_to(chunk_sum[None], (shards,) + chunk_sum.shape)
     down_sum = lax.all_to_all(spread, "tp", split_axis=0, concat_axis=0, tiled=True).reshape(
         slot_total, rank

time: 141 us -> 136 us (0.965)
  blocking collectives: 27 us -> 22.6 us
  waiting for transfers between devices: 72.8 us -> 69.9 us
  starting transfers between devices: 24.7 us -> 26.7 us
    all_to_all x1, waiting for transfers between devices: 56.5 us -> 52 us  [body(): lax.all_to_all(send_rows, 'ad', split_axis=0, concat_axis=0, tiled=True)]
    all_to_all x1, blocking collectives: 19 us -> 14.6 us  [body(): lax.all_to_all(chunks, 'tp', split_axis=0, concat_axis=0, tiled=True)]
    ppermute x0 -> x1, starting transfers between devices: none -> 1.92 us  [body(): lax.ppermute(give, 'tp', [(k, k ^ 1) for k in range(tp_size)])]
    ppermute x0 -> x1, waiting for transfers between devices: none -> 1.67 us  [body(): lax.ppermute(give, 'tp', [(k, k ^ 1) for k in range(tp_size)])]
  transfers between devices with their start and end apart: 2 -> 3, of which waited for: 2 -> 3; matrix products, arithmetic and copies ran while one was open for 3% -> 4% of each run, Pallas kernels for 0% -> 0%
where the time goes in v11:
time: 136 us; the launch traced here: 135 us
  waiting for transfers between devices  69.9 us (51%)
  starting transfers between devices  26.7 us (20%)
  blocking collectives  22.6 us (17%)
  matrix products  7.96 us (6%)
  local copies, waits for them, and re-layouts  6.13 us (5%)
  other arithmetic  1.78 us (1%)
    all_to_all x1, waiting for transfers between devices, body(): lax.all_to_all(send_rows, 'ad', split_axis=0, concat_axis=0, tiled=True)  52 us
    all_to_all x1, starting transfers between devices, body(): lax.all_to_all(send_rows, 'ad', split_axis=0, concat_axis=0, tiled=True)  18.8 us
    all_to_all x1, waiting for transfers between devices, body(): lax.all_to_all(adapter_update, 'ad', split_axis=0, concat_axis=0, tiled=T...  16.2 us
    all_to_all x1, blocking collectives, body(): lax.all_to_all(chunks, 'tp', split_axis=0, concat_axis=0, tiled=True)  14.6 us
    all_to_all x1, blocking collectives, body(): lax.all_to_all(spread, 'tp', split_axis=0, concat_axis=0, tiled=True)  8 us
    all_to_all x1, starting transfers between devices, body(): lax.all_to_all(adapter_update, 'ad', split_axis=0, concat_axis=0, tiled=T...  5.94 us
    dot_general x1, local copies, waits for them, and re-layouts, body(): jnp.dot(gathered_rows, key_base_weight, preferred_element_type=jnp.float32)  2.86 us
  transfers between devices with their start and end apart: 3, of which 3 were waited for; matrix products, arithmetic and copies ran while one was open for 4% of the time, Pallas kernels for 0%

profile of v11, /device:TPU:2, one launch (start us, length us, event | category | flops | bytes accessed | tf_op | source)
XLA Modules:
  0.0 135.3 jit_solution(13525467066487789401)
XLA Ops:
  0.0 0.0 copy-start
  0.0 0.8 add_select_fusion.1
  0.8 0.1 broadcast_in_dim.8
  0.8 0.1 fusion.16
  0.9 0.1 reduce_window_sum.11
  1.1 0.2 select_reduce_fusion
  1.3 0.1 add_add_fusion
  1.3 0.1 eq.55
  1.4 0.1 broadcast_in_dim.9
  1.5 2.6 %fusion = bf16[64,8,1152]{2,1,0:T(8,128)(2,1)} fusion(bf16[192,128]{1,0:T(8,128)(2,1)S(1)} %broadcast_in_dim.9, bf16[192,1024]{1,0:T(8,128)(2,1)} %bitcast.69, s32[192]{0:T(256)S(1)} %eq.55), kind=kOutput, calls=%fused_computation.1 | convolution fusion | flops 228065280 | bytes 1622784 | tf_op jit(solution)/shard_map/dot_general | solution.py:47
  4.1 18.8 %all-to-all-start = ((bf16[64,8,1152]{2,1,0:T(8,128)(2,1)}), bf16[64,8,1152]{2,1,0:T(8,128)(2,1)}, u32[]{:S(2)}, u32[]{:S(2)}) async-start(bf16[64,8,1152]{2,1,0:T(8,128)(2,1)} %fusion), calls=%async_computation | async-start | bytes 2359296 | tf_op jit(solution)/shard_map/all_to_all | solution.py:49
  22.9 2.9 %copy.18 = bf16[1024,1024]{1,0:T(8,128)(2,1)S(1)} copy(bf16[1024,1024]{0,1:T(8,128)(2,1)} %bitcast.66) | data formatting | bytes 4194304 | tf_op jit(solution)/shard_map/dot_general | solution.py:20
  25.8 1.8 %fusion.22 = f32[192,8,128]{2,0,1:T(8,128)S(1)} fusion(bf16[192,1024,1]{1,0,2:T(8,128)(2,1)} %bitcast.70, bf16[8,128,1024]{2,1,0:T(8,128)(2,1)S(1)} %bitcast.63), kind=kOutput, calls=%fused_computation.49 | convolution fusion | flops 402653184 | bytes 3276800 | tf_op jit(solution)/shard_map/dot_general | solution.py:20
  27.7 1.9 %collective-permute-start = (f32[8,96,128]{2,1,0:T(8,128)S(1)}, f32[8,96,128]{2,1,0:T(8,128)S(1)}, u32[]{:S(2)}, u32[]{:S(2)}) collective-permute-start(f32[8,96,128]{2,1,0:T(8,128)S(1)} %dynamic-slice_bitcast_fusion), channel_id=1, source_target_pairs={{0,1},{1,0},{2,3},{3,2},{4,5},{5,4},{6,7},{7,6},{8,9},{9,8},{10,11... | collective-permute-start | bytes 1179656 | tf_op jit(solution)/shard_map/ppermute | solution.py:29
  29.6 1.7 %collective-permute-done = f32[8,96,128]{2,1,0:T(8,128)S(1)} collective-permute-done((f32[8,96,128]{2,1,0:T(8,128)S(1)}, f32[8,96,128]{2,1,0:T(8,128)S(1)}, u32[]{:S(2)}, u32[]{:S(2)}) %collective-permute-start) | collective-permute-done | bytes 393248 | tf_op jit(solution)/shard_map/ppermute | solution.py:29
  31.4 0.2 copy.28
  31.6 52.0 %all-to-all-done = bf16[64,8,1152]{2,1,0:T(8,128)(2,1)} async-done(((bf16[64,8,1152]{2,1,0:T(8,128)(2,1)}), bf16[64,8,1152]{2,1,0:T(8,128)(2,1)}, u32[]{:S(2)}, u32[]{:S(2)}) %all-to-all-start) | async-done | bytes 1179680 | tf_op jit(solution)/shard_map/all_to_all | solution.py:49
  83.6 1.0 slice_reduce_fusion.1
  84.7 0.0 copy-done
  84.7 1.7 %fusion.4 = f32[512,256]{0,1:S(1)} fusion(bf16[1024,256]{0,1:T(8,128)(2,1)S(1)} %bitcast.62, bf16[512,1152]{1,0:T(8,128)(2,1)} %bitcast.2), kind=kOutput, calls=%fused_computation.7 | convolution fusion | flops 268435456 | bytes 2097152
  86.4 0.1 fusion.17
  86.5 0.1 multiply_reduce_fusion
  86.5 0.1 copy.12
  86.6 0.1 reshape.123
  86.8 0.0 copy-start.1
  86.8 0.4 all_to_all.18
  87.2 14.6 %all_to_all.27 = f32[8,1,16384]{2,1,0:T(1,128)S(1)} all-to-all(f32[8,1,16384]{2,1,0:T(1,128)S(1)} %all_to_all.18), channel_id=1, replica_groups=mesh['ad'=64,'tp'=8] {'tp'}, dimensions={0} | all-to-all | bytes 1048576 | tf_op jit(solution)/shard_map/all_to_all | solution.py:65
  101.8 0.3 copy.27
  102.2 0.1 broadcast_in_dim.10
  102.3 0.1 copy.16
  102.4 0.2 reshape.136
  102.6 8.0 %all_to_all.28 = bf16[8,2,2048]{2,1,0:T(2,128)(2,1)S(1)} all-to-all(bf16[8,2,2048]{2,1,0:T(2,128)(2,1)S(1)} %reshape.136), channel_id=1, replica_groups=mesh['ad'=64,'tp'=8] {'tp'}, dimensions={0} | all-to-all | bytes 131072 | tf_op jit(solution)/shard_map/all_to_all | solution.py:71
  110.6 0.1 reshape.137
  110.7 0.1 copy.17
  110.8 0.1 convert_element_type.57
  110.9 0.0 copy-done.1
  111.0 0.9 fusion.2
  111.9 5.9 %all-to-all-start.3 = ((bf16[64,8,128]{2,1,0:T(8,128)(2,1)}), bf16[64,8,128]{2,1,0:T(8,128)(2,1)S(1)}, u32[]{:S(2)}, u32[]{:S(2)}) async-start(bf16[64,8,128]{2,1,0:T(8,128)(2,1)} %fusion.2), calls=%async_computation.3 | async-start | bytes 262144 | tf_op jit(solution)/shard_map/all_to_all | solution.py:83
  117.9 0.3 reduce.2
  118.2 16.2 %all-to-all-done.3 = bf16[64,8,128]{2,1,0:T(8,128)(2,1)S(1)} async-done(((bf16[64,8,128]{2,1,0:T(8,128)(2,1)}), bf16[64,8,128]{2,1,0:T(8,128)(2,1)S(1)}, u32[]{:S(2)}, u32[]{:S(2)}) %all-to-all-start.3) | async-done | bytes 131104 | tf_op jit(solution)/shard_map/all_to_all | solution.py:83
  134.3 0.9 fusion.3
  (9 shorter events, 0.2 us)
Async XLA Ops:
  0.0 84.7 %copy-start = (bf16[4,1024,64]{1,2,0:T(8,128)(2,1)S(1)}, bf16[4,1024,64]{1,2,0:T(8,128)(2,1)}, u32[]{:S(2)}) copy-start(bf16[4,1024,64]{1,2,0:T(8,128)(2,1)} %param.8) | copy-start | bytes 1572868
  4.1 79.5 %all-to-all-start = ((bf16[64,8,1152]{2,1,0:T(8,128)(2,1)}), bf16[64,8,1152]{2,1,0:T(8,128)(2,1)}, u32[]{:S(2)}, u32[]{:S(2)}) async-start(bf16[64,8,1152]{2,1,0:T(8,128)(2,1)} %fusion), calls=%async_computation | async-start | bytes 2359296 | tf_op jit(solution)/shard_map/all_to_all | solution.py:49
  27.7 3.6 %collective-permute-start = (f32[8,96,128]{2,1,0:T(8,128)S(1)}, f32[8,96,128]{2,1,0:T(8,128)S(1)}, u32[]{:S(2)}, u32[]{:S(2)}) collective-permute-start(f32[8,96,128]{2,1,0:T(8,128)S(1)} %dynamic-slice_bitcast_fusion), channel_id=1, source_target_pairs={{0,1},{1,0},{2,3},{3,2},{4,5},{5,4},{6,7},{7,6},{8,9},{9,8},{10,11... | collective-permute-start | bytes 1179656 | tf_op jit(solution)/shard_map/ppermute | solution.py:29
  86.8 24.1 %copy-start.1 = (bf16[4,64,128]{2,1,0:T(8,128)(2,1)S(1)}, bf16[4,64,128]{2,1,0:T(8,128)(2,1)}, u32[]{:S(2)}) copy-start(bf16[4,64,128]{2,1,0:T(8,128)(2,1)} %param.9) | copy-start | bytes 196612
  111.9 22.5 %all-to-all-start.3 = ((bf16[64,8,128]{2,1,0:T(8,128)(2,1)}), bf16[64,8,128]{2,1,0:T(8,128)(2,1)S(1)}, u32[]{:S(2)}, u32[]{:S(2)}) async-start(bf16[64,8,128]{2,1,0:T(8,128)(2,1)} %fusion.2), calls=%async_computation.3 | async-start | bytes 262144 | tf_op jit(solution)/shard_map/all_to_all | solution.py:83

commit v12 on v7

--- a/solution.py
+++ b/solution.py
@@ -21,9 +21,17 @@
     tp_size = lax.axis_size("tp")
     key_feature_width = partial_base.shape[1] // tp_size
     base_pieces = partial_base.reshape(row_total, tp_size, key_feature_width).transpose(1, 0, 2)
-    base_keys_output = jnp.sum(
-        lax.all_to_all(base_pieces, "tp", split_axis=0, concat_axis=0, tiled=True), axis=0
-    )
+    tp_index = lax.axis_index("tp")
+    base_left = base_pieces
+    bit = 1
+    while bit < tp_size:
+        base_left = base_left.reshape(base_left.shape[0] // 2, 2, row_total, key_feature_width)
+        side = (tp_index // bit) % 2
+        keep = lax.dynamic_index_in_dim(base_left, side, axis=1, keepdims=False)
+        give = lax.dynamic_index_in_dim(base_left, 1 - side, axis=1, keepdims=False)
+        base_left = keep + lax.ppermute(give, "tp", [(k, k ^ bit) for k in range(tp_size)])
+        bit *= 2
+    base_keys_output = base_left.reshape(row_total, key_feature_width)
 
     index_list = row_adapter_index.reshape(step_count, row_dev)
     owner_group = index_list // adapter_number
@@ -44,7 +52,6 @@
     send_rows = jnp.dot(dispatch, rows_tagged, preferred_element_type=jnp.float32).astype(jnp.bfloat16)
     send_rows = send_rows.reshape(groups, slots_per_group, width_per_shard + TAG_WIDTH)
     incoming = lax.all_to_all(send_rows, "ad", split_axis=0, concat_axis=0, tiled=True)
-    incoming, base_keys_output = lax.optimization_barrier((incoming, base_keys_output))
     incoming = incoming.reshape(slot_total, width_per_shard + TAG_WIDTH)
     incoming_rows = incoming[:, :width_per_shard]
     incoming_labels = incoming[:, width_per_shard]
@@ -56,6 +63,7 @@
     selector = (incoming_labels[:, None] == labels[None, :]).astype(jnp.float32)
     down_part = jnp.sum(down_all * selector[:, :, None], axis=1)
     shards = lax.axis_size("tp")
+    chunk_width = slot_total // shards * rank
     chunks = down_part.reshape(shards, slot_total // shards, rank)
     chunk_sum = jnp.sum(lax.all_to_all(chunks, "tp", split_axis=0, concat_axis=0, tiled=True), axis=0)
     spread = jnp.broadcast_to(chunk_sum[None], (shards,) + chunk_sum.shape)

time: 145 us -> 135 us (0.931)
  blocking collectives: 38.7 us -> 0 us
  starting transfers between devices: 23.1 us -> 41.3 us
  waiting for transfers between devices: 71.2 us -> 75.1 us
  matrix products: 4.98 us -> 7.31 us
  local copies, waits for them, and re-layouts: 4.84 us -> 7 us
    all_to_all x3 -> x0, blocking collectives: 38.7 us -> none  [the longest x1 22.3 us: body(): lax.all_to_all(adapter_update, 'ad', split_axis=0, concat_axis=0, tiled=T...]
    all_to_all x1 -> x3, waiting for transfers between devices: 10.8 us -> 21.2 us  [the longest x1 13.4 us: body(): lax.all_to_all(adapter_update, 'ad', split_axis=0, concat_axis=0, tiled=T...]
    all_to_all x1 -> x3, starting transfers between devices: 4.47 us -> 13.8 us  [the longest x1 5.96 us: body(): lax.all_to_all(adapter_update, 'ad', split_axis=0, concat_axis=0, tiled=T...]
    ppermute x0 -> x3, starting transfers between devices: none -> 8.68 us  [body(): lax.ppermute(give, 'tp', [(k, k ^ bit) for k in range(tp_size)])]
    all_to_all x1, waiting for transfers between devices: 60.4 us -> 54 us  [body(): lax.all_to_all(send_rows, 'ad', split_axis=0, concat_axis=0, tiled=True)]
  transfers between devices with their start and end apart: 2 -> 7, of which waited for: 2 -> 4; matrix products, arithmetic and copies ran while one was open for 2% -> 8% of each run, Pallas kernels for 0% -> 0%
where the time goes in v12:
time: 135 us; the launch traced here: 134 us
  waiting for transfers between devices  75.1 us (56%)
  starting transfers between devices  41.3 us (31%)
  matrix products  7.31 us (5%)
  local copies, waits for them, and re-layouts  7 us (5%)
  other arithmetic  3.07 us (2%)
    all_to_all x1, waiting for transfers between devices, body(): lax.all_to_all(send_rows, 'ad', split_axis=0, concat_axis=0, tiled=True)  54 us
    all_to_all x1, starting transfers between devices, body(): lax.all_to_all(send_rows, 'ad', split_axis=0, concat_axis=0, tiled=True)  18.8 us
    all_to_all x1, waiting for transfers between devices, body(): lax.all_to_all(adapter_update, 'ad', split_axis=0, concat_axis=0, tiled=T...  13.4 us
    ppermute x3, starting transfers between devices, body(): lax.ppermute(give, 'tp', [(k, k ^ bit) for k in range(tp_size)])  8.68 us
    all_to_all x1, waiting for transfers between devices, body(): lax.all_to_all(chunks, 'tp', split_axis=0, concat_axis=0, tiled=True)  6.04 us
    all_to_all x1, starting transfers between devices, body(): lax.all_to_all(adapter_update, 'ad', split_axis=0, concat_axis=0, tiled=T...  5.96 us
    all_to_all x1, starting transfers between devices, body(): lax.all_to_all(chunks, 'tp', split_axis=0, concat_axis=0, tiled=True)  4.47 us
    all_to_all x1, starting transfers between devices, body(): lax.all_to_all(spread, 'tp', split_axis=0, concat_axis=0, tiled=True)  3.35 us
  transfers between devices with their start and end apart: 7, of which 4 were waited for; matrix products, arithmetic and copies ran while one was open for 8% of the time, Pallas kernels for 0%

profile of v12, /device:TPU:2, one launch (start us, length us, event | category | flops | bytes accessed | tf_op | source)
XLA Modules:
  0.0 134.1 jit_solution(1025380687045668010)
XLA Ops:
  0.0 0.0 copy-start
  0.0 0.8 fusion.19
  0.8 0.1 fusion.16
  0.9 0.1 reduce_window_sum.11
  1.0 0.2 select_reduce_fusion
  1.2 0.1 add_add_fusion
  1.3 0.1 eq.57
  1.3 0.1 broadcast_in_dim.6
  1.4 0.1 broadcast_in_dim.7
  1.5 2.6 %fusion = bf16[64,8,1152]{2,1,0:T(8,128)(2,1)} fusion(bf16[192,128]{1,0:T(8,128)(2,1)S(1)} %broadcast_in_dim.7, bf16[192,1024]{1,0:T(8,128)(2,1)} %bitcast.61, s32[192]{0:T(256)S(1)} %eq.57), kind=kOutput, calls=%fused_computation.1 | convolution fusion | flops 228065280 | bytes 1622784 | tf_op jit(solution)/shard_map/dot_general | solution.py:52
  4.1 18.8 %all-to-all-start = ((bf16[64,8,1152]{2,1,0:T(8,128)(2,1)}), bf16[64,8,1152]{2,1,0:T(8,128)(2,1)}, u32[]{:S(2)}, u32[]{:S(2)}) async-start(bf16[64,8,1152]{2,1,0:T(8,128)(2,1)} %fusion), calls=%async_computation | async-start | bytes 2359296 | tf_op jit(solution)/shard_map/all_to_all | solution.py:54
  22.9 2.9 %copy.14 = bf16[1024,1024]{1,0:T(8,128)(2,1)S(1)} copy(bf16[1024,1024]{0,1:T(8,128)(2,1)} %bitcast.60) | data formatting | bytes 4194304 | tf_op jit(solution)/shard_map/dot_general | solution.py:20
  25.8 1.8 %fusion.22 = f32[192,8,128]{2,0,1:T(8,128)S(1)} fusion(bf16[192,1024,1]{1,0,2:T(8,128)(2,1)} %bitcast.62, bf16[8,128,1024]{2,1,0:T(8,128)(2,1)S(1)} %bitcast.57), kind=kOutput, calls=%fused_computation.49 | convolution fusion | flops 402653184 | bytes 3276800 | tf_op jit(solution)/shard_map/dot_general | solution.py:20
  27.7 1.9 %collective-permute-start = (f32[4,192,128]{2,1,0:T(8,128)S(1)}, f32[4,192,128]{2,1,0:T(8,128)S(1)}, u32[]{:S(2)}, u32[]{:S(2)}) collective-permute-start(f32[4,192,128]{2,1,0:T(8,128)S(1)} %dynamic-slice_bitcast_fusion), channel_id=1, source_target_pairs={{0,1},{1,0},{2,3},{3,2},{4,5},{5,4},{6,7},{7,6},{8,9},{9,8},{10,11... | collective-permute-start | bytes 1179656 | tf_op jit(solution)/shard_map/ppermute | solution.py:32
  29.7 54.0 %all-to-all-done = bf16[64,8,1152]{2,1,0:T(8,128)(2,1)} async-done(((bf16[64,8,1152]{2,1,0:T(8,128)(2,1)}), bf16[64,8,1152]{2,1,0:T(8,128)(2,1)}, u32[]{:S(2)}, u32[]{:S(2)}) %all-to-all-start) | async-done | bytes 1179680 | tf_op jit(solution)/shard_map/all_to_all | solution.py:54
  83.6 1.0 slice_reduce_fusion
  84.7 0.1 fusion.17
  84.7 0.0 copy-done
  84.7 1.7 %fusion.3 = f32[512,256]{0,1:S(1)} fusion(bf16[1024,256]{0,1:T(8,128)(2,1)S(1)} %bitcast.56, bf16[512,1152]{1,0:T(8,128)(2,1)} %bitcast.14), kind=kOutput, calls=%fused_computation.5 | convolution fusion | flops 268435456 | bytes 2097152
  86.4 0.1 multiply_reduce_fusion
  86.5 0.1 reshape.126
  86.6 0.1 copy.16
  86.7 0.0 copy-start.1
  86.7 0.8 reshape.135
  87.5 4.5 %all-to-all-start.1 = ((f32[8,1,4096]{2,1,0:T(1,128)}), f32[8,1,4096]{2,1,0:T(1,128)S(1)}, u32[]{:S(2)}, u32[]{:S(2)}) async-start(f32[8,1,4096]{2,1,0:T(1,128)} %reshape.135), calls=%async_computation.1 | async-start | bytes 262144 | tf_op jit(solution)/shard_map/all_to_all | solution.py:68
  92.0 0.0 collective-permute-done
  92.0 6.0 %all-to-all-done.1 = f32[8,1,4096]{2,1,0:T(1,128)S(1)} async-done(((f32[8,1,4096]{2,1,0:T(1,128)}), f32[8,1,4096]{2,1,0:T(1,128)S(1)}, u32[]{:S(2)}, u32[]{:S(2)}) %all-to-all-start.1) | async-done | bytes 131104 | tf_op jit(solution)/shard_map/all_to_all | solution.py:68
  98.1 0.5 broadcast.97
  98.6 1.0 reduce.2
  99.5 0.1 reshape.136
  99.7 0.8 reshape.137
  100.5 3.3 %all-to-all-start.2 = ((bf16[8,2,2048]{2,1,0:T(2,128)(2,1)}), bf16[8,2,2048]{2,1,0:T(2,128)(2,1)S(1)}, u32[]{:S(2)}, u32[]{:S(2)}) async-start(bf16[8,2,2048]{2,1,0:T(2,128)(2,1)} %reshape.137), calls=%async_computation.2 | async-start | bytes 131072 | tf_op jit(solution)/shard_map/all_to_all | solution.py:70
  103.9 3.8 %collective-permute-start.1 = (f32[2,192,128]{2,1,0:T(8,128)S(1)}, f32[2,192,128]{2,1,0:T(8,128)S(1)}, u32[]{:S(2)}, u32[]{:S(2)}) collective-permute-start(f32[2,192,128]{2,1,0:T(8,128)S(1)} %dynamic-slice_bitcast_fusion.1), channel_id=1, source_target_pairs={{0,2},{1,3},{2,0},{3,1},{4,6},{5,7},{6,4},{7,5},{8,10},{9,11},{10,... | collective-permute-start | bytes 589832 | tf_op jit(solution)/shard_map/ppermute | solution.py:32
  107.7 1.7 %all-to-all-done.2 = bf16[8,2,2048]{2,1,0:T(2,128)(2,1)S(1)} async-done(((bf16[8,2,2048]{2,1,0:T(2,128)(2,1)}), bf16[8,2,2048]{2,1,0:T(2,128)(2,1)S(1)}, u32[]{:S(2)}, u32[]{:S(2)}) %all-to-all-start.2) | async-done | bytes 65568 | tf_op jit(solution)/shard_map/all_to_all | solution.py:70
  109.4 0.1 reshape.138
  109.5 0.1 copy.13
  109.6 0.1 convert_element_type.57
  109.8 0.0 copy-done.1
  109.8 0.9 fusion.2
  110.7 6.0 %all-to-all-start.3 = ((bf16[64,8,128]{2,1,0:T(8,128)(2,1)}), bf16[64,8,128]{2,1,0:T(8,128)(2,1)S(1)}, u32[]{:S(2)}, u32[]{:S(2)}) async-start(bf16[64,8,128]{2,1,0:T(8,128)(2,1)} %fusion.2), calls=%async_computation.3 | async-start | bytes 262144 | tf_op jit(solution)/shard_map/all_to_all | solution.py:82
  116.7 0.0 collective-permute-done.1
  116.8 2.9 %collective-permute-start.2 = (f32[1,192,128]{2,1,0:T(8,128)S(1)}, f32[1,192,128]{2,1,0:T(8,128)S(1)}, u32[]{:S(2)}, u32[]{:S(2)}) collective-permute-start(f32[1,192,128]{2,1,0:T(8,128)S(1)} %constant_dynamic-slice_fusion), channel_id=1, source_target_pairs={{0,4},{1,5},{2,6},{3,7},{4,0},{5,1},{6,2},{7,3},{8,12},{9,13},{10,... | collective-permute-start | bytes 294920 | tf_op jit(solution)/shard_map/ppermute | solution.py:32
  119.7 13.4 %all-to-all-done.3 = bf16[64,8,128]{2,1,0:T(8,128)(2,1)S(1)} async-done(((bf16[64,8,128]{2,1,0:T(8,128)(2,1)}), bf16[64,8,128]{2,1,0:T(8,128)(2,1)S(1)}, u32[]{:S(2)}, u32[]{:S(2)}) %all-to-all-start.3) | async-done | bytes 131104 | tf_op jit(solution)/shard_map/all_to_all | solution.py:82
  133.2 0.3 fusion.5
  133.5 0.0 collective-permute-done.2
  133.5 0.6 fusion.15
  (9 shorter events, 0.2 us)
Async XLA Ops:
  0.0 84.7 %copy-start = (bf16[4,1024,64]{1,2,0:T(8,128)(2,1)S(1)}, bf16[4,1024,64]{1,2,0:T(8,128)(2,1)}, u32[]{:S(2)}) copy-start(bf16[4,1024,64]{1,2,0:T(8,128)(2,1)} %param.8) | copy-start | bytes 1572868
  4.1 79.5 %all-to-all-start = ((bf16[64,8,1152]{2,1,0:T(8,128)(2,1)}), bf16[64,8,1152]{2,1,0:T(8,128)(2,1)}, u32[]{:S(2)}, u32[]{:S(2)}) async-start(bf16[64,8,1152]{2,1,0:T(8,128)(2,1)} %fusion), calls=%async_computation | async-start | bytes 2359296 | tf_op jit(solution)/shard_map/all_to_all | solution.py:54
  27.7 64.3 %collective-permute-start = (f32[4,192,128]{2,1,0:T(8,128)S(1)}, f32[4,192,128]{2,1,0:T(8,128)S(1)}, u32[]{:S(2)}, u32[]{:S(2)}) collective-permute-start(f32[4,192,128]{2,1,0:T(8,128)S(1)} %dynamic-slice_bitcast_fusion), channel_id=1, source_target_pairs={{0,1},{1,0},{2,3},{3,2},{4,5},{5,4},{6,7},{7,6},{8,9},{9,8},{10,11... | collective-permute-start | bytes 1179656 | tf_op jit(solution)/shard_map/ppermute | solution.py:32
  86.7 23.1 %copy-start.1 = (bf16[4,64,128]{2,1,0:T(8,128)(2,1)S(1)}, bf16[4,64,128]{2,1,0:T(8,128)(2,1)}, u32[]{:S(2)}) copy-start(bf16[4,64,128]{2,1,0:T(8,128)(2,1)} %param.9) | copy-start | bytes 196612
  87.5 10.6 %all-to-all-start.1 = ((f32[8,1,4096]{2,1,0:T(1,128)}), f32[8,1,4096]{2,1,0:T(1,128)S(1)}, u32[]{:S(2)}, u32[]{:S(2)}) async-start(f32[8,1,4096]{2,1,0:T(1,128)} %reshape.135), calls=%async_computation.1 | async-start | bytes 262144 | tf_op jit(solution)/shard_map/all_to_all | solution.py:68
  100.5 8.9 %all-to-all-start.2 = ((bf16[8,2,2048]{2,1,0:T(2,128)(2,1)}), bf16[8,2,2048]{2,1,0:T(2,128)(2,1)S(1)}, u32[]{:S(2)}, u32[]{:S(2)}) async-start(bf16[8,2,2048]{2,1,0:T(2,128)(2,1)} %reshape.137), calls=%async_computation.2 | async-start | bytes 131072 | tf_op jit(solution)/shard_map/all_to_all | solution.py:70
  103.9 12.8 %collective-permute-start.1 = (f32[2,192,128]{2,1,0:T(8,128)S(1)}, f32[2,192,128]{2,1,0:T(8,128)S(1)}, u32[]{:S(2)}, u32[]{:S(2)}) collective-permute-start(f32[2,192,128]{2,1,0:T(8,128)S(1)} %dynamic-slice_bitcast_fusion.1), channel_id=1, source_target_pairs={{0,2},{1,3},{2,0},{3,1},{4,6},{5,7},{6,4},{7,5},{8,10},{9,11},{10,... | collective-permute-start | bytes 589832 | tf_op jit(solution)/shard_map/ppermute | solution.py:32
  110.7 22.5 %all-to-all-start.3 = ((bf16[64,8,128]{2,1,0:T(8,128)(2,1)}), bf16[64,8,128]{2,1,0:T(8,128)(2,1)S(1)}, u32[]{:S(2)}, u32[]{:S(2)}) async-start(bf16[64,8,128]{2,1,0:T(8,128)(2,1)} %fusion.2), calls=%async_computation.3 | async-start | bytes 262144 | tf_op jit(solution)/shard_map/all_to_all | solution.py:82
  116.8 16.7 %collective-permute-start.2 = (f32[1,192,128]{2,1,0:T(8,128)S(1)}, f32[1,192,128]{2,1,0:T(8,128)S(1)}, u32[]{:S(2)}, u32[]{:S(2)}) collective-permute-start(f32[1,192,128]{2,1,0:T(8,128)S(1)} %constant_dynamic-slice_fusion), channel_id=1, source_target_pairs={{0,4},{1,5},{2,6},{3,7},{4,0},{5,1},{6,2},{7,3},{8,12},{9,13},{10,... | collective-permute-start | bytes 294920 | tf_op jit(solution)/shard_map/ppermute | solution.py:32

commit v13 on v12

--- a/solution.py
+++ b/solution.py
@@ -52,6 +52,7 @@
     send_rows = jnp.dot(dispatch, rows_tagged, preferred_element_type=jnp.float32).astype(jnp.bfloat16)
     send_rows = send_rows.reshape(groups, slots_per_group, width_per_shard + TAG_WIDTH)
     incoming = lax.all_to_all(send_rows, "ad", split_axis=0, concat_axis=0, tiled=True)
+    incoming, base_keys_output = lax.optimization_barrier((incoming, base_keys_output))
     incoming = incoming.reshape(slot_total, width_per_shard + TAG_WIDTH)
     incoming_rows = incoming[:, :width_per_shard]
     incoming_labels = incoming[:, width_per_shard]

time: 135 us -> 132 us (0.978)
  blocking collectives: 0 us -> 40.6 us
  waiting for transfers between devices: 75.1 us -> 45.2 us
  starting transfers between devices: 41.3 us -> 29.3 us
    all_to_all x0 -> x3, blocking collectives: none -> 40.6 us  [the longest x1 22.2 us: body(): lax.all_to_all(adapter_update, 'ad', split_axis=0, concat_axis=0, tiled=T...]
    all_to_all x3 -> x0, waiting for transfers between devices: 21.2 us -> none  [the longest x1 13.4 us: body(): lax.all_to_all(adapter_update, 'ad', split_axis=0, concat_axis=0, tiled=T...]
    all_to_all x1, waiting for transfers between devices: 54 us -> 35.3 us  [body(): lax.all_to_all(send_rows, 'ad', split_axis=0, concat_axis=0, tiled=True)]
    all_to_all x3 -> x0, starting transfers between devices: 13.8 us -> none  [the longest x1 5.96 us: body(): lax.all_to_all(adapter_update, 'ad', split_axis=0, concat_axis=0, tiled=T...]
    ppermute x3, waiting for transfers between devices: 0.01 us -> 9.83 us  [body(): lax.ppermute(give, 'tp', [(k, k ^ bit) for k in range(tp_size)])]
    ppermute x3, starting transfers between devices: 8.68 us -> 10.5 us  [body(): lax.ppermute(give, 'tp', [(k, k ^ bit) for k in range(tp_size)])]
  transfers between devices with their start and end apart: 7 -> 4, of which waited for: 4 -> 4; matrix products, arithmetic and copies ran while one was open for 8% -> 4% of each run, Pallas kernels for 0% -> 0%
where the time goes in v13:
time: 132 us; the launch traced here: 131 us
  waiting for transfers between devices  45.2 us (34%)
  blocking collectives  40.6 us (31%)
  starting transfers between devices  29.3 us (22%)
  matrix products  6.68 us (5%)
  local copies, waits for them, and re-layouts  5.74 us (4%)
  other arithmetic  3.07 us (2%)
    all_to_all x1, waiting for transfers between devices, body(): lax.all_to_all(send_rows, 'ad', split_axis=0, concat_axis=0, tiled=True)  35.3 us
    all_to_all x1, blocking collectives, body(): lax.all_to_all(adapter_update, 'ad', split_axis=0, concat_axis=0, tiled=T...  22.2 us
    all_to_all x1, starting transfers between devices, body(): lax.all_to_all(send_rows, 'ad', split_axis=0, concat_axis=0, tiled=True)  18.8 us
    ppermute x3, starting transfers between devices, body(): lax.ppermute(give, 'tp', [(k, k ^ bit) for k in range(tp_size)])  10.5 us
    all_to_all x1, blocking collectives, body(): lax.all_to_all(chunks, 'tp', split_axis=0, concat_axis=0, tiled=True)  10.4 us
    ppermute x3, waiting for transfers between devices, body(): lax.ppermute(give, 'tp', [(k, k ^ bit) for k in range(tp_size)])  9.83 us
    all_to_all x1, blocking collectives, body(): lax.all_to_all(spread, 'tp', split_axis=0, concat_axis=0, tiled=True)  8 us
    dot_general x1, local copies, waits for them, and re-layouts, body(): jnp.dot(gathered_rows, key_base_weight, preferred_element_type=jnp.float32)  2.86 us
  transfers between devices with their start and end apart: 4, of which 4 were waited for; matrix products, arithmetic and copies ran while one was open for 4% of the time, Pallas kernels for 0%

profile of v13, /device:TPU:2, one launch (start us, length us, event | category | flops | bytes accessed | tf_op | source)
XLA Modules:
  0.0 130.9 jit_solution(11738890557309041496)
XLA Ops:
  0.0 0.0 copy-start
  0.0 0.8 add_select_fusion.1
  0.8 0.1 fusion.15
  0.9 0.1 reduce_window_sum.11
  1.0 0.2 select_reduce_fusion
  1.2 0.1 add_add_fusion
  1.3 0.1 eq.57
  1.3 0.1 broadcast_in_dim.6
  1.4 0.1 broadcast_in_dim.7
  1.5 2.6 %fusion = bf16[64,8,1152]{2,1,0:T(8,128)(2,1)} fusion(bf16[192,128]{1,0:T(8,128)(2,1)S(1)} %broadcast_in_dim.7, bf16[192,1024]{1,0:T(8,128)(2,1)} %bitcast.59, s32[192]{0:T(256)S(1)} %eq.57), kind=kOutput, calls=%fused_computation.1 | convolution fusion | flops 228065280 | bytes 1622784 | tf_op jit(solution)/shard_map/dot_general | solution.py:52
  4.1 18.8 %all-to-all-start = ((bf16[64,8,1152]{2,1,0:T(8,128)(2,1)}), bf16[64,8,1152]{2,1,0:T(8,128)(2,1)}, u32[]{:S(2)}, u32[]{:S(2)}) async-start(bf16[64,8,1152]{2,1,0:T(8,128)(2,1)} %fusion), calls=%async_computation | async-start | bytes 2359296 | tf_op jit(solution)/shard_map/all_to_all | solution.py:54
  22.9 2.9 %copy.14 = bf16[1024,1024]{1,0:T(8,128)(2,1)S(1)} copy(bf16[1024,1024]{0,1:T(8,128)(2,1)} %bitcast.58) | data formatting | bytes 4194304 | tf_op jit(solution)/shard_map/dot_general | solution.py:20
  25.8 1.8 %fusion.21 = f32[192,8,128]{2,0,1:T(8,128)S(1)} fusion(bf16[192,1024,1]{1,0,2:T(8,128)(2,1)} %bitcast.60, bf16[8,128,1024]{2,1,0:T(8,128)(2,1)S(1)} %bitcast.55), kind=kOutput, calls=%fused_computation.49 | convolution fusion | flops 402653184 | bytes 3276800 | tf_op jit(solution)/shard_map/dot_general | solution.py:20
  27.7 1.9 %collective-permute-start = (f32[4,192,128]{2,1,0:T(8,128)S(1)}, f32[4,192,128]{2,1,0:T(8,128)S(1)}, u32[]{:S(2)}, u32[]{:S(2)}) collective-permute-start(f32[4,192,128]{2,1,0:T(8,128)S(1)} %dynamic-slice_bitcast_fusion), channel_id=1, source_target_pairs={{0,1},{1,0},{2,3},{3,2},{4,5},{5,4},{6,7},{7,6},{8,9},{9,8},{10,11... | collective-permute-start | bytes 1179656 | tf_op jit(solution)/shard_map/ppermute | solution.py:32
  29.7 1.6 %collective-permute-done = f32[4,192,128]{2,1,0:T(8,128)S(1)} collective-permute-done((f32[4,192,128]{2,1,0:T(8,128)S(1)}, f32[4,192,128]{2,1,0:T(8,128)S(1)}, u32[]{:S(2)}, u32[]{:S(2)}) %collective-permute-start) | collective-permute-done | bytes 393248 | tf_op jit(solution)/shard_map/ppermute | solution.py:32
  31.4 3.5 %collective-permute-start.1 = (f32[2,192,128]{2,1,0:T(8,128)S(1)}, f32[2,192,128]{2,1,0:T(8,128)S(1)}, u32[]{:S(2)}, u32[]{:S(2)}) collective-permute-start(f32[2,192,128]{2,1,0:T(8,128)S(1)} %dynamic-slice_bitcast_fusion.1), channel_id=1, source_target_pairs={{0,2},{1,3},{2,0},{3,1},{4,6},{5,7},{6,4},{7,5},{8,10},{9,11},{10,... | collective-permute-start | bytes 589832 | tf_op jit(solution)/shard_map/ppermute | solution.py:32
  34.9 5.3 %collective-permute-done.1 = f32[2,192,128]{2,1,0:T(8,128)S(1)} collective-permute-done((f32[2,192,128]{2,1,0:T(8,128)S(1)}, f32[2,192,128]{2,1,0:T(8,128)S(1)}, u32[]{:S(2)}, u32[]{:S(2)}) %collective-permute-start.1) | collective-permute-done | bytes 196640 | tf_op jit(solution)/shard_map/ppermute | solution.py:32
  40.3 5.1 %collective-permute-start.2 = (f32[1,192,128]{2,1,0:T(8,128)S(1)}, f32[1,192,128]{2,1,0:T(8,128)S(1)}, u32[]{:S(2)}, u32[]{:S(2)}) collective-permute-start(f32[1,192,128]{2,1,0:T(8,128)S(1)} %constant_dynamic-slice_fusion), channel_id=1, source_target_pairs={{0,4},{1,5},{2,6},{3,7},{4,0},{5,1},{6,2},{7,3},{8,12},{9,13},{10,... | collective-permute-start | bytes 294920 | tf_op jit(solution)/shard_map/ppermute | solution.py:32
  45.4 2.9 %collective-permute-done.2 = f32[1,192,128]{2,1,0:T(8,128)S(1)} collective-permute-done((f32[1,192,128]{2,1,0:T(8,128)S(1)}, f32[1,192,128]{2,1,0:T(8,128)S(1)}, u32[]{:S(2)}, u32[]{:S(2)}) %collective-permute-start.2) | collective-permute-done | bytes 98336 | tf_op jit(solution)/shard_map/ppermute | solution.py:32
  48.3 35.3 %all-to-all-done = bf16[64,8,1152]{2,1,0:T(8,128)(2,1)} async-done(((bf16[64,8,1152]{2,1,0:T(8,128)(2,1)}), bf16[64,8,1152]{2,1,0:T(8,128)(2,1)}, u32[]{:S(2)}, u32[]{:S(2)}) %all-to-all-start) | async-done | bytes 1179680 | tf_op jit(solution)/shard_map/all_to_all | solution.py:54
  83.6 1.0 slice_reduce_fusion
  84.7 0.0 copy-done
  84.7 1.7 %fusion.3 = f32[512,256]{0,1:S(1)} fusion(bf16[1024,256]{0,1:T(8,128)(2,1)S(1)} %bitcast.54, bf16[512,1152]{1,0:T(8,128)(2,1)} %bitcast.14), kind=kOutput, calls=%fused_computation.5 | convolution fusion | flops 268435456 | bytes 2097152
  86.4 0.1 fusion.16
  86.5 0.0 copy-start.1
  86.5 0.1 multiply_reduce_fusion
  86.5 0.1 reshape.126
  86.6 0.1 copy.16
  86.7 0.2 reshape.135
  86.9 10.4 %all_to_all.20 = f32[8,1,4096]{2,1,0:T(1,128)S(1)} all-to-all(f32[8,1,4096]{2,1,0:T(1,128)S(1)} %reshape.135), channel_id=1, replica_groups=mesh['ad'=64,'tp'=8] {'tp'}, dimensions={0} | all-to-all | bytes 262144 | tf_op jit(solution)/shard_map/all_to_all | solution.py:69
  97.2 0.5 broadcast.97
  97.7 1.0 reduce.2
  98.7 0.1 reshape.136
  98.9 0.2 reshape.137
  99.0 8.0 %all_to_all.21 = bf16[8,2,2048]{2,1,0:T(2,128)(2,1)S(1)} all-to-all(bf16[8,2,2048]{2,1,0:T(2,128)(2,1)S(1)} %reshape.137), channel_id=1, replica_groups=mesh['ad'=64,'tp'=8] {'tp'}, dimensions={0} | all-to-all | bytes 131072 | tf_op jit(solution)/shard_map/all_to_all | solution.py:71
  107.0 0.1 reshape.138
  107.2 0.1 copy.13
  107.3 0.1 convert_element_type.57
  107.4 0.0 copy-done.1
  107.4 0.3 fusion.2
  107.7 22.2 %all_to_all.22 = bf16[64,8,128]{2,1,0:T(8,128)(2,1)S(1)} all-to-all(bf16[64,8,128]{2,1,0:T(8,128)(2,1)S(1)} %fusion.2), channel_id=1, replica_groups=mesh['ad'=64,'tp'=8] {'ad'}, dimensions={0} | all-to-all | bytes 262144 | tf_op jit(solution)/shard_map/all_to_all | solution.py:83
  129.9 0.3 fusion.5
  130.3 0.6 add_convert_fusion
  (10 shorter events, 0.2 us)
Async XLA Ops:
  0.0 84.7 %copy-start = (bf16[4,1024,64]{1,2,0:T(8,128)(2,1)S(1)}, bf16[4,1024,64]{1,2,0:T(8,128)(2,1)}, u32[]{:S(2)}) copy-start(bf16[4,1024,64]{1,2,0:T(8,128)(2,1)} %param.8) | copy-start | bytes 1572868
  4.1 79.5 %all-to-all-start = ((bf16[64,8,1152]{2,1,0:T(8,128)(2,1)}), bf16[64,8,1152]{2,1,0:T(8,128)(2,1)}, u32[]{:S(2)}, u32[]{:S(2)}) async-start(bf16[64,8,1152]{2,1,0:T(8,128)(2,1)} %fusion), calls=%async_computation | async-start | bytes 2359296 | tf_op jit(solution)/shard_map/all_to_all | solution.py:54
  27.7 3.6 %collective-permute-start = (f32[4,192,128]{2,1,0:T(8,128)S(1)}, f32[4,192,128]{2,1,0:T(8,128)S(1)}, u32[]{:S(2)}, u32[]{:S(2)}) collective-permute-start(f32[4,192,128]{2,1,0:T(8,128)S(1)} %dynamic-slice_bitcast_fusion), channel_id=1, source_target_pairs={{0,1},{1,0},{2,3},{3,2},{4,5},{5,4},{6,7},{7,6},{8,9},{9,8},{10,11... | collective-permute-start | bytes 1179656 | tf_op jit(solution)/shard_map/ppermute | solution.py:32
  31.4 8.8 %collective-permute-start.1 = (f32[2,192,128]{2,1,0:T(8,128)S(1)}, f32[2,192,128]{2,1,0:T(8,128)S(1)}, u32[]{:S(2)}, u32[]{:S(2)}) collective-permute-start(f32[2,192,128]{2,1,0:T(8,128)S(1)} %dynamic-slice_bitcast_fusion.1), channel_id=1, source_target_pairs={{0,2},{1,3},{2,0},{3,1},{4,6},{5,7},{6,4},{7,5},{8,10},{9,11},{10,... | collective-permute-start | bytes 589832 | tf_op jit(solution)/shard_map/ppermute | solution.py:32
  40.3 8.0 %collective-permute-start.2 = (f32[1,192,128]{2,1,0:T(8,128)S(1)}, f32[1,192,128]{2,1,0:T(8,128)S(1)}, u32[]{:S(2)}, u32[]{:S(2)}) collective-permute-start(f32[1,192,128]{2,1,0:T(8,128)S(1)} %constant_dynamic-slice_fusion), channel_id=1, source_target_pairs={{0,4},{1,5},{2,6},{3,7},{4,0},{5,1},{6,2},{7,3},{8,12},{9,13},{10,... | collective-permute-start | bytes 294920 | tf_op jit(solution)/shard_map/ppermute | solution.py:32
  86.5 21.0 %copy-start.1 = (bf16[4,64,128]{2,1,0:T(8,128)(2,1)S(1)}, bf16[4,64,128]{2,1,0:T(8,128)(2,1)}, u32[]{:S(2)}) copy-start(bf16[4,64,128]{2,1,0:T(8,128)(2,1)} %param.9) | copy-start | bytes 196612

commit v14 on v13

--- a/solution.py
+++ b/solution.py
@@ -49,7 +49,13 @@
     tag_values = (local_index + 1).astype(jnp.bfloat16).reshape(row_total, 1)
     tag_block = jnp.broadcast_to(tag_values, (row_total, TAG_WIDTH))
     rows_tagged = jnp.concatenate([gathered_rows, tag_block], axis=1)
-    send_rows = jnp.dot(dispatch, rows_tagged, preferred_element_type=jnp.float32).astype(jnp.bfloat16)
+    row_of_slot = jnp.sum(
+        (slot_index[None, :] == jnp.arange(slot_total, dtype=jnp.int32)[:, None]).astype(jnp.int32)
+        * (jnp.arange(row_total, dtype=jnp.int32)[None, :] - row_total),
+        axis=1,
+    ) + row_total
+    rows_padded = jnp.concatenate([rows_tagged, jnp.zeros((1, rows_tagged.shape[1]), rows_tagged.dtype)])
+    send_rows = jnp.take(rows_padded, row_of_slot, axis=0, mode="clip")
     send_rows = send_rows.reshape(groups, slots_per_group, width_per_shard + TAG_WIDTH)
     incoming = lax.all_to_all(send_rows, "ad", split_axis=0, concat_axis=0, tiled=True)
     incoming, base_keys_output = lax.optimization_barrier((incoming, base_keys_output))
@@ -64,7 +70,6 @@
     selector = (incoming_labels[:, None] == labels[None, :]).astype(jnp.float32)
     down_part = jnp.sum(down_all * selector[:, :, None], axis=1)
     shards = lax.axis_size("tp")
-    chunk_width = slot_total // shards * rank
     chunks = down_part.reshape(shards, slot_total // shards, rank)
     chunk_sum = jnp.sum(lax.all_to_all(chunks, "tp", split_axis=0, concat_axis=0, tiled=True), axis=0)
     spread = jnp.broadcast_to(chunk_sum[None], (shards,) + chunk_sum.shape)

time: 132 us -> 133 us (level)
  local copies, waits for them, and re-layouts: 5.74 us -> 8.58 us
  matrix products: 6.68 us -> 4.07 us
    gather x0 -> x1, local copies, waits for them, and re-layouts: none -> 2.85 us  [body(): send_rows = jnp.take(rows_padded, row_of_slot, axis=0, mode='clip')]
    dot_general x1 -> x0, matrix products: 2.56 us -> none  [body(): jnp.dot(dispatch, rows_tagged, preferred_element_type=jnp.float32)]
where the time goes in v14:
time: 133 us; the launch traced here: 132 us
  waiting for transfers between devices  45.2 us (34%)
  blocking collectives  40.8 us (31%)
  starting transfers between devices  29.3 us (22%)
  local copies, waits for them, and re-layouts  8.58 us (6%)
  other arithmetic  4.27 us (3%)
  matrix products  4.07 us (3%)
    all_to_all x1, waiting for transfers between devices, body(): lax.all_to_all(send_rows, 'ad', split_axis=0, concat_axis=0, tiled=True)  35.3 us
    all_to_all x1, blocking collectives, body(): lax.all_to_all(adapter_update, 'ad', split_axis=0, concat_axis=0, tiled=T...  22.3 us
    all_to_all x1, starting transfers between devices, body(): lax.all_to_all(send_rows, 'ad', split_axis=0, concat_axis=0, tiled=True)  18.8 us
    ppermute x3, starting transfers between devices, body(): lax.ppermute(give, 'tp', [(k, k ^ bit) for k in range(tp_size)])  10.5 us
    all_to_all x1, blocking collectives, body(): lax.all_to_all(chunks, 'tp', split_axis=0, concat_axis=0, tiled=True)  10.5 us
    ppermute x3, waiting for transfers between devices, body(): lax.ppermute(give, 'tp', [(k, k ^ bit) for k in range(tp_size)])  9.83 us
    all_to_all x1, blocking collectives, body(): lax.all_to_all(spread, 'tp', split_axis=0, concat_axis=0, tiled=True)  8 us
    dot_general x1, local copies, waits for them, and re-layouts, body(): jnp.dot(gathered_rows, key_base_weight, preferred_element_type=jnp.float32)  2.86 us
  transfers between devices with their start and end apart: 4, of which 4 were waited for; matrix products, arithmetic and copies ran while one was open for 4% of the time, Pallas kernels for 0%

profile of v14, /device:TPU:2, one launch (start us, length us, event | category | flops | bytes accessed | tf_op | source)
XLA Modules:
  0.0 132.5 jit_solution(4442862389739648651)
XLA Ops:
  0.0 0.0 copy-start
  0.0 0.8 add_select_fusion
  0.8 0.1 fusion.13
  0.9 0.1 reduce_window_sum.11
  1.0 0.2 select_reduce_fusion.1
  1.2 0.1 add_add_fusion
  1.3 0.1 eq.64
  1.3 0.1 select_reduce_fusion
  1.5 0.1 broadcast_in_dim.7
  1.6 0.1 broadcast_in_dim.8
  1.7 1.0 fusion.6
  2.7 2.9 %gather_fusion = bf16[512,1152]{1,0:T(8,128)(2,1)} fusion(bf16[193,1152]{1,0:T(8,128)(2,1)S(1)} %fusion.6, s32[1024]{0:T(1024)S(1)} %pad_clamp_fusion), kind=kCustom, calls=%fused_computation | custom fusion | bytes 2361344 | tf_op jit(solution)/shard_map/jit(_take)/gather | solution.py:58
  5.6 18.8 %all-to-all-start = ((bf16[64,8,1152]{2,1,0:T(8,128)(2,1)}), bf16[64,8,1152]{2,1,0:T(8,128)(2,1)}, u32[]{:S(2)}, u32[]{:S(2)}) async-start(bf16[64,8,1152]{2,1,0:T(8,128)(2,1)} %bitcast.1), calls=%async_computation | async-start | bytes 2359296 | tf_op jit(solution)/shard_map/all_to_all | solution.py:60
  24.4 2.9 %copy.17 = bf16[1024,1024]{1,0:T(8,128)(2,1)S(1)} copy(bf16[1024,1024]{0,1:T(8,128)(2,1)} %bitcast.57) | data formatting | bytes 4194304 | tf_op jit(solution)/shard_map/dot_general | solution.py:20
  27.3 1.8 %fusion.18 = f32[192,8,128]{2,0,1:T(8,128)S(1)} fusion(bf16[192,1024,1]{1,0,2:T(8,128)(2,1)} %bitcast.59, bf16[8,128,1024]{2,1,0:T(8,128)(2,1)S(1)} %bitcast.54), kind=kOutput, calls=%fused_computation.51 | convolution fusion | flops 402653184 | bytes 3276800 | tf_op jit(solution)/shard_map/dot_general | solution.py:20
  29.2 1.9 %collective-permute-start = (f32[4,192,128]{2,1,0:T(8,128)S(1)}, f32[4,192,128]{2,1,0:T(8,128)S(1)}, u32[]{:S(2)}, u32[]{:S(2)}) collective-permute-start(f32[4,192,128]{2,1,0:T(8,128)S(1)} %dynamic-slice_bitcast_fusion), channel_id=1, source_target_pairs={{0,1},{1,0},{2,3},{3,2},{4,5},{5,4},{6,7},{7,6},{8,9},{9,8},{10,11... | collective-permute-start | bytes 1179656 | tf_op jit(solution)/shard_map/ppermute | solution.py:32
  31.2 1.6 %collective-permute-done = f32[4,192,128]{2,1,0:T(8,128)S(1)} collective-permute-done((f32[4,192,128]{2,1,0:T(8,128)S(1)}, f32[4,192,128]{2,1,0:T(8,128)S(1)}, u32[]{:S(2)}, u32[]{:S(2)}) %collective-permute-start) | collective-permute-done | bytes 393248 | tf_op jit(solution)/shard_map/ppermute | solution.py:32
  32.9 3.5 %collective-permute-start.1 = (f32[2,192,128]{2,1,0:T(8,128)S(1)}, f32[2,192,128]{2,1,0:T(8,128)S(1)}, u32[]{:S(2)}, u32[]{:S(2)}) collective-permute-start(f32[2,192,128]{2,1,0:T(8,128)S(1)} %dynamic-slice_bitcast_fusion.1), channel_id=1, source_target_pairs={{0,2},{1,3},{2,0},{3,1},{4,6},{5,7},{6,4},{7,5},{8,10},{9,11},{10,... | collective-permute-start | bytes 589832 | tf_op jit(solution)/shard_map/ppermute | solution.py:32
  36.4 5.3 %collective-permute-done.1 = f32[2,192,128]{2,1,0:T(8,128)S(1)} collective-permute-done((f32[2,192,128]{2,1,0:T(8,128)S(1)}, f32[2,192,128]{2,1,0:T(8,128)S(1)}, u32[]{:S(2)}, u32[]{:S(2)}) %collective-permute-start.1) | collective-permute-done | bytes 196640 | tf_op jit(solution)/shard_map/ppermute | solution.py:32
  41.8 5.1 %collective-permute-start.2 = (f32[1,192,128]{2,1,0:T(8,128)S(1)}, f32[1,192,128]{2,1,0:T(8,128)S(1)}, u32[]{:S(2)}, u32[]{:S(2)}) collective-permute-start(f32[1,192,128]{2,1,0:T(8,128)S(1)} %constant_dynamic-slice_fusion), channel_id=1, source_target_pairs={{0,4},{1,5},{2,6},{3,7},{4,0},{5,1},{6,2},{7,3},{8,12},{9,13},{10,... | collective-permute-start | bytes 294920 | tf_op jit(solution)/shard_map/ppermute | solution.py:32
  46.9 2.9 %collective-permute-done.2 = f32[1,192,128]{2,1,0:T(8,128)S(1)} collective-permute-done((f32[1,192,128]{2,1,0:T(8,128)S(1)}, f32[1,192,128]{2,1,0:T(8,128)S(1)}, u32[]{:S(2)}, u32[]{:S(2)}) %collective-permute-start.2) | collective-permute-done | bytes 98336 | tf_op jit(solution)/shard_map/ppermute | solution.py:32
  49.8 35.3 %all-to-all-done = bf16[64,8,1152]{2,1,0:T(8,128)(2,1)} async-done(((bf16[64,8,1152]{2,1,0:T(8,128)(2,1)}), bf16[64,8,1152]{2,1,0:T(8,128)(2,1)}, u32[]{:S(2)}, u32[]{:S(2)}) %all-to-all-start) | async-done | bytes 1179680 | tf_op jit(solution)/shard_map/all_to_all | solution.py:60
  85.1 1.0 slice_reduce_fusion
  86.2 0.0 copy-done
  86.2 1.7 %fusion.2 = f32[512,256]{0,1:S(1)} fusion(bf16[1024,256]{0,1:T(8,128)(2,1)S(1)} %bitcast.53, bf16[512,1152]{1,0:T(8,128)(2,1)} %bitcast.14), kind=kOutput, calls=%fused_computation.4 | convolution fusion | flops 268435456 | bytes 2097152
  87.9 0.1 fusion.14
  88.0 0.1 multiply_reduce_fusion
  88.0 0.1 reshape.140
  88.1 0.1 copy.19
  88.2 0.2 reshape.158
  88.4 0.0 copy-start.1
  88.4 10.5 %all_to_all.20 = f32[8,1,4096]{2,1,0:T(1,128)S(1)} all-to-all(f32[8,1,4096]{2,1,0:T(1,128)S(1)} %reshape.158), channel_id=1, replica_groups=mesh['ad'=64,'tp'=8] {'tp'}, dimensions={0} | all-to-all | bytes 262144 | tf_op jit(solution)/shard_map/all_to_all | solution.py:74
  98.9 0.5 broadcast.133
  99.4 1.0 reduce.2
  100.3 0.1 reshape.159
  100.5 0.2 reshape.160
  100.7 8.0 %all_to_all.21 = bf16[8,2,2048]{2,1,0:T(2,128)(2,1)S(1)} all-to-all(bf16[8,2,2048]{2,1,0:T(2,128)(2,1)S(1)} %reshape.160), channel_id=1, replica_groups=mesh['ad'=64,'tp'=8] {'tp'}, dimensions={0} | all-to-all | bytes 131072 | tf_op jit(solution)/shard_map/all_to_all | solution.py:76
  108.7 0.1 reshape.161
  108.8 0.1 copy.16
  108.9 0.1 convert_element_type.54
  109.1 0.0 copy-done.1
  109.1 0.3 fusion.1
  109.3 22.3 %all_to_all.22 = bf16[64,8,128]{2,1,0:T(8,128)(2,1)S(1)} all-to-all(bf16[64,8,128]{2,1,0:T(8,128)(2,1)S(1)} %fusion.1), channel_id=1, replica_groups=mesh['ad'=64,'tp'=8] {'ad'}, dimensions={0} | all-to-all | bytes 262144 | tf_op jit(solution)/shard_map/all_to_all | solution.py:88
  131.6 0.3 fusion.7
  131.9 0.6 add_convert_fusion
  (13 shorter events, 0.2 us)
Async XLA Ops:
  0.0 86.2 %copy-start = (bf16[4,1024,64]{1,2,0:T(8,128)(2,1)S(1)}, bf16[4,1024,64]{1,2,0:T(8,128)(2,1)}, u32[]{:S(2)}) copy-start(bf16[4,1024,64]{1,2,0:T(8,128)(2,1)} %param.8) | copy-start | bytes 1572868
  5.6 79.5 %all-to-all-start = ((bf16[64,8,1152]{2,1,0:T(8,128)(2,1)}), bf16[64,8,1152]{2,1,0:T(8,128)(2,1)}, u32[]{:S(2)}, u32[]{:S(2)}) async-start(bf16[64,8,1152]{2,1,0:T(8,128)(2,1)} %bitcast.1), calls=%async_computation | async-start | bytes 2359296 | tf_op jit(solution)/shard_map/all_to_all | solution.py:60
  29.2 3.6 %collective-permute-start = (f32[4,192,128]{2,1,0:T(8,128)S(1)}, f32[4,192,128]{2,1,0:T(8,128)S(1)}, u32[]{:S(2)}, u32[]{:S(2)}) collective-permute-start(f32[4,192,128]{2,1,0:T(8,128)S(1)} %dynamic-slice_bitcast_fusion), channel_id=1, source_target_pairs={{0,1},{1,0},{2,3},{3,2},{4,5},{5,4},{6,7},{7,6},{8,9},{9,8},{10,11... | collective-permute-start | bytes 1179656 | tf_op jit(solution)/shard_map/ppermute | solution.py:32
  32.9 8.8 %collective-permute-start.1 = (f32[2,192,128]{2,1,0:T(8,128)S(1)}, f32[2,192,128]{2,1,0:T(8,128)S(1)}, u32[]{:S(2)}, u32[]{:S(2)}) collective-permute-start(f32[2,192,128]{2,1,0:T(8,128)S(1)} %dynamic-slice_bitcast_fusion.1), channel_id=1, source_target_pairs={{0,2},{1,3},{2,0},{3,1},{4,6},{5,7},{6,4},{7,5},{8,10},{9,11},{10,... | collective-permute-start | bytes 589832 | tf_op jit(solution)/shard_map/ppermute | solution.py:32
  41.8 8.0 %collective-permute-start.2 = (f32[1,192,128]{2,1,0:T(8,128)S(1)}, f32[1,192,128]{2,1,0:T(8,128)S(1)}, u32[]{:S(2)}, u32[]{:S(2)}) collective-permute-start(f32[1,192,128]{2,1,0:T(8,128)S(1)} %constant_dynamic-slice_fusion), channel_id=1, source_target_pairs={{0,4},{1,5},{2,6},{3,7},{4,0},{5,1},{6,2},{7,3},{8,12},{9,13},{10,... | collective-permute-start | bytes 294920 | tf_op jit(solution)/shard_map/ppermute | solution.py:32
  88.4 20.7 %copy-start.1 = (bf16[4,64,128]{2,1,0:T(8,128)(2,1)S(1)}, bf16[4,64,128]{2,1,0:T(8,128)(2,1)}, u32[]{:S(2)}) copy-start(bf16[4,64,128]{2,1,0:T(8,128)(2,1)} %param.9) | copy-start | bytes 196612

commit v15 on v13

--- a/solution.py
+++ b/solution.py
@@ -64,13 +64,8 @@
     selector = (incoming_labels[:, None] == labels[None, :]).astype(jnp.float32)
     down_part = jnp.sum(down_all * selector[:, :, None], axis=1)
     shards = lax.axis_size("tp")
-    chunk_width = slot_total // shards * rank
-    chunks = down_part.reshape(shards, slot_total // shards, rank)
-    chunk_sum = jnp.sum(lax.all_to_all(chunks, "tp", split_axis=0, concat_axis=0, tiled=True), axis=0)
-    spread = jnp.broadcast_to(chunk_sum[None], (shards,) + chunk_sum.shape)
-    down_sum = lax.all_to_all(spread, "tp", split_axis=0, concat_axis=0, tiled=True).reshape(
-        slot_total, rank
-    )
+    copies = jnp.broadcast_to(down_part[None], (shards,) + down_part.shape)
+    down_sum = jnp.sum(lax.all_to_all(copies, "tp", split_axis=0, concat_axis=0, tiled=True), axis=0)
     down_low = down_sum.astype(jnp.bfloat16)
     spread_rows = (selector.astype(jnp.bfloat16)[:, :, None] * down_low[:, None, :]).reshape(
         slot_total, adapter_number * rank

time: 132 us -> 131 us (level)
  blocking collectives: 40.6 us -> 42.1 us
  local copies, waits for them, and re-layouts: 5.74 us -> 4.35 us
    all_to_all x2 -> x1, blocking collectives: 18.4 us -> 20.2 us  [body(): lax.all_to_all(copies, 'tp', split_axis=0, concat_axis=0, tiled=True)]
where the time goes in v15:
time: 131 us; the launch traced here: 130 us
  waiting for transfers between devices  45.2 us (35%)
  blocking collectives  42.1 us (32%)
  starting transfers between devices  29.3 us (22%)
  matrix products  6.67 us (5%)
  local copies, waits for them, and re-layouts  4.35 us (3%)
  other arithmetic  2.18 us (2%)
    all_to_all x1, waiting for transfers between devices, body(): lax.all_to_all(send_rows, 'ad', split_axis=0, concat_axis=0, tiled=True)  35.3 us
    all_to_all x1, blocking collectives, body(): lax.all_to_all(adapter_update, 'ad', split_axis=0, concat_axis=0, tiled=T...  21.9 us
    all_to_all x1, blocking collectives, body(): lax.all_to_all(copies, 'tp', split_axis=0, concat_axis=0, tiled=True)  20.2 us
    all_to_all x1, starting transfers between devices, body(): lax.all_to_all(send_rows, 'ad', split_axis=0, concat_axis=0, tiled=True)  18.8 us
    ppermute x3, starting transfers between devices, body(): lax.ppermute(give, 'tp', [(k, k ^ bit) for k in range(tp_size)])  10.5 us
    ppermute x3, waiting for transfers between devices, body(): lax.ppermute(give, 'tp', [(k, k ^ bit) for k in range(tp_size)])  9.83 us
    dot_general x1, local copies, waits for them, and re-layouts, body(): jnp.dot(gathered_rows, key_base_weight, preferred_element_type=jnp.float32)  2.86 us
  transfers between devices with their start and end apart: 4, of which 4 were waited for; matrix products, arithmetic and copies ran while one was open for 4% of the time, Pallas kernels for 0%

profile of v15, /device:TPU:2, one launch (start us, length us, event | category | flops | bytes accessed | tf_op | source)
XLA Modules:
  0.0 130.1 jit_solution(12655672097457647793)
XLA Ops:
  0.0 0.0 copy-start
  0.0 0.8 add_select_fusion.1
  0.8 0.1 fusion.15
  0.9 0.1 reduce_window_sum.11
  1.0 0.2 select_reduce_fusion
  1.2 0.1 add_add_fusion
  1.3 0.1 eq.57
  1.3 0.1 broadcast_in_dim.6
  1.4 0.1 broadcast_in_dim.7
  1.5 2.6 %fusion = bf16[64,8,1152]{2,1,0:T(8,128)(2,1)} fusion(bf16[192,128]{1,0:T(8,128)(2,1)S(1)} %broadcast_in_dim.7, bf16[192,1024]{1,0:T(8,128)(2,1)} %bitcast.47, s32[192]{0:T(256)S(1)} %eq.57), kind=kOutput, calls=%fused_computation.1 | convolution fusion | flops 228065280 | bytes 1622784 | tf_op jit(solution)/shard_map/dot_general | solution.py:52
  4.1 18.8 %all-to-all-start = ((bf16[64,8,1152]{2,1,0:T(8,128)(2,1)}), bf16[64,8,1152]{2,1,0:T(8,128)(2,1)}, u32[]{:S(2)}, u32[]{:S(2)}) async-start(bf16[64,8,1152]{2,1,0:T(8,128)(2,1)} %fusion), calls=%async_computation | async-start | bytes 2359296 | tf_op jit(solution)/shard_map/all_to_all | solution.py:54
  22.9 2.9 %copy.13 = bf16[1024,1024]{1,0:T(8,128)(2,1)S(1)} copy(bf16[1024,1024]{0,1:T(8,128)(2,1)} %bitcast.46) | data formatting | bytes 4194304 | tf_op jit(solution)/shard_map/dot_general | solution.py:20
  25.8 1.8 %fusion.21 = f32[192,8,128]{2,0,1:T(8,128)S(1)} fusion(bf16[192,1024,1]{1,0,2:T(8,128)(2,1)} %bitcast.48, bf16[8,128,1024]{2,1,0:T(8,128)(2,1)S(1)} %bitcast.43), kind=kOutput, calls=%fused_computation.46 | convolution fusion | flops 402653184 | bytes 3276800 | tf_op jit(solution)/shard_map/dot_general | solution.py:20
  27.7 1.9 %collective-permute-start = (f32[4,192,128]{2,1,0:T(8,128)S(1)}, f32[4,192,128]{2,1,0:T(8,128)S(1)}, u32[]{:S(2)}, u32[]{:S(2)}) collective-permute-start(f32[4,192,128]{2,1,0:T(8,128)S(1)} %dynamic-slice_bitcast_fusion), channel_id=1, source_target_pairs={{0,1},{1,0},{2,3},{3,2},{4,5},{5,4},{6,7},{7,6},{8,9},{9,8},{10,11... | collective-permute-start | bytes 1179656 | tf_op jit(solution)/shard_map/ppermute | solution.py:32
  29.7 1.6 %collective-permute-done = f32[4,192,128]{2,1,0:T(8,128)S(1)} collective-permute-done((f32[4,192,128]{2,1,0:T(8,128)S(1)}, f32[4,192,128]{2,1,0:T(8,128)S(1)}, u32[]{:S(2)}, u32[]{:S(2)}) %collective-permute-start) | collective-permute-done | bytes 393248 | tf_op jit(solution)/shard_map/ppermute | solution.py:32
  31.4 3.5 %collective-permute-start.1 = (f32[2,192,128]{2,1,0:T(8,128)S(1)}, f32[2,192,128]{2,1,0:T(8,128)S(1)}, u32[]{:S(2)}, u32[]{:S(2)}) collective-permute-start(f32[2,192,128]{2,1,0:T(8,128)S(1)} %dynamic-slice_bitcast_fusion.1), channel_id=1, source_target_pairs={{0,2},{1,3},{2,0},{3,1},{4,6},{5,7},{6,4},{7,5},{8,10},{9,11},{10,... | collective-permute-start | bytes 589832 | tf_op jit(solution)/shard_map/ppermute | solution.py:32
  34.9 5.3 %collective-permute-done.1 = f32[2,192,128]{2,1,0:T(8,128)S(1)} collective-permute-done((f32[2,192,128]{2,1,0:T(8,128)S(1)}, f32[2,192,128]{2,1,0:T(8,128)S(1)}, u32[]{:S(2)}, u32[]{:S(2)}) %collective-permute-start.1) | collective-permute-done | bytes 196640 | tf_op jit(solution)/shard_map/ppermute | solution.py:32
  40.3 5.1 %collective-permute-start.2 = (f32[1,192,128]{2,1,0:T(8,128)S(1)}, f32[1,192,128]{2,1,0:T(8,128)S(1)}, u32[]{:S(2)}, u32[]{:S(2)}) collective-permute-start(f32[1,192,128]{2,1,0:T(8,128)S(1)} %constant_dynamic-slice_fusion), channel_id=1, source_target_pairs={{0,4},{1,5},{2,6},{3,7},{4,0},{5,1},{6,2},{7,3},{8,12},{9,13},{10,... | collective-permute-start | bytes 294920 | tf_op jit(solution)/shard_map/ppermute | solution.py:32
  45.4 2.9 %collective-permute-done.2 = f32[1,192,128]{2,1,0:T(8,128)S(1)} collective-permute-done((f32[1,192,128]{2,1,0:T(8,128)S(1)}, f32[1,192,128]{2,1,0:T(8,128)S(1)}, u32[]{:S(2)}, u32[]{:S(2)}) %collective-permute-start.2) | collective-permute-done | bytes 98336 | tf_op jit(solution)/shard_map/ppermute | solution.py:32
  48.3 35.3 %all-to-all-done = bf16[64,8,1152]{2,1,0:T(8,128)(2,1)} async-done(((bf16[64,8,1152]{2,1,0:T(8,128)(2,1)}), bf16[64,8,1152]{2,1,0:T(8,128)(2,1)}, u32[]{:S(2)}, u32[]{:S(2)}) %all-to-all-start) | async-done | bytes 1179680 | tf_op jit(solution)/shard_map/all_to_all | solution.py:54
  83.6 1.0 slice_reduce_fusion
  84.7 0.0 copy-done
  84.7 1.7 %fusion.3 = f32[512,256]{0,1:S(1)} fusion(bf16[1024,256]{0,1:T(8,128)(2,1)S(1)} %bitcast.42, bf16[512,1152]{1,0:T(8,128)(2,1)} %bitcast.14), kind=kOutput, calls=%fused_computation.5 | convolution fusion | flops 268435456 | bytes 2097152
  86.4 0.1 fusion.16
  86.5 0.1 multiply_reduce_fusion
  86.5 0.0 copy-start.1
  86.5 0.1 broadcast_in_dim.8
  86.6 20.2 %all_to_all.15 = f32[8,512,64]{1,2,0:T(8,128)S(1)} all-to-all(f32[8,512,64]{1,2,0:T(8,128)S(1)} %broadcast_in_dim.8), channel_id=1, replica_groups=mesh['ad'=64,'tp'=8] {'tp'}, dimensions={0} | all-to-all | bytes 2097152 | tf_op jit(solution)/shard_map/all_to_all | solution.py:68
  106.9 0.1 reduce_sum.29
  107.0 0.0 copy-done.1
  107.0 0.3 fusion.2
  107.3 21.9 %all_to_all.16 = bf16[64,8,128]{2,1,0:T(8,128)(2,1)S(1)} all-to-all(bf16[64,8,128]{2,1,0:T(8,128)(2,1)S(1)} %fusion.2), channel_id=1, replica_groups=mesh['ad'=64,'tp'=8] {'ad'}, dimensions={0} | all-to-all | bytes 262144 | tf_op jit(solution)/shard_map/all_to_all | solution.py:78
  129.2 0.3 fusion.5
  129.5 0.6 add_convert_fusion
  (8 shorter events, 0.2 us)
Async XLA Ops:
  0.0 84.7 %copy-start = (bf16[4,1024,64]{1,2,0:T(8,128)(2,1)S(1)}, bf16[4,1024,64]{1,2,0:T(8,128)(2,1)}, u32[]{:S(2)}) copy-start(bf16[4,1024,64]{1,2,0:T(8,128)(2,1)} %param.8) | copy-start | bytes 1572868
  4.1 79.5 %all-to-all-start = ((bf16[64,8,1152]{2,1,0:T(8,128)(2,1)}), bf16[64,8,1152]{2,1,0:T(8,128)(2,1)}, u32[]{:S(2)}, u32[]{:S(2)}) async-start(bf16[64,8,1152]{2,1,0:T(8,128)(2,1)} %fusion), calls=%async_computation | async-start | bytes 2359296 | tf_op jit(solution)/shard_map/all_to_all | solution.py:54
  27.7 3.6 %collective-permute-start = (f32[4,192,128]{2,1,0:T(8,128)S(1)}, f32[4,192,128]{2,1,0:T(8,128)S(1)}, u32[]{:S(2)}, u32[]{:S(2)}) collective-permute-start(f32[4,192,128]{2,1,0:T(8,128)S(1)} %dynamic-slice_bitcast_fusion), channel_id=1, source_target_pairs={{0,1},{1,0},{2,3},{3,2},{4,5},{5,4},{6,7},{7,6},{8,9},{9,8},{10,11... | collective-permute-start | bytes 1179656 | tf_op jit(solution)/shard_map/ppermute | solution.py:32
  31.4 8.8 %collective-permute-start.1 = (f32[2,192,128]{2,1,0:T(8,128)S(1)}, f32[2,192,128]{2,1,0:T(8,128)S(1)}, u32[]{:S(2)}, u32[]{:S(2)}) collective-permute-start(f32[2,192,128]{2,1,0:T(8,128)S(1)} %dynamic-slice_bitcast_fusion.1), channel_id=1, source_target_pairs={{0,2},{1,3},{2,0},{3,1},{4,6},{5,7},{6,4},{7,5},{8,10},{9,11},{10,... | collective-permute-start | bytes 589832 | tf_op jit(solution)/shard_map/ppermute | solution.py:32
  40.3 8.0 %collective-permute-start.2 = (f32[1,192,128]{2,1,0:T(8,128)S(1)}, f32[1,192,128]{2,1,0:T(8,128)S(1)}, u32[]{:S(2)}, u32[]{:S(2)}) collective-permute-start(f32[1,192,128]{2,1,0:T(8,128)S(1)} %constant_dynamic-slice_fusion), channel_id=1, source_target_pairs={{0,4},{1,5},{2,6},{3,7},{4,0},{5,1},{6,2},{7,3},{8,12},{9,13},{10,... | collective-permute-start | bytes 294920 | tf_op jit(solution)/shard_map/ppermute | solution.py:32
  86.5 20.5 %copy-start.1 = (bf16[4,64,128]{2,1,0:T(8,128)(2,1)S(1)}, bf16[4,64,128]{2,1,0:T(8,128)(2,1)}, u32[]{:S(2)}) copy-start(bf16[4,64,128]{2,1,0:T(8,128)(2,1)} %param.9) | copy-start | bytes 196612

commit v16 on v15

--- a/solution.py
+++ b/solution.py
@@ -64,8 +64,17 @@
     selector = (incoming_labels[:, None] == labels[None, :]).astype(jnp.float32)
     down_part = jnp.sum(down_all * selector[:, :, None], axis=1)
     shards = lax.axis_size("tp")
-    copies = jnp.broadcast_to(down_part[None], (shards,) + down_part.shape)
-    down_sum = jnp.sum(lax.all_to_all(copies, "tp", split_axis=0, concat_axis=0, tiled=True), axis=0)
+    half_slots = slot_total // 2
+    down_halves = down_part.reshape(2, half_slots, rank)
+    core = tp_index % 2
+    keep_down = lax.dynamic_index_in_dim(down_halves, core, axis=0, keepdims=False)
+    give_down = lax.dynamic_index_in_dim(down_halves, 1 - core, axis=0, keepdims=False)
+    pair_down = keep_down + lax.ppermute(give_down, "tp", [(k, k ^ 1) for k in range(shards)])
+    copies = jnp.broadcast_to(pair_down[None], (shards,) + pair_down.shape)
+    moved_down = lax.all_to_all(copies, "tp", split_axis=0, concat_axis=0, tiled=True)
+    down_sum = jnp.sum(moved_down.reshape(shards // 2, 2, half_slots, rank), axis=0).reshape(
+        slot_total, rank
+    )
     down_low = down_sum.astype(jnp.bfloat16)
     spread_rows = (selector.astype(jnp.bfloat16)[:, :, None] * down_low[:, None, :]).reshape(
         slot_total, adapter_number * rank

time: 131 us -> 128 us (0.977)
  the two profiles are of different devices: /device:TPU:2 before, /device:TPU:8 now
where the time goes in v16:
time: 128 us
  waiting for transfers between devices  48.5 us (38%)
  blocking collectives  36.5 us (29%)
  starting transfers between devices  29.2 us (23%)
  matrix products  6.67 us (5%)
  local copies, waits for them, and re-layouts  4.49 us (4%)
  other arithmetic  2.14 us (2%)
    all_to_all x1, waiting for transfers between devices, body(): lax.all_to_all(send_rows, 'ad', split_axis=0, concat_axis=0, tiled=True)  35.4 us
    all_to_all x1, blocking collectives, body(): lax.all_to_all(adapter_update, 'ad', split_axis=0, concat_axis=0, tiled=T...  22.9 us
    all_to_all x1, starting transfers between devices, body(): lax.all_to_all(send_rows, 'ad', split_axis=0, concat_axis=0, tiled=True)  18.8 us
    all_to_all x1, blocking collectives, body(): lax.all_to_all(copies, 'tp', split_axis=0, concat_axis=0, tiled=True)  13.6 us
    ppermute x3, waiting for transfers between devices, body(): lax.ppermute(give, 'tp', [(k, k ^ bit) for k in range(tp_size)])  11.9 us
    ppermute x3, starting transfers between devices, body(): lax.ppermute(give, 'tp', [(k, k ^ bit) for k in range(tp_size)])  8.48 us
    dot_general x1, local copies, waits for them, and re-layouts, body(): jnp.dot(gathered_rows, key_base_weight, preferred_element_type=jnp.float32)  2.86 us
  transfers between devices with their start and end apart: 5, of which 5 were waited for; matrix products, arithmetic and copies ran while one was open for 4% of the time, Pallas kernels for 0%

profile of v16, /device:TPU:8, one launch (start us, length us, event | category | flops | bytes accessed | tf_op | source)
XLA Modules:
  0.0 127.8 jit_solution(15587143019924369389)
XLA Ops:
  0.0 0.0 copy-start
  0.0 0.8 add_select_fusion.1
  0.8 0.1 fusion.15
  0.9 0.1 reduce_window_sum.11
  1.0 0.2 select_reduce_fusion
  1.2 0.1 add_add_fusion
  1.3 0.1 eq.58
  1.3 0.1 broadcast_in_dim.6
  1.4 0.1 broadcast_in_dim.7
  1.5 2.6 %fusion = bf16[64,8,1152]{2,1,0:T(8,128)(2,1)} fusion(bf16[192,128]{1,0:T(8,128)(2,1)S(1)} %broadcast_in_dim.7, bf16[192,1024]{1,0:T(8,128)(2,1)} %bitcast.60, s32[192]{0:T(256)S(1)} %eq.58), kind=kOutput, calls=%fused_computation.1 | convolution fusion | flops 228065280 | bytes 1622784 | tf_op jit(solution)/shard_map/dot_general | solution.py:52
  4.1 18.8 %all-to-all-start = ((bf16[64,8,1152]{2,1,0:T(8,128)(2,1)}), bf16[64,8,1152]{2,1,0:T(8,128)(2,1)}, u32[]{:S(2)}, u32[]{:S(2)}) async-start(bf16[64,8,1152]{2,1,0:T(8,128)(2,1)} %fusion), calls=%async_computation | async-start | bytes 2359296 | tf_op jit(solution)/shard_map/all_to_all | solution.py:54
  22.9 2.9 %copy.12 = bf16[1024,1024]{1,0:T(8,128)(2,1)S(1)} copy(bf16[1024,1024]{0,1:T(8,128)(2,1)} %bitcast.58) | data formatting | bytes 4194304 | tf_op jit(solution)/shard_map/dot_general | solution.py:20
  25.8 1.8 %fusion.21 = f32[192,8,128]{2,0,1:T(8,128)S(1)} fusion(bf16[192,1024,1]{1,0,2:T(8,128)(2,1)} %bitcast.61, bf16[8,128,1024]{2,1,0:T(8,128)(2,1)S(1)} %bitcast.55), kind=kOutput, calls=%fused_computation.51 | convolution fusion | flops 402653184 | bytes 3276800 | tf_op jit(solution)/shard_map/dot_general | solution.py:20
  27.7 1.9 %collective-permute-start = (f32[4,192,128]{2,1,0:T(8,128)S(1)}, f32[4,192,128]{2,1,0:T(8,128)S(1)}, u32[]{:S(2)}, u32[]{:S(2)}) collective-permute-start(f32[4,192,128]{2,1,0:T(8,128)S(1)} %dynamic-slice_bitcast_fusion), channel_id=1, source_target_pairs={{0,1},{1,0},{2,3},{3,2},{4,5},{5,4},{6,7},{7,6},{8,9},{9,8},{10,11... | collective-permute-start | bytes 1179656 | tf_op jit(solution)/shard_map/ppermute | solution.py:32
  29.7 1.6 %collective-permute-done = f32[4,192,128]{2,1,0:T(8,128)S(1)} collective-permute-done((f32[4,192,128]{2,1,0:T(8,128)S(1)}, f32[4,192,128]{2,1,0:T(8,128)S(1)}, u32[]{:S(2)}, u32[]{:S(2)}) %collective-permute-start) | collective-permute-done | bytes 393248 | tf_op jit(solution)/shard_map/ppermute | solution.py:32
  31.4 2.4 %collective-permute-start.1 = (f32[2,192,128]{2,1,0:T(8,128)S(1)}, f32[2,192,128]{2,1,0:T(8,128)S(1)}, u32[]{:S(2)}, u32[]{:S(2)}) collective-permute-start(f32[2,192,128]{2,1,0:T(8,128)S(1)} %dynamic-slice_bitcast_fusion.1), channel_id=1, source_target_pairs={{0,2},{1,3},{2,0},{3,1},{4,6},{5,7},{6,4},{7,5},{8,10},{9,11},{10,... | collective-permute-start | bytes 589832 | tf_op jit(solution)/shard_map/ppermute | solution.py:32
  33.8 6.4 %collective-permute-done.1 = f32[2,192,128]{2,1,0:T(8,128)S(1)} collective-permute-done((f32[2,192,128]{2,1,0:T(8,128)S(1)}, f32[2,192,128]{2,1,0:T(8,128)S(1)}, u32[]{:S(2)}, u32[]{:S(2)}) %collective-permute-start.1) | collective-permute-done | bytes 196640 | tf_op jit(solution)/shard_map/ppermute | solution.py:32
  40.3 4.2 %collective-permute-start.2 = (f32[1,192,128]{2,1,0:T(8,128)S(1)}, f32[1,192,128]{2,1,0:T(8,128)S(1)}, u32[]{:S(2)}, u32[]{:S(2)}) collective-permute-start(f32[1,192,128]{2,1,0:T(8,128)S(1)} %constant_dynamic-slice_fusion.1), channel_id=1, source_target_pairs={{0,4},{1,5},{2,6},{3,7},{4,0},{5,1},{6,2},{7,3},{8,12},{9,13},{10,... | collective-permute-start | bytes 294920 | tf_op jit(solution)/shard_map/ppermute | solution.py:32
  44.5 3.8 %collective-permute-done.2 = f32[1,192,128]{2,1,0:T(8,128)S(1)} collective-permute-done((f32[1,192,128]{2,1,0:T(8,128)S(1)}, f32[1,192,128]{2,1,0:T(8,128)S(1)}, u32[]{:S(2)}, u32[]{:S(2)}) %collective-permute-start.2) | collective-permute-done | bytes 98336 | tf_op jit(solution)/shard_map/ppermute | solution.py:32
  48.3 35.4 %all-to-all-done = bf16[64,8,1152]{2,1,0:T(8,128)(2,1)} async-done(((bf16[64,8,1152]{2,1,0:T(8,128)(2,1)}), bf16[64,8,1152]{2,1,0:T(8,128)(2,1)}, u32[]{:S(2)}, u32[]{:S(2)}) %all-to-all-start) | async-done | bytes 1179680 | tf_op jit(solution)/shard_map/all_to_all | solution.py:54
  83.7 1.0 slice_reduce_fusion
  84.7 0.0 copy-done
  84.7 1.7 %fusion.3 = f32[512,256]{0,1:S(1)} fusion(bf16[1024,256]{0,1:T(8,128)(2,1)S(1)} %bitcast.54, bf16[512,1152]{1,0:T(8,128)(2,1)} %bitcast.14), kind=kOutput, calls=%fused_computation.5 | convolution fusion | flops 268435456 | bytes 2097152
  86.4 0.0 copy-start.1
  86.4 0.1 fusion.16
  86.5 0.1 multiply_reduce_fusion
  86.6 0.1 reshape.129
  86.7 0.1 constant_dynamic-slice_fusion
  86.8 1.9 %collective-permute-start.3 = (f32[256,64]{0,1:T(8,128)S(1)}, f32[256,64]{0,1:T(8,128)S(1)}, u32[]{:S(2)}, u32[]{:S(2)}) collective-permute-start(f32[256,64]{0,1:T(8,128)S(1)} %bitcast.66), channel_id=1, source_target_pairs={{0,1},{1,0},{2,3},{3,2},{4,5},{5,4},{6,7},{7,6},{8,9},{9,8},{10,11... | collective-permute-start | bytes 196616 | tf_op jit(solution)/shard_map/ppermute | solution.py:72
  88.7 1.2 collective-permute-done.3
  90.0 13.6 %all_to_all.15 = f32[8,256,64]{1,2,0:T(8,128)S(1)} all-to-all(f32[8,256,64]{1,2,0:T(8,128)S(1)} %broadcast_in_dim.8), channel_id=1, replica_groups=mesh['ad'=64,'tp'=8] {'tp'}, dimensions={0} | all-to-all | bytes 1048576 | tf_op jit(solution)/shard_map/all_to_all | solution.py:74
  103.7 0.0 copy-done.1
  103.7 0.3 fusion.2
  104.0 22.9 %all_to_all.16 = bf16[64,8,128]{2,1,0:T(8,128)(2,1)S(1)} all-to-all(bf16[64,8,128]{2,1,0:T(8,128)(2,1)S(1)} %fusion.2), channel_id=1, replica_groups=mesh['ad'=64,'tp'=8] {'ad'}, dimensions={0} | all-to-all | bytes 262144 | tf_op jit(solution)/shard_map/all_to_all | solution.py:87
  126.8 0.3 fusion.5
  127.1 0.6 add_convert_fusion
  (13 shorter events, 0.3 us)
Async XLA Ops:
  0.0 84.7 %copy-start = (bf16[4,1024,64]{1,2,0:T(8,128)(2,1)S(1)}, bf16[4,1024,64]{1,2,0:T(8,128)(2,1)}, u32[]{:S(2)}) copy-start(bf16[4,1024,64]{1,2,0:T(8,128)(2,1)} %param.8) | copy-start | bytes 1572868
  4.1 79.6 %all-to-all-start = ((bf16[64,8,1152]{2,1,0:T(8,128)(2,1)}), bf16[64,8,1152]{2,1,0:T(8,128)(2,1)}, u32[]{:S(2)}, u32[]{:S(2)}) async-start(bf16[64,8,1152]{2,1,0:T(8,128)(2,1)} %fusion), calls=%async_computation | async-start | bytes 2359296 | tf_op jit(solution)/shard_map/all_to_all | solution.py:54
  27.7 3.6 %collective-permute-start = (f32[4,192,128]{2,1,0:T(8,128)S(1)}, f32[4,192,128]{2,1,0:T(8,128)S(1)}, u32[]{:S(2)}, u32[]{:S(2)}) collective-permute-start(f32[4,192,128]{2,1,0:T(8,128)S(1)} %dynamic-slice_bitcast_fusion), channel_id=1, source_target_pairs={{0,1},{1,0},{2,3},{3,2},{4,5},{5,4},{6,7},{7,6},{8,9},{9,8},{10,11... | collective-permute-start | bytes 1179656 | tf_op jit(solution)/shard_map/ppermute | solution.py:32
  31.4 8.8 %collective-permute-start.1 = (f32[2,192,128]{2,1,0:T(8,128)S(1)}, f32[2,192,128]{2,1,0:T(8,128)S(1)}, u32[]{:S(2)}, u32[]{:S(2)}) collective-permute-start(f32[2,192,128]{2,1,0:T(8,128)S(1)} %dynamic-slice_bitcast_fusion.1), channel_id=1, source_target_pairs={{0,2},{1,3},{2,0},{3,1},{4,6},{5,7},{6,4},{7,5},{8,10},{9,11},{10,... | collective-permute-start | bytes 589832 | tf_op jit(solution)/shard_map/ppermute | solution.py:32
  40.3 8.0 %collective-permute-start.2 = (f32[1,192,128]{2,1,0:T(8,128)S(1)}, f32[1,192,128]{2,1,0:T(8,128)S(1)}, u32[]{:S(2)}, u32[]{:S(2)}) collective-permute-start(f32[1,192,128]{2,1,0:T(8,128)S(1)} %constant_dynamic-slice_fusion.1), channel_id=1, source_target_pairs={{0,4},{1,5},{2,6},{3,7},{4,0},{5,1},{6,2},{7,3},{8,12},{9,13},{10,... | collective-permute-start | bytes 294920 | tf_op jit(solution)/shard_map/ppermute | solution.py:32
  86.4 17.3 %copy-start.1 = (bf16[4,64,128]{2,1,0:T(8,128)(2,1)S(1)}, bf16[4,64,128]{2,1,0:T(8,128)(2,1)}, u32[]{:S(2)}) copy-start(bf16[4,64,128]{2,1,0:T(8,128)(2,1)} %param.9) | copy-start | bytes 196612
  86.8 3.1 %collective-permute-start.3 = (f32[256,64]{0,1:T(8,128)S(1)}, f32[256,64]{0,1:T(8,128)S(1)}, u32[]{:S(2)}, u32[]{:S(2)}) collective-permute-start(f32[256,64]{0,1:T(8,128)S(1)} %bitcast.66), channel_id=1, source_target_pairs={{0,1},{1,0},{2,3},{3,2},{4,5},{5,4},{6,7},{7,6},{8,9},{9,8},{10,11... | collective-permute-start | bytes 196616 | tf_op jit(solution)/shard_map/ppermute | solution.py:72
